TPU v7x, 128 devices: a whole 4x4x4 slice. The times are simulated.
128 devices in a mesh: grp: 4 (over x_hi, core), sub: 32 (over x_lo, y, z).
Axes of the slice: x: 4 (x_hi: 2, x_lo: 2; x = x_hi * 2 + x_lo), y: 4, z: 4, core: 2. Of those that a mesh axis runs over, the one named last changes fastest.
Arguments:
- template: bfloat16 [96, 96, 128], P('sub'), may hold values from -4 to 4
- subjects: bfloat16 [128, 96, 96, 128], P(('grp', 'sub')), may hold values from -40 to 40
Outputs:
- velocity: float32 [96, 3, 96, 128], P('sub')
- new_template: float32 [96, 96, 128], P('sub')
- similarity: float32 [], replicated
All inputs are finite; a program needn't handle non-finite values.
Results may differ from a plain program's by a relative error of at most 0.0003.
Values may be sent and summed in bfloat16 or wider, within the bound.
No kernel may reach another device: no remote copies, remote signals or barrier semaphores. Data moves between devices by JAX's collectives and lax.ppermute only.
A program may use at most 128 MiB of HBM per device.

v0:
```python
import math

import jax
import jax.numpy as jnp
from jax import lax
from jax.sharding import PartitionSpec as P

RADIUS = 4
REACH = 5


EPSILON = 1e-05
STEP_LENGTH = 0.5
VARIANCE = 3.0
HIGH = lax.Precision.HIGHEST


def padded_2(x, sides, width):
    for axis, dim in sides:
        devices, length = (lax.axis_size(axis), x.shape[dim])
        up = [(i, (i + 1) % devices) for i in range(devices - 1)]
        down = [(j, i) for i, j in up]
        last = lax.slice_in_dim(x, length - width, length, axis=dim)
        initial = lax.slice_in_dim(x, 0, width, axis=dim)
        before = lax.ppermute(last, axis, up)
        after = lax.ppermute(initial, axis, down)
        x = jnp.concatenate([before, x, after], axis=dim)
    return x


def band_matrix(length, extent, weighted):
    row_ids = lax.broadcasted_iota(jnp.int32, (length, length), 0)
    col_ids = lax.broadcasted_iota(jnp.int32, (length, length), 1)
    inside = jnp.abs(row_ids - col_ids) <= extent
    if weighted:
        kernel_sum = sum(
            (math.exp(-offset * offset / (2.0 * VARIANCE)) for offset in range(-extent, extent + 1))
        )
        offset_f = (row_ids - col_ids).astype(jnp.float32)
        values = jnp.exp(-offset_f * offset_f / (2.0 * VARIANCE)) / kernel_sum
        return jnp.where(inside, values, 0.0)
    return jnp.where(inside, 1.0 / (2 * extent + 1), 0.0).astype(jnp.float32)


def filter_volume(volume, along_z, along_x, along_y):
    result = jnp.dot(volume, along_y, precision=HIGH, preferred_element_type=jnp.float32)
    result = jnp.einsum(
        "ab,zby->zay", along_x, result, precision=HIGH, preferred_element_type=jnp.float32
    )
    return jnp.einsum(
        "ab,bxy->axy", along_z, result, precision=HIGH, preferred_element_type=jnp.float32
    )


def central(volume):
    padded = jnp.pad(volume, 1)
    along_z = (padded[2:, 1:-1, 1:-1] - padded[:-2, 1:-1, 1:-1]) * 0.5
    along_x = (padded[1:-1, 2:, 1:-1] - padded[1:-1, :-2, 1:-1]) * 0.5
    along_y = (padded[1:-1, 1:-1, 2:] - padded[1:-1, 1:-1, :-2]) * 0.5
    return jnp.stack([along_z, along_x, along_y], axis=1)


def on_device(template, subjects):
    fixed_image = lax.all_gather(template, "sub", axis=0, tiled=True).astype(jnp.float32)
    depth, height, width = fixed_image.shape
    box_z = band_matrix(depth, RADIUS, False)
    box_x = band_matrix(height, RADIUS, False)
    box_y = band_matrix(width, RADIUS, False)
    gauss_z = band_matrix(depth, REACH, True)
    gauss_x = band_matrix(height, REACH, True)
    gauss_y = band_matrix(width, REACH, True)
    mean_i = filter_volume(fixed_image, box_z, box_x, box_y)
    mean_ii = filter_volume(fixed_image * fixed_image, box_z, box_x, box_y)
    var_i = mean_ii - mean_i * mean_i
    centred_i = fixed_image - mean_i
    gradients = central(fixed_image)
    moving = subjects[0].astype(jnp.float32)
    mean_j = filter_volume(moving, box_z, box_x, box_y)
    mean_jj = filter_volume(moving * moving, box_z, box_x, box_y)
    mean_ij = filter_volume(fixed_image * moving, box_z, box_x, box_y)
    cross_sum = mean_ij - mean_i * mean_j
    var_j = mean_jj - mean_j * mean_j
    denominator = var_i * var_j + EPSILON
    factor = (
        2.0
        * cross_sum
        / denominator
        * (moving - mean_j - cross_sum / (var_i + EPSILON) * centred_i)
    )
    force_total = factor[:, None] * gradients
    cc_local = jnp.sum(cross_sum * cross_sum / denominator)
    planar = jnp.einsum(
        "zcxb,ba->zcxa", force_total, gauss_y, precision=HIGH, preferred_element_type=jnp.float32
    )
    planar = jnp.einsum(
        "ab,zcby->zcay", gauss_x, planar, precision=HIGH, preferred_element_type=jnp.float32
    )
    group_count = lax.axis_size("grp")
    subject_count = subjects.shape[0] * group_count * lax.axis_size("sub")
    smooth = jnp.einsum(
        "ab,bcxy->acxy", gauss_z, planar, precision=HIGH, preferred_element_type=jnp.float32
    )
    intensity = moving[:, None]
    owner_part = lax.psum_scatter(
        jnp.concatenate([smooth, intensity], axis=1), "sub", scatter_dimension=0, tiled=True
    )
    summed = lax.psum(owner_part, "grp")
    mean_velocity = summed[:, :3] / subject_count
    mean_image = summed[:, 3] / subject_count
    padded_mean = padded_2(mean_image, (("sub", 0),), 1)
    velocity_square = jnp.sum(mean_velocity * mean_velocity)
    image_square = jnp.sum(mean_image * mean_image)
    cc_total = lax.psum(cc_local, ("grp", "sub"))
    velocity_total, image_sq_total = lax.psum((velocity_square, image_square), "sub")
    cell_count = depth * height * width
    velocity_norm = jnp.sqrt(velocity_total / cell_count + EPSILON)
    image_norm = jnp.sqrt(image_sq_total / cell_count + EPSILON)
    velocity = STEP_LENGTH * mean_velocity / velocity_norm
    slope_z = (padded_mean[2:] - padded_mean[:-2]) * 0.5
    padded_x = jnp.pad(mean_image, ((0, 0), (1, 1), (0, 0)))
    slope_x = (padded_x[:, 2:] - padded_x[:, :-2]) * 0.5
    padded_y = jnp.pad(mean_image, ((0, 0), (0, 0), (1, 1)))
    slope_y = (padded_y[:, :, 2:] - padded_y[:, :, :-2]) * 0.5
    advected = velocity[:, 0] * slope_z + velocity[:, 1] * slope_x + velocity[:, 2] * slope_y
    new_template = (mean_image - advected) / image_norm
    similarity = cc_total / (subject_count * cell_count)
    return (velocity, new_template, similarity)


def solution(mesh):
    placed = (P("sub", None, None), P(("grp", "sub"), None, None, None))
    return jax.shard_map(
        on_device,
        mesh=mesh,
        in_specs=placed,
        out_specs=(P("sub", None, None, None), P("sub", None, None), P()),
        check_vma=False,
    )
```

profile of v0, /device:TPU:0, one launch (start us, length us, event | category | flops | bytes accessed | tf_op | source)
XLA Modules:
  0.0 769.4 jit_solution(3366972188630262749)
XLA Ops:
  7.2 0.0 all-gather.2.cloned.1.call-start
  7.2 0.7 all-gather.2.cloned.1.call-update
  7.9 0.0 reduce-scatter.2.cloned.1.call-start
  7.9 5.9 fusion.30
  13.9 6.3 copy.25
  20.1 9.0 %convolution_bitcast_fusion.1 = f32[96,96,128]{1,0,2:T(8,128)} fusion(f32[96,96,128]{1,0,2:T(8,128)} %copy.25), kind=kOutput, calls=%fused_computation.45 | convolution fusion | flops 1358991360 | bytes 9437184 | tf_op jit(solution)/shard_map/ab,zby->zay/dot_general | solution.py:47
  29.1 0.0 copy-start
  29.1 6.4 copy.26
  35.5 0.0 copy-done
  35.5 0.0 copy-start.3
  35.5 3.1 bitcast_convert_fusion
  38.6 0.8 copy-done.3
  39.4 5.9 fusion.81
  45.3 120.0 %all-gather.2.cloned.1.call-done = bf16[96,96,128]{2,1,0:T(8,128)(2,1)} async-done(((bf16[3,96,128]{2,1,0:T(8,128)(2,1)}), bf16[96,96,128]{2,1,0:T(8,128)(2,1)}) %all-gather.2.cloned.1.call-update) | async-done | bytes 2359312 | tf_op jit(solution)/shard_map/all_gather | solution.py:64
  165.3 3.8 convert_multiply_fusion
  169.2 7.6 fusion.17
  176.7 5.1 convolution_bitcast_fusion.3
  181.9 9.9 %fusion.15 = f32[96,96,128]{2,0,1:T(8,128)} fusion(f32[96,96,128]{2,1,0:T(8,128)S(1)} %convolution_bitcast_fusion.3), kind=kOutput, calls=%fused_computation.27 | convolution fusion | flops 1358991360 | bytes 9437184 | tf_op jit(solution)/shard_map/ab,bxy->axy/dot_general | solution.py:50
  191.8 7.6 fusion.21
  199.4 4.9 convolution_bitcast_fusion.4
  204.3 9.9 %fusion.19 = f32[96,96,128]{2,0,1:T(8,128)} fusion(f32[96,96,128]{2,1,0:T(8,128)S(1)} %convolution_bitcast_fusion.4), kind=kOutput, calls=%fused_computation.31 | convolution fusion | flops 1358991360 | bytes 9437184 | tf_op jit(solution)/shard_map/ab,bxy->axy/dot_general | solution.py:50
  214.2 7.6 fusion.25
  221.7 0.0 copy-start.1
  221.8 6.1 convolution_bitcast_fusion.6
  227.9 0.0 copy-done.1
  227.9 3.7 convolution_bitcast_fusion.5
  231.6 6.3 copy.22
  237.8 9.0 %convolution_bitcast_fusion.2 = f32[96,96,128]{1,0,2:T(8,128)} fusion(f32[96,96,128]{1,0,2:T(8,128)} %copy.22), kind=kOutput, calls=%fused_computation.46 | convolution fusion | flops 1358991360 | bytes 9437184 | tf_op jit(solution)/shard_map/ab,zby->zay/dot_general | solution.py:47
  246.8 6.3 copy.23
  253.1 0.0 copy-start.2
  253.1 8.8 %fusion.84 = f32[96,96,128]{2,0,1:T(8,128)} fusion(f32[96,96,128]{2,0,1:T(8,128)} %copy.23), kind=kOutput, calls=%fused_computation.118 | convolution fusion | flops 1358991360 | bytes 9437184 | tf_op jit(solution)/shard_map/ab,bxy->axy/dot_general | solution.py:50
  261.9 0.0 copy-done.2
  261.9 0.8 copy_convert_fusion
  262.6 7.5 fusion.8
  270.2 0.0 copy-start.4
  270.2 21.9 %fusion.27 = (f32[]{:T(128)}, f32[96,96,128]{2,0,1:T(8,128)}) fusion(f32[96,96,128]{2,0,1:T(8,128)} %fusion.84, f32[96,96,128]{2,0,1:T(8,128)} %fusion.81, f32[96,96,128]{2,0,1:T(8,128)} %fusion.15, f32[96,96,128]{2,0,1:T(8,128)} %fusion.19, bf16[96,96,128]{2,1,0:T(8,128)(2,1)S(1)} %copy-done.2, bf16[1,96,96,128]{3,2,1,0:T(8,128)(2,1)S(1)} %copy-done, ...), kind=kOutput, calls=%fused_computation.43 | convolution fusion | flops 1384943616 | bytes 33030148 | tf_op jit(solution)/shard_map/ab,bxy->axy/dot_general | solution.py:50
  292.0 0.0 copy-done.4
  292.0 0.0 copy-done.5
  292.0 5.2 maximum_multiply_fusion
  297.2 22.1 %fusion.2 = f32[96,3,96,128]{3,2,1,0:T(8,128)S(1)} fusion(f32[96,3,96,128]{3,0,2,1:T(8,128)S(1)} %maximum_multiply_fusion), kind=kOutput, calls=%fused_computation.10 | convolution fusion | flops 5435965440 | bytes 28311552 | tf_op jit(solution)/shard_map/zcxb,ba->zcxa/dot_general | solution.py:92
  319.3 0.0 slice-start
  319.3 15.9 %convolution_bitcast_fusion = f32[96,3,96,128]{3,2,1,0:T(8,128)} fusion(f32[96,3,96,128]{3,2,1,0:T(8,128)S(1)} %fusion.2), kind=kOutput, calls=%fused_computation.12 | convolution fusion | flops 4076946432 | bytes 28311552 | tf_op jit(solution)/shard_map/ab,zcby->zcay/dot_general | solution.py:95
  335.2 25.3 %fusion = f32[96,3,96,128]{3,0,2,1:T(8,128)S(1)} fusion(f32[96,3,96,128]{3,2,1,0:T(8,128)} %convolution_bitcast_fusion), kind=kOutput, calls=%fused_computation.8 | convolution fusion | flops 4076946432 | bytes 28311552 | tf_op jit(solution)/shard_map/ab,bcxy->acxy/dot_general | solution.py:100
  360.5 0.0 slice-done
  360.6 0.0 slice-done.1
  360.6 7.1 pad_maximum_fusion
  367.7 15.8 %copy.34 = f32[96,4,96,128]{3,2,1,0:T(8,128)} copy(f32[96,4,96,128]{3,0,2,1:T(8,128)} %pad_maximum_fusion) | data formatting | bytes 37748736 | tf_op jit(solution)/shard_map/concatenate | solution.py:105
  383.5 0.0 reduce-scatter.2.cloned.1.call-update
  383.5 0.0 all-reduce.6.cloned.1.call-start
  383.5 218.5 %reduce-scatter.2.cloned.1.call-done = f32[3,4,96,128]{3,2,1,0:T(8,128)} async-done(((f32[96,4,96,128]{3,2,1,0:T(8,128)}), f32[3,4,96,128]{3,2,1,0:T(8,128)}) %reduce-scatter.2.cloned.1.call-update) | async-done | bytes 589840 | tf_op jit(solution)/shard_map/reduce_scatter | solution.py:104
  602.0 0.0 all-reduce.6.cloned.1.call-update
  602.0 63.3 %psum.31 = f32[]{:T(128)} all-reduce(f32[]{:T(128)} %get-tuple-element.14), channel_id=1, replica_groups=mesh['grp'=4,'sub'=32] {'grp','sub'}, use_global_device_ids=true, to_apply=%region_7.8 | all-reduce | flops 1 | bytes 8 | tf_op jit(solution)/shard_map/psum | solution.py:113
  665.3 0.0 all-reduce.6.cloned.1.call-done
  665.3 1.7 multiply_reduce_fusion
  667.1 1.6 multiply_reduce_fusion.1
  669.3 81.3 %all-reduce.3 = (f32[]{:T(128)}, f32[]{:T(128)}) all-reduce(f32[]{:T(128)} %multiply_reduce_fusion, f32[]{:T(128)} %multiply_reduce_fusion.1), channel_id=1, replica_groups=mesh['grp'=4,'sub'=32] {'sub'}, use_global_device_ids=true, to_apply=%region_3.4 | all-reduce | flops 2 | bytes 16 | tf_op jit(solution)/shard_map/psum | solution.py:114
  751.3 0.9 slice_multiply_fusion
  752.3 1.3 collective-permute-start
  753.6 4.5 collective-permute-start.1
  758.1 1.1 multiply_divide_fusion.1
  759.9 0.8 copy.36
  760.7 0.0 collective-permute-done
  760.7 0.0 collective-permute-done.1
  760.7 0.8 fusion.39
  (4 shorter events, 0.0 us)
Async XLA Ops:
  7.2 158.2 %all-gather.2.cloned.1.call-start = ((), (), s32[]{:S(2)}) async-start(), calls=%async_computation.1 | async-start | bytes 2433024 | tf_op jit(solution)/shard_map/all_gather | solution.py:64
  7.9 594.1 %reduce-scatter.2.cloned.1.call-start = ((), (), s32[]{:S(2)}) async-start(), calls=%async_computation.2 | async-start | bytes 19464192 | tf_op jit(solution)/shard_map/reduce_scatter | solution.py:104
  29.1 6.4 copy-start
  35.5 3.9 copy-start.3
  221.7 6.2 copy-start.1
  253.1 8.8 %copy-start.2 = (bf16[96,96,128]{2,1,0:T(8,128)(2,1)S(1)}, bf16[96,96,128]{2,1,0:T(8,128)(2,1)}, u32[]{:S(2)}) copy-start(bf16[96,96,128]{2,1,0:T(8,128)(2,1)} %all-gather.2.cloned.1.call-done) | copy-start | bytes 7077892
  270.2 21.9 %copy-start.4 = (f32[96,1,96,128]{3,0,2,1:T(8,128)S(1)}, f32[96,1,96,128]{3,0,2,1:T(8,128)}, u32[]{:S(2)}) copy-start(f32[96,1,96,128]{3,0,2,1:T(8,128)} %get-tuple-element.16) | copy-start | bytes 14155780
  270.2 21.9 %copy-start.5 = (f32[96,1,96,128]{3,0,2,1:T(8,128)S(1)}, f32[96,1,96,128]{3,0,2,1:T(8,128)}, u32[]{:S(2)}) copy-start(f32[96,1,96,128]{3,0,2,1:T(8,128)} %get-tuple-element.17) | copy-start | bytes 14155780
  319.3 41.2 %slice-start = ((s8[4718592]{0:T(1024)(128)(4,1)}), s8[4194304]{0:T(1024)(128)(4,1)S(1)}, s32[]{:S(2)}) async-start(s8[4718592]{0:T(1024)(128)(4,1)} %bitcast.107), calls=%async_computation.4 | async-start | bytes 8388608
  335.2 25.3 %slice-start.1 = ((s8[4718592]{0:T(1024)(128)(4,1)}), s8[524288]{0:T(1024)(128)(4,1)S(1)}, s32[]{:S(2)}) async-start(s8[4718592]{0:T(1024)(128)(4,1)} %bitcast.107), calls=%async_computation.5 | async-start | bytes 1048576
  383.5 281.9 %all-reduce.6.cloned.1.call-start = ((), (), s32[]{:S(2)}) async-start(), calls=%async_computation.3 | async-start | bytes 1179648 | tf_op jit(solution)/shard_map/psum | solution.py:107
  752.3 8.4 %collective-permute-start = (f32[1,96,128]{2,1,0:T(8,128)S(1)}, f32[1,96,128]{2,1,0:T(8,128)S(1)}, u32[]{:S(2)}, u32[]{:S(2)}) collective-permute-start(f32[1,96,128]{2,1,0:T(8,128)S(1)} %get-tuple-element.24), channel_id=1, source_target_pairs={{1,0},{2,1},{3,2},{4,3},{5,4},{6,5},{7,6},{8,7},{9,8},{10,9},{11,1... | collective-permute-start | bytes 147464 | tf_op jit(solution)/shard_map/ppermute | solution.py:26
  753.6 7.1 collective-permute-start.1
Sparse Core Ops, SparseCore 0:
  9.6 155.6 all-gather.1
  383.6 218.3 reduce-scatter.1
  604.5 40.6 all-reduce.5
where the time goes:
time: 778 us; the launch traced here: 769 us
  waiting for transfers between devices  339 us (44%)
  matrix products  186 us (24%)
  blocking collectives  145 us (19%)
  local copies, waits for them, and re-layouts  42.6 us (5%)
  other arithmetic  33.7 us (4%)
  between operations  17.4 us (2%)
    reduce_scatter x1, waiting for transfers between devices, on_device(): lax.psum_scatter(jnp.concatenate([smooth, intensity], axis=1), 'sub', sca...  218 us
    all_gather x1, waiting for transfers between devices, on_device(): lax.all_gather(template, 'sub', axis=0, tiled=True).astype(jnp.float32)  120 us
    psum x1, blocking collectives, on_device(): lax.psum((velocity_square, image_square), 'sub')  81.3 us
    psum x1, blocking collectives, on_device(): cc_total = lax.psum(cc_local, ('grp', 'sub'))  63.3 us
    dot_general x5, matrix products, filter_volume(): jnp.einsum('ab,bxy->axy', along_z, result, precision=HIGH, preferred_elem...  56.4 us
    dot_general x5, matrix products, filter_volume(): jnp.einsum('ab,zby->zay', along_x, result, precision=HIGH, preferred_elem...  34.1 us
    dot_general x5, matrix products, filter_volume(): jnp.dot(volume, along_y, precision=HIGH, preferred_element_type=jnp.float32)  32.2 us
    dot_general x1, matrix products, on_device(): jnp.einsum('ab,bcxy->acxy', gauss_z, planar, precision=HIGH, preferred_el...  25.3 us
  transfers between devices with their start and end apart: 5, of which 2 were waited for; matrix products, arithmetic and copies ran while one was open for 5% of the time, Pallas kernels for 0%

commit v1 on v0

v1 whole, which is shorter than its diff:
```python
import math

import jax
import jax.numpy as jnp
from jax import lax
from jax.experimental import pallas as pl
from jax.experimental.pallas import tpu as pltpu
from jax.sharding import PartitionSpec as P

RADIUS = 4
REACH = 5
EPSILON = 1e-05
STEP_LENGTH = 0.5
VARIANCE = 3.0
HIGH = lax.Precision.HIGHEST
F32 = jnp.float32
BF16 = jnp.bfloat16

NZ, NX, NY = 96, 96, 128
WIN = 56
OWN = 48
COUNT = 729.0
BOTH = ("grp", "sub")
DEVICES = 128


def place(xh, co, xl, y, z):
    return (xh * 2 + co) * 32 + xl * 16 + y * 4 + z


def pairs(move):
    out = []
    for xh in range(2):
        for co in range(2):
            for xl in range(2):
                for y in range(4):
                    for z in range(4):
                        target = move(xh, co, xl, y, z)
                        if target is not None:
                            out.append((place(xh, co, xl, y, z), place(*target)))
    return out


def first_round(k):
    return pairs(
        lambda xh, co, xl, y, z: (xh, co, xl, y, (z + k) % 4) if co == 0 else (xh, co, xl, (y + k) % 4, z)
    )


def second_round(k):
    return pairs(
        lambda xh, co, xl, y, z: (xh, co, xl, (y + k) % 4, z) if co == 0 else (xh, co, xl, y, (z + k) % 4)
    )


def third_round(k):
    def move(xh, co, xl, y, z):
        x = (xh * 2 + xl + k) % 4
        return (x // 2, co, x % 2, y, z)

    return pairs(move)


CORE_PAIRS = pairs(lambda xh, co, xl, y, z: (xh, 1 - co, xl, y, z))


def slab_shift(k):
    return [
        (g * 32 + s, g * 32 + s + k) for g in range(4) for s in range(32) if 0 <= s + k < 32
    ]


def permute(x, table):
    return lax.ppermute(x, BOTH, table)


def slab_of(idx, kb, ka, kl):
    b = (idx[1] + kb) & 3
    a = (idx[2] + ka) & 3
    xl = (idx[3] + kl) & 1
    core = idx[0]
    y = jnp.where(core == 0, a, b)
    z = jnp.where(core == 0, b, a)
    return xl * 16 + y * 4 + z


def pair_sum_kernel(idx, ja_ref, jb_ref, o0, o1, o2, o3, page):
    shift = pl.multiple_of(idx[0] * 8, 8)
    for kb, out in enumerate((o0, o1, o2, o3)):

        def step(t, carry):
            slab = slab_of(idx, kb, t // 2, t % 2)
            for j in range(3):
                page[...] = ja_ref[slab * 3 + j].astype(F32) + jb_ref[slab * 3 + j].astype(F32)
                out[t, j] = page[pl.ds(shift, OWN), :]
            return carry

        lax.fori_loop(0, 8, step, 0)


def pair_sum(idx, ja, jb):
    vm = pl.BlockSpec(memory_space=pltpu.VMEM)
    return pl.pallas_call(
        pair_sum_kernel,
        out_shape=[jax.ShapeDtypeStruct((8, 3, OWN, NY), F32)] * 4,
        in_specs=[pl.BlockSpec(memory_space=pltpu.SMEM), vm, vm],
        out_specs=[vm] * 4,
        scratch_shapes=[pltpu.VMEM((WIN, NY), F32)],
        compiler_params=pltpu.CompilerParams(vmem_limit_bytes=24 << 20),
        cost_estimate=pl.CostEstimate(flops=10**6, bytes_accessed=6 * 10**6, transcendentals=0),
        name="pair_sum",
    )(idx, ja, jb)


CHUNK = 4
TOP = 16


def split(product):
    high = product.astype(BF16)
    low = (product - high.astype(F32)).astype(BF16)
    return jnp.concatenate([high, low], axis=1)


def factor_kernel(
    idx, i_ref, ja_ref, jb_ref, o0, o1, o2, o3, cc_ref, iext_ref,
    raw, line, three, ring, zsum,
):
    shift = pl.multiple_of(idx[0] * 8, 8)
    rows = lax.broadcasted_iota(jnp.int32, (2 * NY, NY), 0)
    cols = lax.broadcasted_iota(jnp.int32, (2 * NY, NY), 1)
    away = jnp.abs((rows & (NY - 1)) - cols)
    band2 = jnp.where(away <= RADIUS, 1.0, 0.0).astype(BF16)
    band1 = band2[:NY]
    zero_page = jnp.zeros((OWN, NY), F32)
    line[...] = jnp.zeros(line.shape, F32)
    for v in range(8):
        for p in range(8):
            ring[v, p] = zero_page
        zsum[v, 0] = zero_page
        zsum[v, 1] = zero_page

    def chunk(i, carry):
        base = i * CHUNK

        @pl.when(i < NZ // CHUNK)
        def _():
            def load(ref):
                return ref[pl.ds(base, CHUNK)].reshape(CHUNK * WIN, NY)

            bi, ba, bb = load(i_ref), load(ja_ref), load(jb_ref)
            fi, fa, fb = bi.astype(F32), ba.astype(F32), bb.astype(F32)
            for n, f in enumerate((fi, fa, fb)):
                raw[n, pl.ds(base, CHUNK)] = f.reshape(CHUNK, WIN, NY)

            def dot(lhs, rhs):
                return jnp.dot(lhs, rhs, preferred_element_type=F32)

            makers = (
                lambda: dot(bi, band1),
                lambda: dot(split(fi * fi), band2),
                lambda: dot(ba, band1),
                lambda: dot(split(fa * fa), band2),
                lambda: dot(split(fi * fa), band2),
                lambda: dot(bb, band1),
                lambda: dot(split(fb * fb), band2),
                lambda: dot(split(fi * fb), band2),
            )
            for v in range(8):
                sums = makers[v]()
                for j in range(CHUNK):
                    line[v, j, pl.ds(TOP, WIN), :] = sums[j * WIN : (j + 1) * WIN]
            for v in range(8):
                for j in range(CHUNK):
                    three[v, j, pl.ds(8, 72), :] = (
                        line[v, j, pl.ds(7, 72), :]
                        + line[v, j, pl.ds(8, 72), :]
                        + line[v, j, pl.ds(9, 72), :]
                    )
            for v in range(8):
                for j in range(CHUNK):
                    slot = (base + j) & 7
                    ring[v, slot] = (
                        three[v, j, pl.ds(TOP - 3 + shift, OWN), :]
                        + three[v, j, pl.ds(TOP + shift, OWN), :]
                        + three[v, j, pl.ds(TOP + 3 + shift, OWN), :]
                    )

        @pl.when(i >= NZ // CHUNK)
        def _():
            for v in range(8):
                for j in range(CHUNK):
                    ring[v, (base + j) & 7] = zero_page

        for v in range(8):
            for j in range(CHUNK):
                z = base - 1 + j
                zsum[v, z + 3] = ring[v, (z + 7) & 7] + ring[v, z & 7] + ring[v, (z + 1) & 7]
        return carry

    lax.fori_loop(0, NZ // CHUNK + 1, chunk, 0)

    eps_b = EPSILON * COUNT**2
    eps_bc = EPSILON * COUNT**4

    def block(out, kb, t, cc):
        slab = slab_of(idx, kb, t // 2, t % 2)
        for j in range(3):
            z = slab * 3 + j
            for r in range(OWN // 8):
                part = pl.ds(r * 8, 8)

                def box(v):
                    return zsum[v, z, part, :] + zsum[v, z + 3, part, :] + zsum[v, z + 6, part, :]

                own = pl.ds(shift + r * 8, 8)
                si = box(0)
                var_i = COUNT * box(1) - si * si
                centred = raw[0, z, own, :] - si * (1.0 / COUNT)
                slope = centred / (var_i + eps_b)
                total = None
                for n in range(2):
                    sj = box(2 + 3 * n)
                    var_j = COUNT * box(3 + 3 * n) - sj * sj
                    cross = COUNT * box(4 + 3 * n) - si * sj
                    gain = cross / (var_i * var_j + eps_bc)
                    cc = cc + cross * gain
                    moved = raw[1 + n, z, own, :] - sj * (1.0 / COUNT) - cross * slope
                    term = gain * moved
                    total = term if total is None else total + term
                out[t, j, part, :] = total * (2.0 * COUNT**2)
        return cc

    cc = jnp.zeros((8, NY), F32)
    for kb, out in enumerate((o0, o1, o2, o3)):
        cc = lax.fori_loop(0, 8, lambda t, cc, out=out, kb=kb: block(out, kb, t, cc), cc)
    cc_ref[...] = cc

    start = idx[4] * 3 - 6
    for j in range(15):
        z = start + j
        inside = jnp.logical_and(z >= 0, z < NZ)
        page = raw[0, jnp.clip(z, 0, NZ - 1), pl.ds(shift, OWN), :]
        iext_ref[j] = jnp.where(inside, page, 0.0)


def factors(idx, image, ja, jb):
    vm = pl.BlockSpec(memory_space=pltpu.VMEM)
    block = jax.ShapeDtypeStruct((8, 3, OWN, NY), F32)
    return pl.pallas_call(
        factor_kernel,
        out_shape=[block] * 4
        + [jax.ShapeDtypeStruct((8, NY), F32), jax.ShapeDtypeStruct((15, OWN, NY), F32)],
        in_specs=[pl.BlockSpec(memory_space=pltpu.SMEM), vm, vm, vm],
        out_specs=[vm] * 6,
        scratch_shapes=[
            pltpu.VMEM((3, NZ, WIN, NY), F32),
            pltpu.VMEM((8, CHUNK, 88, NY), F32),
            pltpu.VMEM((8, CHUNK, 88, NY), F32),
            pltpu.VMEM((8, 8, OWN, NY), F32),
            pltpu.VMEM((8, NZ + 6, OWN, NY), F32),
        ],
        compiler_params=pltpu.CompilerParams(vmem_limit_bytes=60 << 20),
        cost_estimate=pl.CostEstimate(flops=10**9, bytes_accessed=10**7, transcendentals=0),
        name="factors",
    )(idx, image, ja, jb)


def gauss(extent):
    weights = [math.exp(-o * o / (2.0 * VARIANCE)) for o in range(-extent, extent + 1)]
    total = sum(weights)
    return [w / total for w in weights]


def smooth_kernel(f_ref, i_ref, u_ref, sq_ref, prod):
    weights = gauss(REACH)
    norm = sum(math.exp(-o * o / (2.0 * VARIANCE)) for o in range(-REACH, REACH + 1))

    def matrix(n):
        r = lax.broadcasted_iota(jnp.int32, (n, n), 0)
        c = lax.broadcasted_iota(jnp.int32, (n, n), 1)
        d = (r - c).astype(F32)
        return jnp.where(jnp.abs(r - c) <= REACH, jnp.exp(-d * d / (2.0 * VARIANCE)) / norm, 0.0)

    gx, gy = matrix(NX), matrix(NY)
    row = lax.broadcasted_iota(jnp.int32, (NX, NY), 0)
    lane = lax.broadcasted_iota(jnp.int32, (NX, NY), 1)
    for p in range(13):
        f = f_ref[p] * 0.5
        here = i_ref[p + 1]
        prod[0, p] = f * (i_ref[p + 2] - i_ref[p])
        below = jnp.where(row == NX - 1, 0.0, pltpu.roll(here, NX - 1, 0))
        above = jnp.where(row == 0, 0.0, pltpu.roll(here, 1, 0))
        prod[1, p] = f * (below - above)
        right = jnp.where(lane == NY - 1, 0.0, pltpu.roll(here, NY - 1, 1))
        left = jnp.where(lane == 0, 0.0, pltpu.roll(here, 1, 1))
        prod[2, p] = f * (right - left)
    square = jnp.zeros((NX, NY), F32)
    for d in range(3):
        for j in range(3):
            acc = prod[d, j] * weights[0]
            for o in range(1, 11):
                acc = acc + prod[d, j + o] * weights[o]
            acc = jnp.dot(acc, gy, precision=HIGH, preferred_element_type=F32)
            acc = jnp.dot(gx, acc, precision=HIGH, preferred_element_type=F32)
            u = acc * (1.0 / DEVICES)
            u_ref[j, d] = u
            square = square + u * u
    sq_ref[...] = jnp.sum(square, axis=0, keepdims=True)


def smooth_slab(f, image):
    vm = pl.BlockSpec(memory_space=pltpu.VMEM)
    return pl.pallas_call(
        smooth_kernel,
        out_shape=[
            jax.ShapeDtypeStruct((3, 3, NX, NY), F32),
            jax.ShapeDtypeStruct((1, NY), F32),
        ],
        in_specs=[vm, vm],
        out_specs=[vm, vm],
        scratch_shapes=[pltpu.VMEM((3, 13, NX, NY), F32)],
        compiler_params=pltpu.CompilerParams(vmem_limit_bytes=24 << 20),
        name="smooth_slab",
    )(f, image)


def two_rounds(blocks):
    got = [permute(blocks[k], first_round(k)) for k in (1, 2, 3)]
    total = blocks[0] + got[0] + got[1] + got[2]
    parts = [total[2 * k : 2 * k + 2] for k in range(4)]
    got = [permute(parts[k], second_round(k)) for k in (1, 2, 3)]
    return parts[0] + got[0] + got[1] + got[2]


def on_device(template, subjects):
    grp = lax.axis_index("grp")
    sub = lax.axis_index("sub")
    core = grp % 2
    xl, y, z = sub // 16, (sub // 4) % 4, sub % 4
    first = jnp.where(core == 0, z, y)
    second = jnp.where(core == 0, y, z)
    idx = jnp.stack([core, first, second, xl, sub]).astype(jnp.int32)

    moving = subjects[0]
    keep = lax.dynamic_slice_in_dim(moving, 40 * core, WIN, axis=1)
    give = lax.dynamic_slice_in_dim(moving, 40 * (1 - core), WIN, axis=1)
    take = permute(give, CORE_PAIRS)

    mine = lax.dynamic_slice_in_dim(template, 40 * core, WIN, axis=1)
    image = lax.all_to_all(
        jnp.broadcast_to(mine[None], (32, 3, WIN, NY)), "sub", 0, 0, tiled=True
    ).reshape(NZ, WIN, NY)

    j_blocks = pair_sum(idx, keep, take)
    *f_blocks, cc, i_half = factors(idx, image, keep, take)
    j_part = two_rounds(j_blocks)
    f_part = two_rounds(f_blocks)
    both = jnp.concatenate([f_part, j_part], axis=1)
    half = both[0] + permute(both[0], third_round(2))
    half = half + permute(both[1], third_round(1)) + permute(both[1], third_round(3))

    def joined(own):
        other = permute(own, CORE_PAIRS)
        low = jnp.where(core == 0, own, other)
        high = jnp.where(core == 0, other, own)
        return jnp.concatenate([low, high], axis=1)

    i_slab = joined(i_half.astype(BF16)).astype(F32)
    slab = joined(half)
    f_slab, m_slab = slab[:3], slab[3:] * (1.0 / DEVICES)
    up1 = permute(jnp.concatenate([f_slab, m_slab[2:]], axis=0), slab_shift(1))
    up2 = permute(f_slab[1:], slab_shift(2))
    down1 = permute(jnp.concatenate([f_slab, m_slab[:1]], axis=0), slab_shift(-1))
    down2 = permute(f_slab[:2], slab_shift(-2))
    f_ext = jnp.concatenate([up2, up1[:3], f_slab, down1[:3], down2], axis=0)
    u, square = smooth_slab(f_ext, i_slab)

    msq = jnp.sum(m_slab * m_slab)
    cc = jnp.sum(cc)
    lane = lax.broadcasted_iota(jnp.int32, (1, NY), 1)
    cc_row = jnp.where(lane == 0, cc, 0.0)
    cc_row = cc_row + permute(cc_row, CORE_PAIRS)
    cc_row = cc_row + permute(cc_row, pairs(lambda xh, co, xl, y, z: (1 - xh, co, xl, y, z)))
    row = jnp.where(lane == 0, jnp.sum(square), jnp.where(lane == 1, msq, jnp.sum(cc_row)))
    rows = lax.all_to_all(jnp.broadcast_to(row[None], (32, 1, NY)), "sub", 0, 0, tiled=True)
    totals = jnp.sum(rows[:, 0, :3], axis=0)

    cells = NZ * NX * NY
    velocity_norm = jnp.sqrt(totals[0] / cells + EPSILON)
    image_norm = jnp.sqrt(totals[1] / cells + EPSILON)
    velocity = u * (STEP_LENGTH / velocity_norm)
    m_ext = jnp.concatenate([up1[3:], m_slab, down1[3:]], axis=0)
    slope_z = (m_ext[2:] - m_ext[:-2]) * 0.5
    padded_x = jnp.pad(m_slab, ((0, 0), (1, 1), (0, 0)))
    slope_x = (padded_x[:, 2:] - padded_x[:, :-2]) * 0.5
    padded_y = jnp.pad(m_slab, ((0, 0), (0, 0), (1, 1)))
    slope_y = (padded_y[:, :, 2:] - padded_y[:, :, :-2]) * 0.5
    advected = velocity[:, 0] * slope_z + velocity[:, 1] * slope_x + velocity[:, 2] * slope_y
    new_template = (m_slab - advected) / image_norm
    similarity = totals[2] / (DEVICES * cells)
    return velocity, new_template, similarity


def solution(mesh):
    return jax.shard_map(
        on_device,
        mesh=mesh,
        in_specs=(P("sub", None, None), P(("grp", "sub"), None, None, None)),
        out_specs=(P("sub", None, None, None), P("sub", None, None), P()),
        check_vma=False,
    )
```

time: 778 us -> 171 us (0.22)
  waiting for transfers between devices: 339 us -> 59.4 us
  matrix products: 186 us -> 0 us
  blocking collectives: 145 us -> 0 us
  starting transfers between devices: 5.96 us -> 54.8 us
  local copies, waits for them, and re-layouts: 42.6 us -> 10.7 us
  Pallas kernels: 0 us -> 31.6 us
  other arithmetic: 33.7 us -> 9.42 us
  between operations: 17.4 us -> 4.19 us
    reduce_scatter x1 -> x0, waiting for transfers between devices: 218 us -> none  [on_device(): lax.psum_scatter(jnp.concatenate([smooth, intensity], axis=1), 'sub', sca...]
    dot_general x18 -> x0, matrix products: 186 us -> none  [the longest x5 56.4 us: filter_volume(): jnp.einsum('ab,bxy->axy', along_z, result, precision=HIGH, preferred_elem...]
    psum x2 -> x0, blocking collectives: 145 us -> none  [the longest x1 81.3 us: on_device(): lax.psum((velocity_square, image_square), 'sub')]
    all_gather x1 -> x0, waiting for transfers between devices: 120 us -> none  [on_device(): lax.all_gather(template, 'sub', axis=0, tiled=True).astype(jnp.float32)]
    pallas_call x0 -> x3, Pallas kernels: none -> 31.6 us  [the longest x1 26 us: factors(): pl.pallas_call(factor_kernel, out_shape=[block] * 4 + [jax.ShapeDtypeStru...]
    ppermute x2 -> x24, waiting for transfers between devices: 0.01 us -> 31.3 us  [permute(): return lax.ppermute(x, BOTH, table)]
    ppermute x2 -> x24, starting transfers between devices: 5.84 us -> 34.7 us  [permute(): return lax.ppermute(x, BOTH, table)]
    all_to_all x0 -> x2, waiting for transfers between devices: none -> 28.1 us  [the longest x1 19.9 us: on_device(): lax.all_to_all(jnp.broadcast_to(mine[None], (32, 3, WIN, NY)), 'sub', 0,...]
  transfers between devices with their start and end apart: 5 -> 26, of which waited for: 2 -> 14; matrix products, arithmetic and copies ran while one was open for 5% -> 4% of each run, Pallas kernels for 0% -> 1%
where the time goes in v1:
time: 171 us; the launch traced here: 170 us
  waiting for transfers between devices  59.4 us (35%)
  starting transfers between devices  54.8 us (32%)
  Pallas kernels  31.6 us (18%)
  local copies, waits for them, and re-layouts  10.7 us (6%)
  other arithmetic  9.42 us (6%)
  between operations  4.19 us (2%)
    ppermute x24, starting transfers between devices, permute(): return lax.ppermute(x, BOTH, table)  34.7 us
    ppermute x24, waiting for transfers between devices, permute(): return lax.ppermute(x, BOTH, table)  31.3 us
    pallas_call x1, Pallas kernels, factors(): pl.pallas_call(factor_kernel, out_shape=[block] * 4 + [jax.ShapeDtypeStru...  26 us
    all_to_all x1, waiting for transfers between devices, on_device(): lax.all_to_all(jnp.broadcast_to(mine[None], (32, 3, WIN, NY)), 'sub', 0,...  19.9 us
    all_to_all x1, starting transfers between devices, on_device(): lax.all_to_all(jnp.broadcast_to(row[None], (32, 1, NY)), 'sub', 0, 0, til...  10.7 us
    all_to_all x1, starting transfers between devices, on_device(): lax.all_to_all(jnp.broadcast_to(mine[None], (32, 3, WIN, NY)), 'sub', 0,...  9.37 us
    all_to_all x1, waiting for transfers between devices, on_device(): lax.all_to_all(jnp.broadcast_to(row[None], (32, 1, NY)), 'sub', 0, 0, til...  8.2 us
    dynamic_slice x1, local copies, waits for them, and re-layouts, on_device(): give = lax.dynamic_slice_in_dim(moving, 40 * (1 - core), WIN, axis=1)  3.77 us
  transfers between devices with their start and end apart: 26, of which 14 were waited for; matrix products, arithmetic and copies ran while one was open for 4% of the time, Pallas kernels for 1%

profile of v1, /device:TPU:0, one launch (start us, length us, event | category | flops | bytes accessed | tf_op | source)
XLA Modules:
  0.0 170.1 jit_solution(6305535993104057498)
XLA Ops:
  0.6 0.0 copy-start
  0.7 3.8 %dynamic-slice_bitcast_fusion = (bf16[96,56,128]{2,1,0:T(8,128)(2,1)}, bf16[96,56,128]{2,1,0:T(8,128)(2,1)}) fusion(bf16[1,96,96,128]{3,2,1,0:T(8,128)(2,1)} %param.3, s32[]{:T(128)S(6)} %select_n.100, s32[]{:T(128)S(6)} %select_n.99), kind=kLoop, calls=%fused_computation | loop fusion | bytes 5505032 | tf_op jit(solution)/shard_map/dynamic_slice | solution.py:347
  4.5 1.3 broadcast_in_dim.32
  5.7 9.4 %all-to-all-start = ((bf16[32,3,56,128]{3,2,1,0:T(8,128)(2,1)}), bf16[32,3,56,128]{3,2,1,0:T(8,128)(2,1)S(1)}, u32[]{:S(2)}, u32[]{:S(2)}) async-start(bf16[32,3,56,128]{3,2,1,0:T(8,128)(2,1)} %broadcast_in_dim.32), calls=%async_computation | async-start | bytes 2752512 | tf_op jit(solution)/shard_map/all_to_all | solution.py:351
  15.2 0.6 stack.23.idx
  15.8 19.9 %all-to-all-done = bf16[32,3,56,128]{3,2,1,0:T(8,128)(2,1)S(1)} async-done(((bf16[32,3,56,128]{3,2,1,0:T(8,128)(2,1)}), bf16[32,3,56,128]{3,2,1,0:T(8,128)(2,1)S(1)}, u32[]{:S(2)}, u32[]{:S(2)}) %all-to-all-start) | async-done | bytes 1376288 | tf_op jit(solution)/shard_map/all_to_all | solution.py:351
  35.7 1.1 copy-done.5
  36.8 0.5 copy-done.2
  37.3 26.0 %factors.1 = (f32[8,3,48,128]{3,2,1,0:T(8,128)}, f32[8,3,48,128]{3,2,1,0:T(8,128)}, f32[8,3,48,128]{3,2,1,0:T(8,128)}, f32[8,3,48,128]{3,2,1,0:T(8,128)}, f32[8,128]{1,0:T(8,128)}, /*index=5*/f32[15,48,128]{2,1,0:T(8,128)}) custom-call(s32[5]{0:T(128)} %stack.23.idx, bf16[96,56,128]{2,1,0:T(8,128)(2,1)} %bitcast.29, ...), custom_call_target="tpu_custom_call" | custom-call | flops 1000000000 | bytes 10000000 | tf_op jit(solution)/shard_map/factors/pallas_call | solution.py:250
  63.3 1.7 collective-permute-start.3
  65.0 1.4 collective-permute-start.2
  66.4 0.7 collective-permute-start.1
  67.1 1.3 copy-done.3
  68.4 2.5 %pair_sum.1 = (f32[8,3,48,128]{3,2,1,0:T(8,128)S(1)}, f32[8,3,48,128]{3,2,1,0:T(8,128)S(1)}, f32[8,3,48,128]{3,2,1,0:T(8,128)S(1)}, f32[8,3,48,128]{3,2,1,0:T(8,128)}) custom-call(s32[5]{0:T(128)S(1)} %copy-done.4, bf16[96,56,128]{2,1,0:T(8,128)(2,1)S(1)} %copy-done.1, bf16[96,56,128]{2,1,0:T(8,128)(2,1)S(1)} %copy-done.3), custom_call_target="tpu_custom_call" | custom-call | flops 1000000 | bytes 6000000 | tf_op jit(solution)/shard_map/pair_sum/pallas_call | solution.py:103
  70.9 2.5 %collective-permute-start.9 = (f32[8,3,48,128]{3,2,1,0:T(8,128)}, f32[8,3,48,128]{3,2,1,0:T(8,128)S(1)}, u32[]{:S(2)}, u32[]{:S(2)}) collective-permute-start(f32[8,3,48,128]{3,2,1,0:T(8,128)} %get-tuple-element.22), channel_id=1, source_target_pairs={{0,3},{1,0},{2,1},{3,2},{4,7},{5,4},{6,5},{7,6},{8,11},{9,8},{10,9... | collective-permute-start | bytes 1769480 | tf_op jit(solution)/shard_map/ppermute | solution.py:74
  73.4 1.0 collective-permute-start.8
  74.4 0.6 reduce_sum.47
  75.0 0.3 collective-permute-start.7
  75.3 0.6 compare_select_fusion
  76.0 0.8 collective-permute-done.2
  76.8 3.3 %collective-permute-start.22 = (f32[1,128]{1,0:T(1,128)S(1)}, f32[1,128]{1,0:T(1,128)S(1)}, u32[]{:S(2)}, u32[]{:S(2)}) collective-permute-start(f32[1,128]{1,0:T(1,128)S(1)} %compare_select_fusion), channel_id=1, source_target_pairs={{0,32},{1,33},{2,34},{3,35},{4,36},{5,37},{6,38},{7,39},{8,40},{9,... | collective-permute-start | bytes 1544 | tf_op jit(solution)/shard_map/ppermute | solution.py:74
  80.1 2.9 %collective-permute-done.1 = f32[8,3,48,128]{3,2,1,0:T(8,128)} collective-permute-done((f32[8,3,48,128]{3,2,1,0:T(8,128)}, f32[8,3,48,128]{3,2,1,0:T(8,128)}, u32[]{:S(2)}, u32[]{:S(2)}) %collective-permute-start.1) | collective-permute-done | bytes 589856 | tf_op jit(solution)/shard_map/ppermute | solution.py:74
  83.0 1.7 %add_add_fusion.1 = f32[8,3,48,128]{3,2,1,0:T(8,128)S(1)} fusion(f32[8,3,48,128]{3,2,1,0:T(8,128)} %collective-permute-done.3, f32[8,3,48,128]{3,2,1,0:T(8,128)} %collective-permute-done.2, f32[8,3,48,128]{3,2,1,0:T(8,128)} %get-tuple-element.15, f32[8,3,48,128]{3,2,1,0:T(8,128)} %collective-permute-done.1), kind=kLoop, calls=%fused_computation.3 | loop fusion | flops 442368 | bytes 2949120 | tf_op jit(solution)/shard_map/add | solution.py:330
  84.8 1.4 collective-permute-start.6
  86.2 0.4 collective-permute-done.9
  86.6 2.7 %collective-permute-start.5 = (f32[2,3,48,128]{3,2,1,0:T(8,128)S(1)}, f32[2,3,48,128]{3,2,1,0:T(8,128)S(1)}, u32[]{:S(2)}, u32[]{:S(2)}) collective-permute-start(f32[2,3,48,128]{3,2,1,0:T(8,128)S(1)} %get-tuple-element.42), channel_id=1, source_target_pairs={{0,8},{1,9},{2,10},{3,11},{4,12},{5,13},{6,14},{7,15},{8,0},{9,1},... | collective-permute-start | bytes 442376 | tf_op jit(solution)/shard_map/ppermute | solution.py:74
  89.3 0.1 collective-permute-done.8
  89.4 1.3 collective-permute-start.4
  90.7 8.1 %collective-permute-done.7 = f32[8,3,48,128]{3,2,1,0:T(8,128)S(1)} collective-permute-done((f32[8,3,48,128]{3,2,1,0:T(8,128)S(1)}, f32[8,3,48,128]{3,2,1,0:T(8,128)S(1)}, u32[]{:S(2)}, u32[]{:S(2)}) %collective-permute-start.7) | collective-permute-done | bytes 589856 | tf_op jit(solution)/shard_map/ppermute | solution.py:74
  98.8 0.1 add_add_fusion
  98.9 0.0 copy-start.6
  99.0 0.1 collective-permute-start.12
  99.0 1.7 collective-permute-start.11
  100.7 0.5 collective-permute-start.10
  101.3 2.9 %collective-permute-done.12 = f32[2,3,48,128]{3,2,1,0:T(8,128)S(1)} collective-permute-done((f32[2,3,48,128]{3,2,1,0:T(8,128)S(1)}, f32[2,3,48,128]{3,2,1,0:T(8,128)S(1)}, u32[]{:S(2)}, u32[]{:S(2)}) %collective-permute-start.12) | collective-permute-done | bytes 147488 | tf_op jit(solution)/shard_map/ppermute | solution.py:74
  104.2 1.6 collective-permute-done.11
  105.8 1.6 collective-permute-done.10
  107.4 2.2 %collective-permute-start.15 = (f32[6,48,128]{2,1,0:T(8,128)S(1)}, f32[6,48,128]{2,1,0:T(8,128)S(1)}, u32[]{:S(2)}, u32[]{:S(2)}) collective-permute-start(f32[6,48,128]{2,1,0:T(8,128)S(1)} %get-tuple-element.54), channel_id=1, source_target_pairs={{0,80},{1,81},{2,82},{3,83},{4,84},{5,85},{6,86},{7,87},{8,88},{9,... | collective-permute-start | bytes 442376 | tf_op jit(solution)/shard_map/ppermute | solution.py:74
  109.7 2.6 %collective-permute-start.13 = (f32[6,48,128]{2,1,0:T(8,128)S(1)}, f32[6,48,128]{2,1,0:T(8,128)S(1)}, u32[]{:S(2)}, u32[]{:S(2)}) collective-permute-start(f32[6,48,128]{2,1,0:T(8,128)S(1)} %get-tuple-element.53), channel_id=1, source_target_pairs={{0,64},{1,65},{2,66},{3,67},{4,68},{5,69},{6,70},{7,71},{8,72},{9,... | collective-permute-start | bytes 442376 | tf_op jit(solution)/shard_map/ppermute | solution.py:74
  112.2 0.7 fusion.24
  112.9 1.0 collective-permute-start.23
  114.0 0.1 collective-permute-start.21
  114.0 4.0 %collective-permute-done.23 = f32[1,128]{1,0:T(1,128)S(1)} collective-permute-done((f32[1,128]{1,0:T(1,128)S(1)}, f32[1,128]{1,0:T(1,128)S(1)}, u32[]{:S(2)}, u32[]{:S(2)}) %collective-permute-start.23) | collective-permute-done | bytes 544 | tf_op jit(solution)/shard_map/ppermute | solution.py:74
  118.1 1.2 add_reduce_fusion
  119.4 0.1 collective-permute-start.16
  119.5 1.3 collective-permute-done.16
  120.9 0.6 multiply_reduce_fusion
  121.5 3.2 %collective-permute-start.17 = (f32[2,96,128]{2,1,0:T(8,128)S(1)}, f32[2,96,128]{2,1,0:T(8,128)S(1)}, u32[]{:S(2)}, u32[]{:S(2)}) collective-permute-start(f32[2,96,128]{2,1,0:T(8,128)S(1)} %get-tuple-element.49), channel_id=1, source_target_pairs={{0,2},{1,3},{2,4},{3,5},{4,6},{5,7},{6,8},{7,9},{8,10},{9,11},{10,... | collective-permute-start | bytes 294920 | tf_op jit(solution)/shard_map/ppermute | solution.py:74
  124.8 4.2 %collective-permute-start.18 = (f32[4,96,128]{2,1,0:T(8,128)S(1)}, f32[4,96,128]{2,1,0:T(8,128)S(1)}, u32[]{:S(2)}, u32[]{:S(2)}) collective-permute-start(f32[4,96,128]{2,1,0:T(8,128)S(1)} %get-tuple-element.56), channel_id=1, source_target_pairs={{0,1},{1,2},{2,3},{3,4},{4,5},{5,6},{6,7},{7,8},{8,9},{9,10},{10,1... | collective-permute-start | bytes 589832 | tf_op jit(solution)/shard_map/ppermute | solution.py:74
  129.0 0.1 maximum_convert_fusion.i_ref
  129.0 1.3 collective-permute-start.19
  130.3 1.5 collective-permute-start.20
  131.9 1.3 collective-permute-done.18
  133.2 6.3 %collective-permute-done.19 = f32[4,96,128]{2,1,0:T(8,128)S(1)} collective-permute-done((f32[4,96,128]{2,1,0:T(8,128)S(1)}, f32[4,96,128]{2,1,0:T(8,128)S(1)}, u32[]{:S(2)}, u32[]{:S(2)}) %collective-permute-start.19) | collective-permute-done | bytes 196640 | tf_op jit(solution)/shard_map/ppermute | solution.py:74
  139.5 3.1 %smooth_slab.1 = (f32[3,3,96,128]{3,2,1,0:T(8,128)S(1)}, f32[1,128]{1,0:T(1,128)S(1)}) custom-call(f32[13,96,128]{2,1,0:T(8,128)S(1)} %constant_dynamic-update-slice_fusion.f_ref, f32[15,96,128]{2,1,0:T(8,128)S(1)} %maximum_convert_fusion.i_ref), custom_call_target="tpu_custom_call" | custom-call | tf_op jit(solution)/shard_map/smooth_slab/pallas_call | solution.py:314
  142.6 0.6 reduce_sum.45
  143.2 1.9 %compare_select_fusion.2 = f32[128]{0:T(128)S(1)} fusion(f32[]{:T(128)} %add_reduce_fusion, f32[]{:T(128)} %get-tuple-element.36, f32[]{:T(128)} %reduce_sum.45), kind=kLoop, calls=%fused_computation.67 | loop fusion | flops 512 | bytes 524 | tf_op jit(solution)/shard_map/jit(_where)/select_n | solution.py:385
  145.1 0.6 broadcast_in_dim.38
  145.7 10.7 %all-to-all-start.1 = ((f32[32,1,128]{2,1,0:T(1,128)}), f32[32,1,128]{2,1,0:T(1,128)S(1)}, u32[]{:S(2)}, u32[]{:S(2)}) async-start(f32[32,1,128]{2,1,0:T(1,128)} %broadcast_in_dim.38), calls=%async_computation.1 | async-start | bytes 32768 | tf_op jit(solution)/shard_map/all_to_all | solution.py:386
  156.5 8.2 %all-to-all-done.1 = f32[32,1,128]{2,1,0:T(1,128)S(1)} async-done(((f32[32,1,128]{2,1,0:T(1,128)}), f32[32,1,128]{2,1,0:T(1,128)S(1)}, u32[]{:S(2)}, u32[]{:S(2)}) %all-to-all-start.1) | async-done | bytes 16416 | tf_op jit(solution)/shard_map/all_to_all | solution.py:386
  164.7 0.1 slice_reduce_fusion
  164.7 0.6 fusion.29
  166.1 0.8 copy.11
  168.2 0.8 fusion.6
  (46 shorter events, 0.5 us)
Async XLA Ops:
  0.6 3.8 %copy-start = (bf16[3,96,128]{2,1,0:T(8,128)(2,1)S(1)}, bf16[3,96,128]{2,1,0:T(8,128)(2,1)}, u32[]{:S(2)}) copy-start(bf16[3,96,128]{2,1,0:T(8,128)(2,1)} %param.2) | copy-start | bytes 221188
  4.4 31.3 %collective-permute-start = (bf16[96,56,128]{2,1,0:T(8,128)(2,1)}, bf16[96,56,128]{2,1,0:T(8,128)(2,1)S(1)}, u32[]{:S(2)}, u32[]{:S(2)}) collective-permute-start(bf16[96,56,128]{2,1,0:T(8,128)(2,1)} %get-tuple-element.38), channel_id=1, source_target_pairs={{0,32},{1,33},{2,34},{3,35},{4,36},{5,37},{6,38},{7,39},{8,40},{9,... | collective-permute-start | bytes 4128776 | tf_op jit(solution)/shard_map/ppermute | solution.py:74
  5.7 30.0 %all-to-all-start = ((bf16[32,3,56,128]{3,2,1,0:T(8,128)(2,1)}), bf16[32,3,56,128]{3,2,1,0:T(8,128)(2,1)S(1)}, u32[]{:S(2)}, u32[]{:S(2)}) async-start(bf16[32,3,56,128]{3,2,1,0:T(8,128)(2,1)} %broadcast_in_dim.32), calls=%async_computation | async-start | bytes 2752512 | tf_op jit(solution)/shard_map/all_to_all | solution.py:351
  35.7 1.1 copy-start.5
  35.7 1.6 copy-start.2
  37.3 29.8 %copy-start.1 = (bf16[96,56,128]{2,1,0:T(8,128)(2,1)S(1)}, bf16[96,56,128]{2,1,0:T(8,128)(2,1)}, u32[]{:S(2)}) copy-start(bf16[96,56,128]{2,1,0:T(8,128)(2,1)} %get-tuple-element.39.ja_ref) | copy-start | bytes 4128772
  37.3 29.8 %copy-start.4 = (s32[5]{0:T(128)S(1)}, s32[5]{0:T(128)}, u32[]{:S(2)}) copy-start(s32[5]{0:T(128)} %stack.23.idx) | copy-start | bytes 64
  63.3 11.7 %collective-permute-start.3 = (f32[8,3,48,128]{3,2,1,0:T(8,128)}, f32[8,3,48,128]{3,2,1,0:T(8,128)}, u32[]{:S(2)}, u32[]{:S(2)}) collective-permute-start(f32[8,3,48,128]{3,2,1,0:T(8,128)} %get-tuple-element.18), channel_id=1, source_target_pairs={{0,3},{1,0},{2,1},{3,2},{4,7},{5,4},{6,5},{7,6},{8,11},{9,8},{10,9... | collective-permute-start | bytes 1769480 | tf_op jit(solution)/shard_map/ppermute | solution.py:74
  65.0 11.8 %collective-permute-start.2 = (f32[8,3,48,128]{3,2,1,0:T(8,128)}, f32[8,3,48,128]{3,2,1,0:T(8,128)}, u32[]{:S(2)}, u32[]{:S(2)}) collective-permute-start(f32[8,3,48,128]{3,2,1,0:T(8,128)} %get-tuple-element.17), channel_id=1, source_target_pairs={{0,2},{1,3},{2,0},{3,1},{4,6},{5,7},{6,4},{7,5},{8,10},{9,11},{10,... | collective-permute-start | bytes 1769480 | tf_op jit(solution)/shard_map/ppermute | solution.py:74
  66.4 16.7 %collective-permute-start.1 = (f32[8,3,48,128]{3,2,1,0:T(8,128)}, f32[8,3,48,128]{3,2,1,0:T(8,128)}, u32[]{:S(2)}, u32[]{:S(2)}) collective-permute-start(f32[8,3,48,128]{3,2,1,0:T(8,128)} %get-tuple-element.16), channel_id=1, source_target_pairs={{0,1},{1,2},{2,3},{3,0},{4,5},{5,6},{6,7},{7,4},{8,9},{9,10},{10,1... | collective-permute-start | bytes 1769480 | tf_op jit(solution)/shard_map/ppermute | solution.py:74
  67.1 1.3 copy-start.3
  68.4 5.9 %copy-start.7 = (f32[8,128]{1,0:T(8,128)S(1)}, f32[8,128]{1,0:T(8,128)}, u32[]{:S(2)}) copy-start(f32[8,128]{1,0:T(8,128)} %get-tuple-element.26) | copy-start | bytes 12292
  70.9 15.7 %collective-permute-start.9 = (f32[8,3,48,128]{3,2,1,0:T(8,128)}, f32[8,3,48,128]{3,2,1,0:T(8,128)S(1)}, u32[]{:S(2)}, u32[]{:S(2)}) collective-permute-start(f32[8,3,48,128]{3,2,1,0:T(8,128)} %get-tuple-element.22), channel_id=1, source_target_pairs={{0,3},{1,0},{2,1},{3,2},{4,7},{5,4},{6,5},{7,6},{8,11},{9,8},{10,9... | collective-permute-start | bytes 1769480 | tf_op jit(solution)/shard_map/ppermute | solution.py:74
  73.4 16.0 %collective-permute-start.8 = (f32[8,3,48,128]{3,2,1,0:T(8,128)S(1)}, f32[8,3,48,128]{3,2,1,0:T(8,128)S(1)}, u32[]{:S(2)}, u32[]{:S(2)}) collective-permute-start(f32[8,3,48,128]{3,2,1,0:T(8,128)S(1)} %get-tuple-element.21), channel_id=1, source_target_pairs={{0,2},{1,3},{2,0},{3,1},{4,6},{5,7},{6,4},{7,5},{8,10},{9,11},{10,... | collective-permute-start | bytes 1769480 | tf_op jit(solution)/shard_map/ppermute | solution.py:74
  75.0 23.8 %collective-permute-start.7 = (f32[8,3,48,128]{3,2,1,0:T(8,128)S(1)}, f32[8,3,48,128]{3,2,1,0:T(8,128)S(1)}, u32[]{:S(2)}, u32[]{:S(2)}) collective-permute-start(f32[8,3,48,128]{3,2,1,0:T(8,128)S(1)} %get-tuple-element.20), channel_id=1, source_target_pairs={{0,1},{1,2},{2,3},{3,0},{4,5},{5,6},{6,7},{7,4},{8,9},{9,10},{10,1... | collective-permute-start | bytes 1769480 | tf_op jit(solution)/shard_map/ppermute | solution.py:74
  76.8 35.4 %collective-permute-start.22 = (f32[1,128]{1,0:T(1,128)S(1)}, f32[1,128]{1,0:T(1,128)S(1)}, u32[]{:S(2)}, u32[]{:S(2)}) collective-permute-start(f32[1,128]{1,0:T(1,128)S(1)} %compare_select_fusion), channel_id=1, source_target_pairs={{0,32},{1,33},{2,34},{3,35},{4,36},{5,37},{6,38},{7,39},{8,40},{9,... | collective-permute-start | bytes 1544 | tf_op jit(solution)/shard_map/ppermute | solution.py:74
  84.8 14.2 %collective-permute-start.6 = (f32[2,3,48,128]{3,2,1,0:T(8,128)S(1)}, f32[2,3,48,128]{3,2,1,0:T(8,128)S(1)}, u32[]{:S(2)}, u32[]{:S(2)}) collective-permute-start(f32[2,3,48,128]{3,2,1,0:T(8,128)S(1)} %get-tuple-element.41), channel_id=1, source_target_pairs={{0,12},{1,13},{2,14},{3,15},{4,0},{5,1},{6,2},{7,3},{8,4},{9,5},{1... | collective-permute-start | bytes 442376 | tf_op jit(solution)/shard_map/ppermute | solution.py:74
  86.6 14.1 %collective-permute-start.5 = (f32[2,3,48,128]{3,2,1,0:T(8,128)S(1)}, f32[2,3,48,128]{3,2,1,0:T(8,128)S(1)}, u32[]{:S(2)}, u32[]{:S(2)}) collective-permute-start(f32[2,3,48,128]{3,2,1,0:T(8,128)S(1)} %get-tuple-element.42), channel_id=1, source_target_pairs={{0,8},{1,9},{2,10},{3,11},{4,12},{5,13},{6,14},{7,15},{8,0},{9,1},... | collective-permute-start | bytes 442376 | tf_op jit(solution)/shard_map/ppermute | solution.py:74
  89.4 11.9 %collective-permute-start.4 = (f32[2,3,48,128]{3,2,1,0:T(8,128)S(1)}, f32[2,3,48,128]{3,2,1,0:T(8,128)S(1)}, u32[]{:S(2)}, u32[]{:S(2)}) collective-permute-start(f32[2,3,48,128]{3,2,1,0:T(8,128)S(1)} %get-tuple-element.40), channel_id=1, source_target_pairs={{0,4},{1,5},{2,6},{3,7},{4,8},{5,9},{6,10},{7,11},{8,12},{9,13},{1... | collective-permute-start | bytes 442376 | tf_op jit(solution)/shard_map/ppermute | solution.py:74
  98.9 15.0 %copy-start.6 = (f32[15,48,128]{2,1,0:T(8,128)S(1)}, f32[15,48,128]{2,1,0:T(8,128)}, u32[]{:S(2)}) copy-start(f32[15,48,128]{2,1,0:T(8,128)} %get-tuple-element.23) | copy-start | bytes 1105924
  99.0 5.2 %collective-permute-start.12 = (f32[2,3,48,128]{3,2,1,0:T(8,128)S(1)}, f32[2,3,48,128]{3,2,1,0:T(8,128)S(1)}, u32[]{:S(2)}, u32[]{:S(2)}) collective-permute-start(f32[2,3,48,128]{3,2,1,0:T(8,128)S(1)} %get-tuple-element.44), channel_id=1, source_target_pairs={{0,12},{1,13},{2,14},{3,15},{4,0},{5,1},{6,2},{7,3},{8,4},{9,5},{1... | collective-permute-start | bytes 442376 | tf_op jit(solution)/shard_map/ppermute | solution.py:74
  99.0 6.8 %collective-permute-start.11 = (f32[2,3,48,128]{3,2,1,0:T(8,128)S(1)}, f32[2,3,48,128]{3,2,1,0:T(8,128)S(1)}, u32[]{:S(2)}, u32[]{:S(2)}) collective-permute-start(f32[2,3,48,128]{3,2,1,0:T(8,128)S(1)} %get-tuple-element.45), channel_id=1, source_target_pairs={{0,8},{1,9},{2,10},{3,11},{4,12},{5,13},{6,14},{7,15},{8,0},{9,1},... | collective-permute-start | bytes 442376 | tf_op jit(solution)/shard_map/ppermute | solution.py:74
  100.7 6.6 %collective-permute-start.10 = (f32[2,3,48,128]{3,2,1,0:T(8,128)S(1)}, f32[2,3,48,128]{3,2,1,0:T(8,128)S(1)}, u32[]{:S(2)}, u32[]{:S(2)}) collective-permute-start(f32[2,3,48,128]{3,2,1,0:T(8,128)S(1)} %get-tuple-element.43), channel_id=1, source_target_pairs={{0,4},{1,5},{2,6},{3,7},{4,8},{5,9},{6,10},{7,11},{8,12},{9,13},{1... | collective-permute-start | bytes 442376 | tf_op jit(solution)/shard_map/ppermute | solution.py:74
  107.4 11.9 %collective-permute-start.15 = (f32[6,48,128]{2,1,0:T(8,128)S(1)}, f32[6,48,128]{2,1,0:T(8,128)S(1)}, u32[]{:S(2)}, u32[]{:S(2)}) collective-permute-start(f32[6,48,128]{2,1,0:T(8,128)S(1)} %get-tuple-element.54), channel_id=1, source_target_pairs={{0,80},{1,81},{2,82},{3,83},{4,84},{5,85},{6,86},{7,87},{8,88},{9,... | collective-permute-start | bytes 442376 | tf_op jit(solution)/shard_map/ppermute | solution.py:74
  109.6 9.7 %collective-permute-start.14 = (f32[6,48,128]{2,1,0:T(8,128)S(1)}, f32[6,48,128]{2,1,0:T(8,128)S(1)}, u32[]{:S(2)}, u32[]{:S(2)}) collective-permute-start(f32[6,48,128]{2,1,0:T(8,128)S(1)} %get-tuple-element.54), channel_id=1, source_target_pairs={{0,16},{1,17},{2,18},{3,19},{4,20},{5,21},{6,22},{7,23},{8,24},{9,... | collective-permute-start | bytes 442376 | tf_op jit(solution)/shard_map/ppermute | solution.py:74
  109.7 9.7 %collective-permute-start.13 = (f32[6,48,128]{2,1,0:T(8,128)S(1)}, f32[6,48,128]{2,1,0:T(8,128)S(1)}, u32[]{:S(2)}, u32[]{:S(2)}) collective-permute-start(f32[6,48,128]{2,1,0:T(8,128)S(1)} %get-tuple-element.53), channel_id=1, source_target_pairs={{0,64},{1,65},{2,66},{3,67},{4,68},{5,69},{6,70},{7,71},{8,72},{9,... | collective-permute-start | bytes 442376 | tf_op jit(solution)/shard_map/ppermute | solution.py:74
  112.9 5.2 %collective-permute-start.23 = (f32[1,128]{1,0:T(1,128)S(1)}, f32[1,128]{1,0:T(1,128)S(1)}, u32[]{:S(2)}, u32[]{:S(2)}) collective-permute-start(f32[1,128]{1,0:T(1,128)S(1)} %fusion.24), channel_id=1, source_target_pairs={{0,64},{1,65},{2,66},{3,67},{4,68},{5,69},{6,70},{7,71},{8,72},{9,... | collective-permute-start | bytes 1544 | tf_op jit(solution)/shard_map/ppermute | solution.py:74
  114.0 5.5 %collective-permute-start.21 = (bf16[15,48,128]{2,1,0:T(8,128)(2,1)S(1)}, bf16[15,48,128]{2,1,0:T(8,128)(2,1)S(1)}, u32[]{:S(2)}, u32[]{:S(2)}) collective-permute-start(bf16[15,48,128]{2,1,0:T(8,128)(2,1)S(1)} %convert_element_type.10), channel_id=1, source_target_pairs={{0,32},{1,33},{2,34},{3,35},{4,36},{5,37},{6,38},{7,39},{8,40},{9,... | collective-permute-start | bytes 552968 | tf_op jit(solution)/shard_map/ppermute | solution.py:74
  119.4 1.5 collective-permute-start.16
  121.5 10.3 %collective-permute-start.17 = (f32[2,96,128]{2,1,0:T(8,128)S(1)}, f32[2,96,128]{2,1,0:T(8,128)S(1)}, u32[]{:S(2)}, u32[]{:S(2)}) collective-permute-start(f32[2,96,128]{2,1,0:T(8,128)S(1)} %get-tuple-element.49), channel_id=1, source_target_pairs={{0,2},{1,3},{2,4},{3,5},{4,6},{5,7},{6,8},{7,9},{8,10},{9,11},{10,... | collective-permute-start | bytes 294920 | tf_op jit(solution)/shard_map/ppermute | solution.py:74
  124.8 8.4 %collective-permute-start.18 = (f32[4,96,128]{2,1,0:T(8,128)S(1)}, f32[4,96,128]{2,1,0:T(8,128)S(1)}, u32[]{:S(2)}, u32[]{:S(2)}) collective-permute-start(f32[4,96,128]{2,1,0:T(8,128)S(1)} %get-tuple-element.56), channel_id=1, source_target_pairs={{0,1},{1,2},{2,3},{3,4},{4,5},{5,6},{6,7},{7,8},{8,9},{9,10},{10,1... | collective-permute-start | bytes 589832 | tf_op jit(solution)/shard_map/ppermute | solution.py:74
  129.0 10.4 %collective-permute-start.19 = (f32[4,96,128]{2,1,0:T(8,128)S(1)}, f32[4,96,128]{2,1,0:T(8,128)S(1)}, u32[]{:S(2)}, u32[]{:S(2)}) collective-permute-start(f32[4,96,128]{2,1,0:T(8,128)S(1)} %get-tuple-element.55), channel_id=1, source_target_pairs={{1,0},{2,1},{3,2},{4,3},{5,4},{6,5},{7,6},{8,7},{9,8},{10,9},{11,1... | collective-permute-start | bytes 589832 | tf_op jit(solution)/shard_map/ppermute | solution.py:74
  130.3 9.1 %collective-permute-start.20 = (f32[2,96,128]{2,1,0:T(8,128)S(1)}, f32[2,96,128]{2,1,0:T(8,128)S(1)}, u32[]{:S(2)}, u32[]{:S(2)}) collective-permute-start(f32[2,96,128]{2,1,0:T(8,128)S(1)} %get-tuple-element.48), channel_id=1, source_target_pairs={{2,0},{3,1},{4,2},{5,3},{6,4},{7,5},{8,6},{9,7},{10,8},{11,9},{12,... | collective-permute-start | bytes 294920 | tf_op jit(solution)/shard_map/ppermute | solution.py:74
  145.7 18.9 %all-to-all-start.1 = ((f32[32,1,128]{2,1,0:T(1,128)}), f32[32,1,128]{2,1,0:T(1,128)S(1)}, u32[]{:S(2)}, u32[]{:S(2)}) async-start(f32[32,1,128]{2,1,0:T(1,128)} %broadcast_in_dim.38), calls=%async_computation.1 | async-start | bytes 32768 | tf_op jit(solution)/shard_map/all_to_all | solution.py:386

commit v2 on v1

v2 whole, which is shorter than its diff:
```python
import math

import jax
import jax.numpy as jnp
from jax import lax
from jax.experimental import pallas as pl
from jax.experimental.pallas import tpu as pltpu
from jax.sharding import PartitionSpec as P

RADIUS = 4
REACH = 5
EPSILON = 1e-05
STEP_LENGTH = 0.5
VARIANCE = 3.0
HIGH = lax.Precision.HIGHEST
F32 = jnp.float32
BF16 = jnp.bfloat16

NZ, NX, NY = 96, 96, 128
WIN = 56
OWN = 48
COUNT = 729.0
BOTH = ("grp", "sub")
DEVICES = 128


def place(xh, co, xl, y, z):
    return (xh * 2 + co) * 32 + xl * 16 + y * 4 + z


def pairs(move):
    out = []
    for xh in range(2):
        for co in range(2):
            for xl in range(2):
                for y in range(4):
                    for z in range(4):
                        target = move(xh, co, xl, y, z)
                        if target is not None:
                            out.append((place(xh, co, xl, y, z), place(*target)))
    return out


def first_round(k):
    return pairs(
        lambda xh, co, xl, y, z: (xh, co, xl, y, (z + k) % 4) if co == 0 else (xh, co, xl, (y + k) % 4, z)
    )


def second_round(k):
    return pairs(
        lambda xh, co, xl, y, z: (xh, co, xl, (y + k) % 4, z) if co == 0 else (xh, co, xl, y, (z + k) % 4)
    )


def third_round(k):
    def move(xh, co, xl, y, z):
        x = (xh * 2 + xl + k) % 4
        return (x // 2, co, x % 2, y, z)

    return pairs(move)


CORE_PAIRS = pairs(lambda xh, co, xl, y, z: (xh, 1 - co, xl, y, z))


def slab_shift(k):
    return [
        (g * 32 + s, g * 32 + s + k) for g in range(4) for s in range(32) if 0 <= s + k < 32
    ]


def permute(x, table):
    return lax.ppermute(x, BOTH, table)


def slab_of(idx, kb, ka, kl):
    b = (idx[1] + kb) & 3
    a = (idx[2] + ka) & 3
    xl = (idx[3] + kl) & 1
    core = idx[0]
    y = jnp.where(core == 0, a, b)
    z = jnp.where(core == 0, b, a)
    return xl * 16 + y * 4 + z


def pair_sum_kernel(idx, ja_ref, jb_ref, o0, o1, o2, o3, page):
    shift = pl.multiple_of(idx[0] * 8, 8)
    for kb, out in enumerate((o0, o1, o2, o3)):

        def step(t, carry):
            slab = slab_of(idx, kb, t // 2, t % 2)
            for j in range(3):
                page[...] = ja_ref[slab * 3 + j].astype(F32) + jb_ref[slab * 3 + j].astype(F32)
                out[t, j] = page[pl.ds(shift, OWN), :]
            return carry

        lax.fori_loop(0, 8, step, 0)


def pair_sum(idx, ja, jb):
    vm = pl.BlockSpec(memory_space=pltpu.VMEM)
    return pl.pallas_call(
        pair_sum_kernel,
        out_shape=[jax.ShapeDtypeStruct((8, 3, OWN, NY), F32)] * 4,
        in_specs=[pl.BlockSpec(memory_space=pltpu.SMEM), vm, vm],
        out_specs=[vm] * 4,
        scratch_shapes=[pltpu.VMEM((WIN, NY), F32)],
        compiler_params=pltpu.CompilerParams(vmem_limit_bytes=24 << 20),
        cost_estimate=pl.CostEstimate(flops=10**6, bytes_accessed=6 * 10**6, transcendentals=0),
        name="pair_sum",
    )(idx, ja, jb)


CHUNK = 4
TOP = 16
PAGES = NZ + 8


def split(product):
    high = product.astype(BF16)
    low = (product - high.astype(F32)).astype(BF16)
    return jnp.concatenate([high, low], axis=1)


def bands():
    rows = lax.broadcasted_iota(jnp.int32, (2 * NY, NY), 0)
    cols = lax.broadcasted_iota(jnp.int32, (2 * NY, NY), 1)
    away = jnp.abs((rows & (NY - 1)) - cols)
    band2 = jnp.where(away <= RADIUS, 1.0, 0.0).astype(BF16)
    return band2[:NY], band2


def plane_sums(makers, shift, even, odd, three, plane):
    band1, band2 = bands()
    volumes = plane.shape[0]
    even[...] = jnp.zeros(even.shape, F32)
    odd[...] = jnp.zeros(odd.shape, F32)
    for v in range(volumes):
        for p in range(4):
            plane[v, NZ + 4 + p] = jnp.zeros((OWN, NY), F32)

    def along_y(thunk, v, line):
        sums = thunk(band1, band2)
        for j in range(CHUNK):
            line[v, j, pl.ds(TOP, WIN), :] = sums[j * WIN : (j + 1) * WIN]

    def along_x(v, line, base):
        for j in range(CHUNK):
            three[v, j] = (
                line[v, j, pl.ds(TOP - 9 + shift, 64), :]
                + line[v, j, pl.ds(TOP - 8 + shift, 64), :]
                + line[v, j, pl.ds(TOP - 7 + shift, 64), :]
            )
        for j in range(CHUNK):
            plane[v, base + j + 4] = (
                three[v, j, pl.ds(5, OWN), :]
                + three[v, j, pl.ds(8, OWN), :]
                + three[v, j, pl.ds(11, OWN), :]
            )

    def both(i, line, other):
        thunks = makers(i * CHUNK)
        for v in range(volumes):
            along_y(thunks[v], v, line)
            along_x(v, other, (i - 1) * CHUNK)

    def step(n, carry):
        both(2 * n, even, odd)
        both(2 * n + 1, odd, even)
        return carry

    lax.fori_loop(0, NZ // CHUNK // 2, step, 0)
    for v in range(volumes):
        along_x(v, odd, NZ - CHUNK)


def dot(lhs, rhs):
    return jnp.dot(lhs, rhs, preferred_element_type=F32)


def load(ref, base):
    return ref[pl.ds(base, CHUNK)].reshape(CHUNK * WIN, NY)


def moving_kernel(idx, ja_ref, jb_ref, plane, even, odd, three):
    shift = pl.multiple_of(idx[0] * 8, 8)

    def makers(base):
        out = []
        for ref in (ja_ref, jb_ref):

            def square(b1, b2, ref=ref):
                f = load(ref, base).astype(F32)
                return dot(split(f * f), b2)

            out.append(lambda b1, b2, ref=ref: dot(load(ref, base), b1))
            out.append(square)
        return out

    plane_sums(makers, shift, even, odd, three, plane)


def moving_planes(idx, ja, jb):
    vm = pl.BlockSpec(memory_space=pltpu.VMEM)
    return pl.pallas_call(
        moving_kernel,
        out_shape=jax.ShapeDtypeStruct((4, PAGES, OWN, NY), F32),
        in_specs=[pl.BlockSpec(memory_space=pltpu.SMEM), vm, vm],
        out_specs=vm,
        scratch_shapes=[
            pltpu.VMEM((4, CHUNK, 88, NY), F32),
            pltpu.VMEM((4, CHUNK, 88, NY), F32),
            pltpu.VMEM((4, CHUNK, 64, NY), F32),
        ],
        compiler_params=pltpu.CompilerParams(vmem_limit_bytes=24 << 20),
        cost_estimate=pl.CostEstimate(flops=4 * 10**9, bytes_accessed=13 * 10**6, transcendentals=0),
        name="moving_planes",
    )(idx, ja, jb)


def factor_kernel(
    idx, i_ref, ja_ref, jb_ref, jplane, o0, o1, o2, o3, cc_ref, iext_ref,
    raw, even, odd, three, iplane,
):
    shift = pl.multiple_of(idx[0] * 8, 8)

    def makers(base):
        def wide(n, keep):
            f = load((i_ref, ja_ref, jb_ref)[n], base).astype(F32)
            if keep:
                raw[n, pl.ds(base, CHUNK)] = f.reshape(CHUNK, WIN, NY)
            return f

        def square(b1, b2):
            f = wide(0, True)
            return dot(split(f * f), b2)

        return [
            lambda b1, b2: dot(load(i_ref, base), b1),
            square,
            lambda b1, b2: dot(split(wide(0, False) * wide(1, True)), b2),
            lambda b1, b2: dot(split(wide(0, False) * wide(2, True)), b2),
        ]

    plane_sums(makers, shift, even, odd, three, iplane)

    eps_b = EPSILON * COUNT**2
    eps_bc = EPSILON * COUNT**4

    def block(out, kb, t, cc):
        slab = slab_of(idx, kb, t // 2, t % 2)
        first = slab * 3
        for r in range(OWN // 8):
            part = pl.ds(r * 8, 8)

            def boxes(ref, v):
                pages = [ref[v, first + p, part, :] for p in range(11)]
                mid = pages[2]
                for p in range(3, 9):
                    mid = mid + pages[p]
                return (
                    mid + (pages[0] + pages[1]),
                    mid + (pages[1] + pages[9]),
                    mid + (pages[9] + pages[10]),
                )

            own = pl.ds(shift + r * 8, 8)
            si, sii = boxes(iplane, 0), boxes(iplane, 1)
            var_i = [COUNT * sii[j] - si[j] * si[j] for j in range(3)]
            slope = [
                (raw[0, first + j, own, :] - si[j] * (1.0 / COUNT)) / (var_i[j] + eps_b)
                for j in range(3)
            ]
            total = [None] * 3
            for n in range(2):
                sj, sjj = boxes(jplane, 2 * n), boxes(jplane, 2 * n + 1)
                sij = boxes(iplane, 2 + n)
                for j in range(3):
                    var_j = COUNT * sjj[j] - sj[j] * sj[j]
                    cross = COUNT * sij[j] - si[j] * sj[j]
                    gain = cross / (var_i[j] * var_j + eps_bc)
                    cc = cc + cross * gain
                    moved = raw[1 + n, first + j, own, :] - sj[j] * (1.0 / COUNT) - cross * slope[j]
                    term = gain * moved
                    total[j] = term if n == 0 else total[j] + term
            for j in range(3):
                out[t, j, part, :] = total[j] * (2.0 * COUNT**2)
        return cc

    cc = jnp.zeros((8, NY), F32)
    for kb, out in enumerate((o0, o1, o2, o3)):
        cc = lax.fori_loop(0, 8, lambda t, cc, out=out, kb=kb: block(out, kb, t, cc), cc)
    cc_ref[...] = cc

    start = idx[4] * 3 - 6
    for j in range(15):
        z = start + j
        inside = jnp.logical_and(z >= 0, z < NZ)
        page = raw[0, jnp.clip(z, 0, NZ - 1), pl.ds(shift, OWN), :]
        iext_ref[j] = jnp.where(inside, page, 0.0)


def factors(idx, image, ja, jb, jplane):
    vm = pl.BlockSpec(memory_space=pltpu.VMEM)
    block = jax.ShapeDtypeStruct((8, 3, OWN, NY), F32)
    return pl.pallas_call(
        factor_kernel,
        out_shape=[block] * 4
        + [jax.ShapeDtypeStruct((8, NY), F32), jax.ShapeDtypeStruct((15, OWN, NY), F32)],
        in_specs=[pl.BlockSpec(memory_space=pltpu.SMEM), vm, vm, vm, vm],
        out_specs=[vm] * 6,
        scratch_shapes=[
            pltpu.VMEM((3, NZ, WIN, NY), F32),
            pltpu.VMEM((4, CHUNK, 88, NY), F32),
            pltpu.VMEM((4, CHUNK, 88, NY), F32),
            pltpu.VMEM((4, CHUNK, 64, NY), F32),
            pltpu.VMEM((4, PAGES, OWN, NY), F32),
        ],
        compiler_params=pltpu.CompilerParams(vmem_limit_bytes=44 << 20),
        cost_estimate=pl.CostEstimate(flops=4 * 10**9, bytes_accessed=18 * 10**6, transcendentals=0),
        name="factors",
    )(idx, image, ja, jb, jplane)


EXT = 18
CC_ROWS = 8


def smooth_kernel(idx, own_ref, other_ref, iown_ref, iother_ref, u_ref, adv_ref, m_ref, st_ref, ext, image, prod):
    mine = pl.multiple_of(idx[0] * OWN, 8)
    others = pl.multiple_of((1 - idx[0]) * OWN, 8)
    for p in range(EXT):
        ext[p, pl.ds(mine, OWN), :] = own_ref[pl.ds(p * OWN, OWN), :]
        ext[p, pl.ds(others, OWN), :] = other_ref[pl.ds(p * OWN, OWN), :]
    for p in range(15):
        image[p, pl.ds(mine, OWN), :] = iown_ref[p]
        image[p, pl.ds(others, OWN), :] = iother_ref[p]

    weights = [math.exp(-o * o / (2.0 * VARIANCE)) for o in range(-REACH, REACH + 1)]
    norm = sum(weights)
    weights = [w / norm for w in weights]

    def matrix(n):
        r = lax.broadcasted_iota(jnp.int32, (n, n), 0)
        c = lax.broadcasted_iota(jnp.int32, (n, n), 1)
        d = (r - c).astype(F32)
        return jnp.where(jnp.abs(r - c) <= REACH, jnp.exp(-d * d / (2.0 * VARIANCE)) / norm, 0.0)

    gx, gy = matrix(NX), matrix(NY)
    row = lax.broadcasted_iota(jnp.int32, (NX, NY), 0)
    lane = lax.broadcasted_iota(jnp.int32, (NX, NY), 1)

    def twice_slopes(here):
        below = jnp.where(row == NX - 1, 0.0, pltpu.roll(here, NX - 1, 0))
        above = jnp.where(row == 0, 0.0, pltpu.roll(here, 1, 0))
        right = jnp.where(lane == NY - 1, 0.0, pltpu.roll(here, NY - 1, 1))
        left = jnp.where(lane == 0, 0.0, pltpu.roll(here, 1, 1))
        return below - above, right - left

    for p in range(13):
        f = ext[p] * 0.5
        sx, sy = twice_slopes(image[p + 1])
        prod[0, p] = f * (image[p + 2] - image[p])
        prod[1, p] = f * sx
        prod[2, p] = f * sy
    square = jnp.zeros((NX, NY), F32)
    image_square = jnp.zeros((NX, NY), F32)
    mean = 1.0 / DEVICES
    for j in range(3):
        m = ext[14 + j] * mean
        sx, sy = twice_slopes(m)
        slopes = ((ext[15 + j] - ext[13 + j]) * mean, sx, sy)
        image_square = image_square + m * m
        moved = None
        for d in range(3):
            acc = prod[d, j] * weights[0]
            for o in range(1, 11):
                acc = acc + prod[d, j + o] * weights[o]
            acc = jnp.dot(acc, gy, precision=HIGH, preferred_element_type=F32)
            acc = jnp.dot(gx, acc, precision=HIGH, preferred_element_type=F32)
            u = acc * mean
            u_ref[j, d] = u
            square = square + u * u
            term = u * slopes[d]
            moved = term if d == 0 else moved + term
        adv_ref[j] = moved * 0.5
        m_ref[j] = m
    tail = pl.ds(EXT * OWN, CC_ROWS)
    cc = jnp.sum(own_ref[tail, :] + other_ref[tail, :])
    one = lax.broadcasted_iota(jnp.int32, (1, NY), 1)
    st_ref[...] = jnp.where(
        one == 0, jnp.sum(square), jnp.where(one == 1, jnp.sum(image_square), cc)
    )


def smooth_slab(idx, own, other, iown, iother):
    vm = pl.BlockSpec(memory_space=pltpu.VMEM)
    return pl.pallas_call(
        smooth_kernel,
        out_shape=[
            jax.ShapeDtypeStruct((3, 3, NX, NY), F32),
            jax.ShapeDtypeStruct((3, NX, NY), F32),
            jax.ShapeDtypeStruct((3, NX, NY), F32),
            jax.ShapeDtypeStruct((1, NY), F32),
        ],
        in_specs=[pl.BlockSpec(memory_space=pltpu.SMEM), vm, vm, vm, vm],
        out_specs=[vm] * 4,
        scratch_shapes=[
            pltpu.VMEM((EXT, NX, NY), F32),
            pltpu.VMEM((15, NX, NY), F32),
            pltpu.VMEM((3, 13, NX, NY), F32),
        ],
        compiler_params=pltpu.CompilerParams(vmem_limit_bytes=24 << 20),
        cost_estimate=pl.CostEstimate(flops=10**8, bytes_accessed=3 * 10**6, transcendentals=0),
        name="smooth_slab",
    )(idx, own, other, iown, iother)


def after(value, *others):
    return lax.optimization_barrier((value, *others))[0]


def round_one(blocks):
    return [permute(blocks[k], first_round(k)) for k in (1, 2, 3)]


def round_two(total):
    parts = [total[2 * k : 2 * k + 2] for k in range(4)]
    got = [permute(parts[k], second_round(k)) for k in (1, 2, 3)]
    return parts[0] + got[0] + got[1] + got[2]


def on_device(template, subjects):
    grp = lax.axis_index("grp")
    sub = lax.axis_index("sub")
    core = grp % 2
    xl, y, z = sub // 16, (sub // 4) % 4, sub % 4
    first = jnp.where(core == 0, z, y)
    second = jnp.where(core == 0, y, z)
    idx = jnp.stack([core, first, second, xl, sub]).astype(jnp.int32)

    mine = lax.dynamic_slice_in_dim(template, 40 * core, WIN, axis=1)
    copies = jnp.broadcast_to(mine[None], (32, 3, WIN, NY))
    copies, moving = lax.optimization_barrier((copies, subjects))
    image = lax.all_to_all(copies, "sub", 0, 0, tiled=True).reshape(NZ, WIN, NY)

    moving = moving[0]
    give = lax.dynamic_slice_in_dim(moving, 40 * (1 - core), WIN, axis=1)
    take = permute(give, CORE_PAIRS)
    keep = lax.dynamic_slice_in_dim(moving, 40 * core, WIN, axis=1)

    j_blocks = pair_sum(idx, keep, take)
    jplane = moving_planes(after(idx, *j_blocks), keep, take)
    j_blocks, jplane = lax.optimization_barrier((j_blocks, jplane))
    j_got = round_one(j_blocks)
    *f_blocks, cc, i_half = factors(idx, image, keep, take, jplane)
    f_got = round_one(f_blocks)
    j_own = after(j_blocks[0], cc)
    j_part = round_two(j_own + j_got[0] + j_got[1] + j_got[2])
    f_part = round_two(f_blocks[0] + f_got[0] + f_got[1] + f_got[2])
    i_other = permute(i_half.astype(BF16), CORE_PAIRS).astype(F32)

    both = jnp.concatenate(
        [
            f_part.reshape(2, 3 * OWN, NY),
            j_part.reshape(2, 3 * OWN, NY),
            jnp.broadcast_to(cc[None], (2, CC_ROWS, NY)),
        ],
        axis=1,
    )
    half = both[0] + permute(both[0], third_round(2))
    half = half + permute(both[1], third_round(1)) + permute(both[1], third_round(3))

    f_half = half[: 3 * OWN]
    m_half = half[3 * OWN : 6 * OWN]
    up1 = permute(jnp.concatenate([f_half, m_half[2 * OWN :]], axis=0), slab_shift(1))
    down1 = permute(jnp.concatenate([f_half, m_half[:OWN]], axis=0), slab_shift(-1))
    up2 = permute(f_half[OWN:], slab_shift(2))
    down2 = permute(f_half[: 2 * OWN], slab_shift(-2))
    ext = jnp.concatenate(
        [
            up2, up1[: 3 * OWN], f_half, down1[: 3 * OWN], down2,
            up1[3 * OWN :], m_half, down1[3 * OWN :], half[6 * OWN :],
        ],
        axis=0,
    )
    other = permute(ext, CORE_PAIRS)
    u, advected, m, stats = smooth_slab(idx, ext, other, i_half, i_other)

    rows = lax.all_to_all(jnp.broadcast_to(stats[None], (32, 1, NY)), "sub", 0, 0, tiled=True)
    totals = jnp.sum(rows[:, 0, :3], axis=0)
    cells = NZ * NX * NY
    velocity_norm = jnp.sqrt(totals[0] / cells + EPSILON)
    image_norm = jnp.sqrt(totals[1] / cells + EPSILON)
    scale = STEP_LENGTH / velocity_norm
    velocity = u * scale
    new_template = (m - advected * scale) / image_norm
    similarity = totals[2] * 0.5 / (DEVICES * cells)
    return velocity, new_template, similarity


def solution(mesh):
    return jax.shard_map(
        on_device,
        mesh=mesh,
        in_specs=(P("sub", None, None), P(("grp", "sub"), None, None, None)),
        out_specs=(P("sub", None, None, None), P("sub", None, None), P()),
        check_vma=False,
    )
```

time: 171 us -> 159 us (0.930)
  waiting for transfers between devices: 59.4 us -> 36.3 us
  blocking collectives: 0 us -> 21.4 us
  other arithmetic: 9.42 us -> 2.09 us
  starting transfers between devices: 54.8 us -> 52.4 us
  local copies, waits for them, and re-layouts: 10.7 us -> 12.7 us
    all_to_all x2 -> x1, waiting for transfers between devices: 28.1 us -> 6.32 us  [on_device(): image = lax.all_to_all(copies, 'sub', 0, 0, tiled=True).reshape(NZ, WIN, NY)]
    all_to_all x0 -> x1, blocking collectives: none -> 21.4 us  [on_device(): lax.all_to_all(jnp.broadcast_to(stats[None], (32, 1, NY)), 'sub', 0, 0, t...]
    all_to_all x2 -> x1, starting transfers between devices: 20.1 us -> 9.49 us  [on_device(): image = lax.all_to_all(copies, 'sub', 0, 0, tiled=True).reshape(NZ, WIN, NY)]
    ppermute x24 -> x22, starting transfers between devices: 34.7 us -> 42.9 us  [permute(): return lax.ppermute(x, BOTH, table)]
    pallas_call x1, Pallas kernels: 26 us -> 18.4 us  [factors(): pl.pallas_call(factor_kernel, out_shape=[block] * 4 + [jax.ShapeDtypeStru...]
    pallas_call x0 -> x1, Pallas kernels: none -> 6.12 us  [moving_planes(): pl.pallas_call(moving_kernel, out_shape=jax.ShapeDtypeStruct((4, PAGES, O...]
    unnamed x21 -> x24, local copies, waits for them, and re-layouts: 3.77 us -> 7.26 us
    reduce_sum x4 -> x0, other arithmetic: 3.09 us -> none  [the longest x1 1.25 us: on_device(): jnp.sum(cc_row)]
  transfers between devices with their start and end apart: 26 -> 23, of which waited for: 14 -> 13; matrix products, arithmetic and copies ran while one was open for 4% -> 0% of each run, Pallas kernels for 1% -> 5%
where the time goes in v2:
time: 159 us
  starting transfers between devices  52.4 us (33%)
  waiting for transfers between devices  36.3 us (23%)
  Pallas kernels  29.9 us (19%)
  blocking collectives  21.4 us (13%)
  local copies, waits for them, and re-layouts  12.7 us (8%)
  between operations  4.19 us (3%)
  other arithmetic  2.09 us (1%)
    ppermute x22, starting transfers between devices, permute(): return lax.ppermute(x, BOTH, table)  42.9 us
    ppermute x22, waiting for transfers between devices, permute(): return lax.ppermute(x, BOTH, table)  30 us
    all_to_all x1, blocking collectives, on_device(): lax.all_to_all(jnp.broadcast_to(stats[None], (32, 1, NY)), 'sub', 0, 0, t...  21.4 us
    pallas_call x1, Pallas kernels, factors(): pl.pallas_call(factor_kernel, out_shape=[block] * 4 + [jax.ShapeDtypeStru...  18.4 us
    all_to_all x1, starting transfers between devices, on_device(): image = lax.all_to_all(copies, 'sub', 0, 0, tiled=True).reshape(NZ, WIN, NY)  9.49 us
    unnamed x24, local copies, waits for them, and re-layouts  7.26 us
    all_to_all x1, waiting for transfers between devices, on_device(): image = lax.all_to_all(copies, 'sub', 0, 0, tiled=True).reshape(NZ, WIN, NY)  6.32 us
    pallas_call x1, Pallas kernels, moving_planes(): pl.pallas_call(moving_kernel, out_shape=jax.ShapeDtypeStruct((4, PAGES, O...  6.12 us
  transfers between devices with their start and end apart: 23, of which 13 were waited for; matrix products, arithmetic and copies ran while one was open for 0% of the time, Pallas kernels for 5%

profile of v2, /device:TPU:0, one launch (start us, length us, event | category | flops | bytes accessed | tf_op | source)
XLA Modules:
  0.0 159.0 jit_solution(3774926407061981697)
XLA Ops:
  0.6 0.0 copy-start
  0.7 0.9 copy-done
  1.5 1.3 broadcast_in_dim.8
  2.8 3.4 %dynamic-slice_bitcast_fusion = (bf16[96,56,128]{2,1,0:T(8,128)(2,1)}, bf16[96,56,128]{2,1,0:T(8,128)(2,1)S(1)}) fusion(bf16[1,96,96,128]{3,2,1,0:T(8,128)(2,1)} %param.3, s32[]{:T(128)S(6)} %select_n.43, s32[]{:T(128)S(6)} %select_n.42), kind=kLoop, calls=%fused_computation | loop fusion | bytes 5505032 | tf_op jit(solution)/shard_map/dynamic_slice | solution.py:449
  6.1 0.0 collective-permute-start
  6.2 9.5 %all-to-all-start = ((bf16[32,3,56,128]{3,2,1,0:T(8,128)(2,1)}), bf16[32,3,56,128]{3,2,1,0:T(8,128)(2,1)}, u32[]{:S(2)}, u32[]{:S(2)}) async-start(bf16[32,3,56,128]{3,2,1,0:T(8,128)(2,1)} %broadcast_in_dim.8), calls=%async_computation | async-start | bytes 2752512 | tf_op jit(solution)/shard_map/all_to_all | solution.py:446
  15.7 0.1 stack.23.idx
  15.8 0.0 collective-permute-done.jb_ref
  15.8 1.6 %pair_sum.1 = (f32[8,3,48,128]{3,2,1,0:T(8,128)S(1)}, f32[8,3,48,128]{3,2,1,0:T(8,128)S(1)}, f32[8,3,48,128]{3,2,1,0:T(8,128)S(1)}, f32[8,3,48,128]{3,2,1,0:T(8,128)S(1)}) custom-call(s32[5]{0:T(128)S(1)} %stack.23.idx, bf16[96,56,128]{2,1,0:T(8,128)(2,1)S(1)} %get-tuple-element.50.ja_ref, bf16[96,56,128]{2,1,0:T(8,128)(2,1)S(1)} %collective-permute-done.jb_ref), custom_call_target="tpu_custom_call" | custom-call | flops 1000000 | bytes 6000000 | tf_op jit(solution)/shard_map/pair_sum/pallas_call | solution.py:103
  17.4 0.8 copy-done.1
  18.2 0.8 copy-done.3
  19.0 0.8 copy-done.5
  19.9 6.1 %moving_planes.1.jplane = f32[4,104,48,128]{3,2,1,0:T(8,128)S(1)} custom-call(s32[5]{0:T(128)S(1)} %stack.23.idx, bf16[96,56,128]{2,1,0:T(8,128)(2,1)S(1)} %get-tuple-element.50.ja_ref, bf16[96,56,128]{2,1,0:T(8,128)(2,1)S(1)} %collective-permute-done.jb_ref), custom_call_target="tpu_custom_call" | custom-call | flops 4000000000 | bytes 13000000 | tf_op jit(solution)/shard_map/moving_planes/pallas_call | solution.py:206
  26.0 3.9 %copy-done.7 = f32[4,104,48,128]{3,2,1,0:T(8,128)} copy-done((f32[4,104,48,128]{3,2,1,0:T(8,128)}, f32[4,104,48,128]{3,2,1,0:T(8,128)S(1)}, u32[]{:S(2)}) %copy-start.7) | copy-done | bytes 10223640
  29.9 6.3 %all-to-all-done = bf16[32,3,56,128]{3,2,1,0:T(8,128)(2,1)} async-done(((bf16[32,3,56,128]{3,2,1,0:T(8,128)(2,1)}), bf16[32,3,56,128]{3,2,1,0:T(8,128)(2,1)}, u32[]{:S(2)}, u32[]{:S(2)}) %all-to-all-start) | async-done | bytes 1376288 | tf_op jit(solution)/shard_map/all_to_all | solution.py:446
  36.2 18.4 %factors.1 = (f32[8,3,48,128]{3,2,1,0:T(8,128)S(1)}, f32[8,3,48,128]{3,2,1,0:T(8,128)S(1)}, f32[8,3,48,128]{3,2,1,0:T(8,128)S(1)}, f32[8,3,48,128]{3,2,1,0:T(8,1...) custom-call(s32[5]{0:T(128)S(1)} %stack.23.idx, bf16[96,56,128]{2,1,0:T(8,128)(2,1)} %bitcast.5.i_ref, ...), custom_call_target="tpu_custom_call" | custom-call | flops 4000000000 | bytes 18000000 | tf_op jit(solution)/shard_map/factors/pallas_call | solution.py:307
  54.6 1.0 collective-permute-start.1
  55.7 2.2 %collective-permute-start.2 = (f32[8,3,48,128]{3,2,1,0:T(8,128)S(1)}, f32[8,3,48,128]{3,2,1,0:T(8,128)S(1)}, u32[]{:S(2)}, u32[]{:S(2)}) collective-permute-start(f32[8,3,48,128]{3,2,1,0:T(8,128)S(1)} %get-tuple-element.36), channel_id=1, source_target_pairs={{0,2},{1,3},{2,0},{3,1},{4,6},{5,7},{6,4},{7,5},{8,10},{9,11},{10,... | collective-permute-start | bytes 1769480 | tf_op jit(solution)/shard_map/ppermute | solution.py:74
  57.8 1.8 %collective-permute-start.3 = (f32[8,3,48,128]{3,2,1,0:T(8,128)S(1)}, f32[8,3,48,128]{3,2,1,0:T(8,128)S(1)}, u32[]{:S(2)}, u32[]{:S(2)}) collective-permute-start(f32[8,3,48,128]{3,2,1,0:T(8,128)S(1)} %get-tuple-element.37), channel_id=1, source_target_pairs={{0,3},{1,0},{2,1},{3,2},{4,7},{5,4},{6,5},{7,6},{8,11},{9,8},{10,9... | collective-permute-start | bytes 1769480 | tf_op jit(solution)/shard_map/ppermute | solution.py:74
  59.7 0.2 collective-permute-start.7
  59.9 1.4 collective-permute-start.8
  61.2 4.6 %collective-permute-done.1 = f32[8,3,48,128]{3,2,1,0:T(8,128)S(1)} collective-permute-done((f32[8,3,48,128]{3,2,1,0:T(8,128)S(1)}, f32[8,3,48,128]{3,2,1,0:T(8,128)S(1)}, u32[]{:S(2)}, u32[]{:S(2)}) %collective-permute-start.1) | collective-permute-done | bytes 589856 | tf_op jit(solution)/shard_map/ppermute | solution.py:74
  65.8 0.5 collective-permute-start.9
  66.3 5.9 %collective-permute-done.2 = f32[8,3,48,128]{3,2,1,0:T(8,128)S(1)} collective-permute-done((f32[8,3,48,128]{3,2,1,0:T(8,128)S(1)}, f32[8,3,48,128]{3,2,1,0:T(8,128)S(1)}, u32[]{:S(2)}, u32[]{:S(2)}) %collective-permute-start.2) | collective-permute-done | bytes 589856 | tf_op jit(solution)/shard_map/ppermute | solution.py:74
  72.1 0.9 collective-permute-done.3
  73.0 0.2 add_add_fusion.1
  73.2 1.4 collective-permute-start.4
  74.6 1.9 %collective-permute-start.6 = (f32[2,3,48,128]{3,2,1,0:T(8,128)S(1)}, f32[2,3,48,128]{3,2,1,0:T(8,128)S(1)}, u32[]{:S(2)}, u32[]{:S(2)}) collective-permute-start(f32[2,3,48,128]{3,2,1,0:T(8,128)S(1)} %get-tuple-element.52), channel_id=1, source_target_pairs={{0,12},{1,13},{2,14},{3,15},{4,0},{5,1},{6,2},{7,3},{8,4},{9,5},{1... | collective-permute-start | bytes 442376 | tf_op jit(solution)/shard_map/ppermute | solution.py:74
  76.5 3.5 %collective-permute-done.7 = f32[8,3,48,128]{3,2,1,0:T(8,128)S(1)} collective-permute-done((f32[8,3,48,128]{3,2,1,0:T(8,128)S(1)}, f32[8,3,48,128]{3,2,1,0:T(8,128)S(1)}, u32[]{:S(2)}, u32[]{:S(2)}) %collective-permute-start.7) | collective-permute-done | bytes 589856 | tf_op jit(solution)/shard_map/ppermute | solution.py:74
  80.0 10.2 %collective-permute-start.5 = (f32[2,3,48,128]{3,2,1,0:T(8,128)S(1)}, f32[2,3,48,128]{3,2,1,0:T(8,128)S(1)}, u32[]{:S(2)}, u32[]{:S(2)}) collective-permute-start(f32[2,3,48,128]{3,2,1,0:T(8,128)S(1)} %get-tuple-element.53), channel_id=1, source_target_pairs={{0,8},{1,9},{2,10},{3,11},{4,12},{5,13},{6,14},{7,15},{8,0},{9,1},... | collective-permute-start | bytes 442376 | tf_op jit(solution)/shard_map/ppermute | solution.py:74
  90.2 0.0 collective-permute-done.8
  90.2 0.0 collective-permute-done.9
  90.2 0.2 add_add_fusion
  90.4 0.7 collective-permute-start.10
  91.2 2.6 %collective-permute-start.12 = (f32[2,3,48,128]{3,2,1,0:T(8,128)S(1)}, f32[2,3,48,128]{3,2,1,0:T(8,128)S(1)}, u32[]{:S(2)}, u32[]{:S(2)}) collective-permute-start(f32[2,3,48,128]{3,2,1,0:T(8,128)S(1)} %get-tuple-element.55), channel_id=1, source_target_pairs={{0,12},{1,13},{2,14},{3,15},{4,0},{5,1},{6,2},{7,3},{8,4},{9,5},{1... | collective-permute-start | bytes 442376 | tf_op jit(solution)/shard_map/ppermute | solution.py:74
  93.8 0.0 collective-permute-done.4
  93.8 0.2 collective-permute-start.11
  94.0 0.0 collective-permute-done.6
  94.0 0.0 collective-permute-done.5
  94.0 2.9 %collective-permute-done.10 = f32[2,3,48,128]{3,2,1,0:T(8,128)S(1)} collective-permute-done((f32[2,3,48,128]{3,2,1,0:T(8,128)S(1)}, f32[2,3,48,128]{3,2,1,0:T(8,128)S(1)}, u32[]{:S(2)}, u32[]{:S(2)}) %collective-permute-start.10) | collective-permute-done | bytes 147488 | tf_op jit(solution)/shard_map/ppermute | solution.py:74
  96.9 1.2 collective-permute-done.12
  98.0 2.4 %collective-permute-done.11 = f32[2,3,48,128]{3,2,1,0:T(8,128)S(1)} collective-permute-done((f32[2,3,48,128]{3,2,1,0:T(8,128)S(1)}, f32[2,3,48,128]{3,2,1,0:T(8,128)S(1)}, u32[]{:S(2)}, u32[]{:S(2)}) %collective-permute-start.11) | collective-permute-done | bytes 147488 | tf_op jit(solution)/shard_map/ppermute | solution.py:74
  100.5 2.8 %collective-permute-start.13 = (f32[296,128]{1,0:T(8,128)S(1)}, f32[296,128]{1,0:T(8,128)S(1)}, u32[]{:S(2)}, u32[]{:S(2)}) collective-permute-start(f32[296,128]{1,0:T(8,128)S(1)} %get-tuple-element.57), channel_id=1, source_target_pairs={{0,64},{1,65},{2,66},{3,67},{4,68},{5,69},{6,70},{7,71},{8,72},{9,... | collective-permute-start | bytes 454664 | tf_op jit(solution)/shard_map/ppermute | solution.py:74
  103.3 1.0 collective-permute-start.15
  104.3 1.0 collective-permute-start.14
  105.4 1.9 %collective-permute-done.13 = f32[296,128]{1,0:T(8,128)S(1)} collective-permute-done((f32[296,128]{1,0:T(8,128)S(1)}, f32[296,128]{1,0:T(8,128)S(1)}, u32[]{:S(2)}, u32[]{:S(2)}) %collective-permute-start.13) | collective-permute-done | bytes 151584 | tf_op jit(solution)/shard_map/ppermute | solution.py:74
  107.3 1.3 collective-permute-done.15
  108.6 2.2 %collective-permute-done.14 = f32[296,128]{1,0:T(8,128)S(1)} collective-permute-done((f32[296,128]{1,0:T(8,128)S(1)}, f32[296,128]{1,0:T(8,128)S(1)}, u32[]{:S(2)}, u32[]{:S(2)}) %collective-permute-start.14) | collective-permute-done | bytes 151584 | tf_op jit(solution)/shard_map/ppermute | solution.py:74
  110.8 1.3 collective-permute-start.19
  112.1 6.1 %collective-permute-start.16 = (f32[96,128]{1,0:T(8,128)S(1)}, f32[96,128]{1,0:T(8,128)S(1)}, u32[]{:S(2)}, u32[]{:S(2)}) collective-permute-start(f32[96,128]{1,0:T(8,128)S(1)} %get-tuple-element.60), channel_id=1, source_target_pairs={{0,2},{1,3},{2,4},{3,5},{4,6},{5,7},{6,8},{7,9},{8,10},{9,11},{10,... | collective-permute-start | bytes 147464 | tf_op jit(solution)/shard_map/ppermute | solution.py:74
  118.2 1.3 collective-permute-start.18
  119.5 4.6 %collective-permute-start.17 = (f32[192,128]{1,0:T(8,128)S(1)}, f32[192,128]{1,0:T(8,128)S(1)}, u32[]{:S(2)}, u32[]{:S(2)}) collective-permute-start(f32[192,128]{1,0:T(8,128)S(1)} %pad_maximum_fusion.1), channel_id=1, source_target_pairs={{0,1},{1,2},{2,3},{3,4},{4,5},{5,6},{6,7},{7,8},{8,9},{9,10},{10,1... | collective-permute-start | bytes 294920 | tf_op jit(solution)/shard_map/ppermute | solution.py:74
  124.1 0.0 collective-permute-done.16
  124.1 2.2 %collective-permute-done.17 = f32[192,128]{1,0:T(8,128)S(1)} collective-permute-done((f32[192,128]{1,0:T(8,128)S(1)}, f32[192,128]{1,0:T(8,128)S(1)}, u32[]{:S(2)}, u32[]{:S(2)}) %collective-permute-start.17) | collective-permute-done | bytes 98336 | tf_op jit(solution)/shard_map/ppermute | solution.py:74
  126.3 0.0 collective-permute-done.19
  126.4 0.1 collective-permute-start.20
  126.5 0.8 collective-permute-start.21
  127.3 1.3 collective-permute-done.21
  128.6 3.8 %smooth_slab.1 = (f32[3,3,96,128]{3,2,1,0:T(8,128)S(1)}, f32[3,96,128]{2,1,0:T(8,128)S(1)}, f32[3,96,128]{2,1,0:T(8,128)S(1)}, f32[1,128]{1,0:T(1,128)S(1)}) custom-call(s32[5]{0:T(128)S(1)} %stack.23.idx, f32[872,128]{1,0:T(8,128)S(1)} %constant_dynamic-update-slice_fusion.own_ref, f32[872,128]{1,0:T(8,128)S(1)} %collective-permute-done.20.other_ref, ...), custom_call_target="tpu_custom_call" | custom-call | flops 100000000 | bytes 3000000 | tf_op jit(solution)/shard_map/smooth_slab/pallas_call | solution.py:399
  132.3 21.4 %all_to_all.10 = f32[32,1,128]{2,1,0:T(1,128)S(1)} all-to-all(f32[32,1,128]{2,1,0:T(1,128)S(1)} %broadcast_in_dim.11), channel_id=1, replica_groups=mesh['grp'=4,'sub'=32] {'sub'}, dimensions={0} | all-to-all | bytes 32768 | tf_op jit(solution)/shard_map/all_to_all | solution.py:491
  153.7 0.1 slice_reduce_fusion
  153.7 0.6 fusion.7
  156.4 0.8 broadcast_multiply_fusion
  157.2 0.7 subtract_divide_fusion
  (38 shorter events, 0.4 us)
Async XLA Ops:
  0.6 0.9 copy-start
  6.1 9.6 %collective-permute-start = (bf16[96,56,128]{2,1,0:T(8,128)(2,1)}, bf16[96,56,128]{2,1,0:T(8,128)(2,1)S(1)}, u32[]{:S(2)}, u32[]{:S(2)}) collective-permute-start(bf16[96,56,128]{2,1,0:T(8,128)(2,1)} %get-tuple-element.49), channel_id=1, source_target_pairs={{0,32},{1,33},{2,34},{3,35},{4,36},{5,37},{6,38},{7,39},{8,40},{9,... | collective-permute-start | bytes 4128776 | tf_op jit(solution)/shard_map/ppermute | solution.py:74
  6.2 30.1 %all-to-all-start = ((bf16[32,3,56,128]{3,2,1,0:T(8,128)(2,1)}), bf16[32,3,56,128]{3,2,1,0:T(8,128)(2,1)}, u32[]{:S(2)}, u32[]{:S(2)}) async-start(bf16[32,3,56,128]{3,2,1,0:T(8,128)(2,1)} %broadcast_in_dim.8), calls=%async_computation | async-start | bytes 2752512 | tf_op jit(solution)/shard_map/all_to_all | solution.py:446
  17.4 0.8 copy-start.1
  18.2 0.8 copy-start.3
  19.0 0.8 copy-start.5
  26.0 3.9 %copy-start.7 = (f32[4,104,48,128]{3,2,1,0:T(8,128)}, f32[4,104,48,128]{3,2,1,0:T(8,128)S(1)}, u32[]{:S(2)}) copy-start(f32[4,104,48,128]{3,2,1,0:T(8,128)S(1)} %moving_planes.1.jplane) | copy-start | bytes 30670852
  36.2 23.4 %copy-start.6 = (f32[8,3,48,128]{3,2,1,0:T(8,128)S(1)}, f32[8,3,48,128]{3,2,1,0:T(8,128)}, u32[]{:S(2)}) copy-start(f32[8,3,48,128]{3,2,1,0:T(8,128)} %copy-done.5) | copy-start | bytes 1769476
  36.2 23.6 %copy-start.4 = (f32[8,3,48,128]{3,2,1,0:T(8,128)S(1)}, f32[8,3,48,128]{3,2,1,0:T(8,128)}, u32[]{:S(2)}) copy-start(f32[8,3,48,128]{3,2,1,0:T(8,128)} %copy-done.3) | copy-start | bytes 1769476
  36.2 29.6 %copy-start.2 = (f32[8,3,48,128]{3,2,1,0:T(8,128)S(1)}, f32[8,3,48,128]{3,2,1,0:T(8,128)}, u32[]{:S(2)}) copy-start(f32[8,3,48,128]{3,2,1,0:T(8,128)} %copy-done.1) | copy-start | bytes 1769476
  54.6 11.2 %collective-permute-start.1 = (f32[8,3,48,128]{3,2,1,0:T(8,128)S(1)}, f32[8,3,48,128]{3,2,1,0:T(8,128)S(1)}, u32[]{:S(2)}, u32[]{:S(2)}) collective-permute-start(f32[8,3,48,128]{3,2,1,0:T(8,128)S(1)} %get-tuple-element.35), channel_id=1, source_target_pairs={{0,1},{1,2},{2,3},{3,0},{4,5},{5,6},{6,7},{7,4},{8,9},{9,10},{10,1... | collective-permute-start | bytes 1769480 | tf_op jit(solution)/shard_map/ppermute | solution.py:74
  55.7 16.5 %collective-permute-start.2 = (f32[8,3,48,128]{3,2,1,0:T(8,128)S(1)}, f32[8,3,48,128]{3,2,1,0:T(8,128)S(1)}, u32[]{:S(2)}, u32[]{:S(2)}) collective-permute-start(f32[8,3,48,128]{3,2,1,0:T(8,128)S(1)} %get-tuple-element.36), channel_id=1, source_target_pairs={{0,2},{1,3},{2,0},{3,1},{4,6},{5,7},{6,4},{7,5},{8,10},{9,11},{10,... | collective-permute-start | bytes 1769480 | tf_op jit(solution)/shard_map/ppermute | solution.py:74
  57.8 15.2 %collective-permute-start.3 = (f32[8,3,48,128]{3,2,1,0:T(8,128)S(1)}, f32[8,3,48,128]{3,2,1,0:T(8,128)S(1)}, u32[]{:S(2)}, u32[]{:S(2)}) collective-permute-start(f32[8,3,48,128]{3,2,1,0:T(8,128)S(1)} %get-tuple-element.37), channel_id=1, source_target_pairs={{0,3},{1,0},{2,1},{3,2},{4,7},{5,4},{6,5},{7,6},{8,11},{9,8},{10,9... | collective-permute-start | bytes 1769480 | tf_op jit(solution)/shard_map/ppermute | solution.py:74
  59.7 20.3 %collective-permute-start.7 = (f32[8,3,48,128]{3,2,1,0:T(8,128)S(1)}, f32[8,3,48,128]{3,2,1,0:T(8,128)S(1)}, u32[]{:S(2)}, u32[]{:S(2)}) collective-permute-start(f32[8,3,48,128]{3,2,1,0:T(8,128)S(1)} %copy-done.6), channel_id=1, source_target_pairs={{0,1},{1,2},{2,3},{3,0},{4,5},{5,6},{6,7},{7,4},{8,9},{9,10},{10,1... | collective-permute-start | bytes 1769480 | tf_op jit(solution)/shard_map/ppermute | solution.py:74
  59.9 30.4 %collective-permute-start.8 = (f32[8,3,48,128]{3,2,1,0:T(8,128)S(1)}, f32[8,3,48,128]{3,2,1,0:T(8,128)S(1)}, u32[]{:S(2)}, u32[]{:S(2)}) collective-permute-start(f32[8,3,48,128]{3,2,1,0:T(8,128)S(1)} %copy-done.4), channel_id=1, source_target_pairs={{0,2},{1,3},{2,0},{3,1},{4,6},{5,7},{6,4},{7,5},{8,10},{9,11},{10,... | collective-permute-start | bytes 1769480 | tf_op jit(solution)/shard_map/ppermute | solution.py:74
  65.8 24.4 %collective-permute-start.9 = (f32[8,3,48,128]{3,2,1,0:T(8,128)S(1)}, f32[8,3,48,128]{3,2,1,0:T(8,128)S(1)}, u32[]{:S(2)}, u32[]{:S(2)}) collective-permute-start(f32[8,3,48,128]{3,2,1,0:T(8,128)S(1)} %copy-done.2), channel_id=1, source_target_pairs={{0,3},{1,0},{2,1},{3,2},{4,7},{5,4},{6,5},{7,6},{8,11},{9,8},{10,9... | collective-permute-start | bytes 1769480 | tf_op jit(solution)/shard_map/ppermute | solution.py:74
  73.2 20.5 %collective-permute-start.4 = (f32[2,3,48,128]{3,2,1,0:T(8,128)S(1)}, f32[2,3,48,128]{3,2,1,0:T(8,128)S(1)}, u32[]{:S(2)}, u32[]{:S(2)}) collective-permute-start(f32[2,3,48,128]{3,2,1,0:T(8,128)S(1)} %get-tuple-element.51), channel_id=1, source_target_pairs={{0,4},{1,5},{2,6},{3,7},{4,8},{5,9},{6,10},{7,11},{8,12},{9,13},{1... | collective-permute-start | bytes 442376 | tf_op jit(solution)/shard_map/ppermute | solution.py:74
  74.6 19.4 %collective-permute-start.6 = (f32[2,3,48,128]{3,2,1,0:T(8,128)S(1)}, f32[2,3,48,128]{3,2,1,0:T(8,128)S(1)}, u32[]{:S(2)}, u32[]{:S(2)}) collective-permute-start(f32[2,3,48,128]{3,2,1,0:T(8,128)S(1)} %get-tuple-element.52), channel_id=1, source_target_pairs={{0,12},{1,13},{2,14},{3,15},{4,0},{5,1},{6,2},{7,3},{8,4},{9,5},{1... | collective-permute-start | bytes 442376 | tf_op jit(solution)/shard_map/ppermute | solution.py:74
  80.0 13.9 %collective-permute-start.5 = (f32[2,3,48,128]{3,2,1,0:T(8,128)S(1)}, f32[2,3,48,128]{3,2,1,0:T(8,128)S(1)}, u32[]{:S(2)}, u32[]{:S(2)}) collective-permute-start(f32[2,3,48,128]{3,2,1,0:T(8,128)S(1)} %get-tuple-element.53), channel_id=1, source_target_pairs={{0,8},{1,9},{2,10},{3,11},{4,12},{5,13},{6,14},{7,15},{8,0},{9,1},... | collective-permute-start | bytes 442376 | tf_op jit(solution)/shard_map/ppermute | solution.py:74
  90.4 6.4 %collective-permute-start.10 = (f32[2,3,48,128]{3,2,1,0:T(8,128)S(1)}, f32[2,3,48,128]{3,2,1,0:T(8,128)S(1)}, u32[]{:S(2)}, u32[]{:S(2)}) collective-permute-start(f32[2,3,48,128]{3,2,1,0:T(8,128)S(1)} %get-tuple-element.54), channel_id=1, source_target_pairs={{0,4},{1,5},{2,6},{3,7},{4,8},{5,9},{6,10},{7,11},{8,12},{9,13},{1... | collective-permute-start | bytes 442376 | tf_op jit(solution)/shard_map/ppermute | solution.py:74
  91.2 6.8 %collective-permute-start.12 = (f32[2,3,48,128]{3,2,1,0:T(8,128)S(1)}, f32[2,3,48,128]{3,2,1,0:T(8,128)S(1)}, u32[]{:S(2)}, u32[]{:S(2)}) collective-permute-start(f32[2,3,48,128]{3,2,1,0:T(8,128)S(1)} %get-tuple-element.55), channel_id=1, source_target_pairs={{0,12},{1,13},{2,14},{3,15},{4,0},{5,1},{6,2},{7,3},{8,4},{9,5},{1... | collective-permute-start | bytes 442376 | tf_op jit(solution)/shard_map/ppermute | solution.py:74
  93.8 6.6 %collective-permute-start.11 = (f32[2,3,48,128]{3,2,1,0:T(8,128)S(1)}, f32[2,3,48,128]{3,2,1,0:T(8,128)S(1)}, u32[]{:S(2)}, u32[]{:S(2)}) collective-permute-start(f32[2,3,48,128]{3,2,1,0:T(8,128)S(1)} %get-tuple-element.56), channel_id=1, source_target_pairs={{0,8},{1,9},{2,10},{3,11},{4,12},{5,13},{6,14},{7,15},{8,0},{9,1},... | collective-permute-start | bytes 442376 | tf_op jit(solution)/shard_map/ppermute | solution.py:74
  100.5 6.8 %collective-permute-start.13 = (f32[296,128]{1,0:T(8,128)S(1)}, f32[296,128]{1,0:T(8,128)S(1)}, u32[]{:S(2)}, u32[]{:S(2)}) collective-permute-start(f32[296,128]{1,0:T(8,128)S(1)} %get-tuple-element.57), channel_id=1, source_target_pairs={{0,64},{1,65},{2,66},{3,67},{4,68},{5,69},{6,70},{7,71},{8,72},{9,... | collective-permute-start | bytes 454664 | tf_op jit(solution)/shard_map/ppermute | solution.py:74
  103.3 5.2 %collective-permute-start.15 = (f32[296,128]{1,0:T(8,128)S(1)}, f32[296,128]{1,0:T(8,128)S(1)}, u32[]{:S(2)}, u32[]{:S(2)}) collective-permute-start(f32[296,128]{1,0:T(8,128)S(1)} %get-tuple-element.58), channel_id=1, source_target_pairs={{0,80},{1,81},{2,82},{3,83},{4,84},{5,85},{6,86},{7,87},{8,88},{9,... | collective-permute-start | bytes 454664 | tf_op jit(solution)/shard_map/ppermute | solution.py:74
  104.3 6.4 %collective-permute-start.14 = (f32[296,128]{1,0:T(8,128)S(1)}, f32[296,128]{1,0:T(8,128)S(1)}, u32[]{:S(2)}, u32[]{:S(2)}) collective-permute-start(f32[296,128]{1,0:T(8,128)S(1)} %get-tuple-element.58), channel_id=1, source_target_pairs={{0,16},{1,17},{2,18},{3,19},{4,20},{5,21},{6,22},{7,23},{8,24},{9,... | collective-permute-start | bytes 454664 | tf_op jit(solution)/shard_map/ppermute | solution.py:74
  110.8 15.5 %collective-permute-start.19 = (f32[96,128]{1,0:T(8,128)S(1)}, f32[96,128]{1,0:T(8,128)S(1)}, u32[]{:S(2)}, u32[]{:S(2)}) collective-permute-start(f32[96,128]{1,0:T(8,128)S(1)} %get-tuple-element.59), channel_id=1, source_target_pairs={{2,0},{3,1},{4,2},{5,3},{6,4},{7,5},{8,6},{9,7},{10,8},{11,9},{12,... | collective-permute-start | bytes 147464 | tf_op jit(solution)/shard_map/ppermute | solution.py:74
  112.1 11.9 %collective-permute-start.16 = (f32[96,128]{1,0:T(8,128)S(1)}, f32[96,128]{1,0:T(8,128)S(1)}, u32[]{:S(2)}, u32[]{:S(2)}) collective-permute-start(f32[96,128]{1,0:T(8,128)S(1)} %get-tuple-element.60), channel_id=1, source_target_pairs={{0,2},{1,3},{2,4},{3,5},{4,6},{5,7},{6,8},{7,9},{8,10},{9,11},{10,... | collective-permute-start | bytes 147464 | tf_op jit(solution)/shard_map/ppermute | solution.py:74
  118.2 8.1 %collective-permute-start.18 = (f32[192,128]{1,0:T(8,128)S(1)}, f32[192,128]{1,0:T(8,128)S(1)}, u32[]{:S(2)}, u32[]{:S(2)}) collective-permute-start(f32[192,128]{1,0:T(8,128)S(1)} %concatenate.16), channel_id=1, source_target_pairs={{1,0},{2,1},{3,2},{4,3},{5,4},{6,5},{7,6},{8,7},{9,8},{10,9},{11,1... | collective-permute-start | bytes 294920 | tf_op jit(solution)/shard_map/ppermute | solution.py:74
  119.5 6.8 %collective-permute-start.17 = (f32[192,128]{1,0:T(8,128)S(1)}, f32[192,128]{1,0:T(8,128)S(1)}, u32[]{:S(2)}, u32[]{:S(2)}) collective-permute-start(f32[192,128]{1,0:T(8,128)S(1)} %pad_maximum_fusion.1), channel_id=1, source_target_pairs={{0,1},{1,2},{2,3},{3,4},{4,5},{5,6},{6,7},{7,8},{8,9},{9,10},{10,1... | collective-permute-start | bytes 294920 | tf_op jit(solution)/shard_map/ppermute | solution.py:74
  126.4 2.2 %collective-permute-start.20 = (f32[872,128]{1,0:T(8,128)S(1)}, f32[872,128]{1,0:T(8,128)S(1)}, u32[]{:S(2)}, u32[]{:S(2)}) collective-permute-start(f32[872,128]{1,0:T(8,128)S(1)} %constant_dynamic-update-slice_fusion.own_ref), channel_id=1, source_target_pairs={{0,32},{1,33},{2,34},{3,35},{4,36},{5,37},{6,38},{7,39},{8,40},{9,... | collective-permute-start | bytes 1339400 | tf_op jit(solution)/shard_map/ppermute | solution.py:74
  126.5 2.0 %collective-permute-start.21 = (bf16[15,48,128]{2,1,0:T(8,128)(2,1)S(1)}, bf16[15,48,128]{2,1,0:T(8,128)(2,1)S(1)}, u32[]{:S(2)}, u32[]{:S(2)}) collective-permute-start(bf16[15,48,128]{2,1,0:T(8,128)(2,1)S(1)} %convert_element_type.6), channel_id=1, source_target_pairs={{0,32},{1,33},{2,34},{3,35},{4,36},{5,37},{6,38},{7,39},{8,40},{9,... | collective-permute-start | bytes 552968 | tf_op jit(solution)/shard_map/ppermute | solution.py:74

commit v3 on v2

--- a/solution.py
+++ b/solution.py
@@ -6,6 +6,7 @@
 from jax.experimental import pallas as pl
 from jax.experimental.pallas import tpu as pltpu
 from jax.sharding import PartitionSpec as P
+
 
 RADIUS = 4
 REACH = 5
@@ -61,12 +62,13 @@
     return pairs(move)
 
 
+TWIN_PAIRS = pairs(lambda xh, co, xl, y, z: (1 - xh, co, xl, y, z))
 CORE_PAIRS = pairs(lambda xh, co, xl, y, z: (xh, 1 - co, xl, y, z))
 
 
 def slab_shift(k):
     return [
-        (g * 32 + s, g * 32 + s + k) for g in range(4) for s in range(32) if 0 <= s + k < 32
+        (g * 32 + s, g * 32 + (s + (k if g < 2 else -k)) % 32) for g in range(4) for s in range(32)
     ]
 
 
@@ -112,7 +114,6 @@
     )(idx, ja, jb)
 
 
-CHUNK = 4
 TOP = 16
 PAGES = NZ + 8
 
@@ -133,7 +134,7 @@
 
 def plane_sums(makers, shift, even, odd, three, plane):
     band1, band2 = bands()
-    volumes = plane.shape[0]
+    volumes, chunk = three.shape[:2]
     even[...] = jnp.zeros(even.shape, F32)
     odd[...] = jnp.zeros(odd.shape, F32)
     for v in range(volumes):
@@ -142,17 +143,17 @@
 
     def along_y(thunk, v, line):
         sums = thunk(band1, band2)
-        for j in range(CHUNK):
+        for j in range(chunk):
             line[v, j, pl.ds(TOP, WIN), :] = sums[j * WIN : (j + 1) * WIN]
 
     def along_x(v, line, base):
-        for j in range(CHUNK):
+        for j in range(chunk):
             three[v, j] = (
                 line[v, j, pl.ds(TOP - 9 + shift, 64), :]
                 + line[v, j, pl.ds(TOP - 8 + shift, 64), :]
                 + line[v, j, pl.ds(TOP - 7 + shift, 64), :]
             )
-        for j in range(CHUNK):
+        for j in range(chunk):
             plane[v, base + j + 4] = (
                 three[v, j, pl.ds(5, OWN), :]
                 + three[v, j, pl.ds(8, OWN), :]
@@ -160,27 +161,31 @@
             )
 
     def both(i, line, other):
-        thunks = makers(i * CHUNK)
+        thunks = makers(i * chunk)
         for v in range(volumes):
             along_y(thunks[v], v, line)
-            along_x(v, other, (i - 1) * CHUNK)
+            along_x(v, other, (i - 1) * chunk)
 
     def step(n, carry):
         both(2 * n, even, odd)
         both(2 * n + 1, odd, even)
         return carry
 
-    lax.fori_loop(0, NZ // CHUNK // 2, step, 0)
+    lax.fori_loop(0, NZ // chunk // 2, step, 0)
     for v in range(volumes):
-        along_x(v, odd, NZ - CHUNK)
+        along_x(v, odd, NZ - chunk)
+
+
+MOVING_CHUNK = 4
+FACTOR_CHUNK = 2
 
 
 def dot(lhs, rhs):
     return jnp.dot(lhs, rhs, preferred_element_type=F32)
 
 
-def load(ref, base):
-    return ref[pl.ds(base, CHUNK)].reshape(CHUNK * WIN, NY)
+def load(ref, base, chunk):
+    return ref[pl.ds(base, chunk)].reshape(chunk * WIN, NY)
 
 
 def moving_kernel(idx, ja_ref, jb_ref, plane, even, odd, three):
@@ -191,10 +196,10 @@
         for ref in (ja_ref, jb_ref):
 
             def square(b1, b2, ref=ref):
-                f = load(ref, base).astype(F32)
+                f = load(ref, base, MOVING_CHUNK).astype(F32)
                 return dot(split(f * f), b2)
 
-            out.append(lambda b1, b2, ref=ref: dot(load(ref, base), b1))
+            out.append(lambda b1, b2, ref=ref: dot(load(ref, base, MOVING_CHUNK), b1))
             out.append(square)
         return out
 
@@ -209,9 +214,9 @@
         in_specs=[pl.BlockSpec(memory_space=pltpu.SMEM), vm, vm],
         out_specs=vm,
         scratch_shapes=[
-            pltpu.VMEM((4, CHUNK, 88, NY), F32),
-            pltpu.VMEM((4, CHUNK, 88, NY), F32),
-            pltpu.VMEM((4, CHUNK, 64, NY), F32),
+            pltpu.VMEM((4, MOVING_CHUNK, 88, NY), F32),
+            pltpu.VMEM((4, MOVING_CHUNK, 88, NY), F32),
+            pltpu.VMEM((4, MOVING_CHUNK, 64, NY), F32),
         ],
         compiler_params=pltpu.CompilerParams(vmem_limit_bytes=24 << 20),
         cost_estimate=pl.CostEstimate(flops=4 * 10**9, bytes_accessed=13 * 10**6, transcendentals=0),
@@ -220,16 +225,18 @@
 
 
 def factor_kernel(
-    idx, i_ref, ja_ref, jb_ref, jplane, o0, o1, o2, o3, cc_ref, iext_ref,
-    raw, even, odd, three, iplane,
+    idx, i_ref, ja_ref, jb_ref, jplane_ref, o0, o1, o2, o3, cc_ref, iext_ref,
+    raw, even, odd, three, iplane, jplane, sem,
 ):
     shift = pl.multiple_of(idx[0] * 8, 8)
+    fetch = pltpu.make_async_copy(jplane_ref, jplane, sem)
+    fetch.start()
 
     def makers(base):
         def wide(n, keep):
-            f = load((i_ref, ja_ref, jb_ref)[n], base).astype(F32)
+            f = load((i_ref, ja_ref, jb_ref)[n], base, FACTOR_CHUNK).astype(F32)
             if keep:
-                raw[n, pl.ds(base, CHUNK)] = f.reshape(CHUNK, WIN, NY)
+                raw[n, pl.ds(base, FACTOR_CHUNK)] = f.reshape(FACTOR_CHUNK, WIN, NY)
             return f
 
         def square(b1, b2):
@@ -237,13 +244,14 @@
             return dot(split(f * f), b2)
 
         return [
-            lambda b1, b2: dot(load(i_ref, base), b1),
+            lambda b1, b2: dot(load(i_ref, base, FACTOR_CHUNK), b1),
             square,
             lambda b1, b2: dot(split(wide(0, False) * wide(1, True)), b2),
             lambda b1, b2: dot(split(wide(0, False) * wide(2, True)), b2),
         ]
 
     plane_sums(makers, shift, even, odd, three, iplane)
+    fetch.wait()
 
     eps_b = EPSILON * COUNT**2
     eps_bc = EPSILON * COUNT**4
@@ -308,34 +316,71 @@
         factor_kernel,
         out_shape=[block] * 4
         + [jax.ShapeDtypeStruct((8, NY), F32), jax.ShapeDtypeStruct((15, OWN, NY), F32)],
-        in_specs=[pl.BlockSpec(memory_space=pltpu.SMEM), vm, vm, vm, vm],
+        in_specs=[pl.BlockSpec(memory_space=pltpu.SMEM), vm, vm, vm]
+        + [pl.BlockSpec(memory_space=pl.ANY)],
         out_specs=[vm] * 6,
         scratch_shapes=[
             pltpu.VMEM((3, NZ, WIN, NY), F32),
-            pltpu.VMEM((4, CHUNK, 88, NY), F32),
-            pltpu.VMEM((4, CHUNK, 88, NY), F32),
-            pltpu.VMEM((4, CHUNK, 64, NY), F32),
+            pltpu.VMEM((4, FACTOR_CHUNK, 88, NY), F32),
+            pltpu.VMEM((4, FACTOR_CHUNK, 88, NY), F32),
+            pltpu.VMEM((4, FACTOR_CHUNK, 64, NY), F32),
             pltpu.VMEM((4, PAGES, OWN, NY), F32),
+            pltpu.VMEM((4, PAGES, OWN, NY), F32),
+            pltpu.SemaphoreType.DMA,
         ],
-        compiler_params=pltpu.CompilerParams(vmem_limit_bytes=44 << 20),
+        compiler_params=pltpu.CompilerParams(vmem_limit_bytes=48 << 20),
         cost_estimate=pl.CostEstimate(flops=4 * 10**9, bytes_accessed=18 * 10**6, transcendentals=0),
         name="factors",
     )(idx, image, ja, jb, jplane)
 
 
-EXT = 18
 CC_ROWS = 8
-
-
-def smooth_kernel(idx, own_ref, other_ref, iown_ref, iother_ref, u_ref, adv_ref, m_ref, st_ref, ext, image, prod):
-    mine = pl.multiple_of(idx[0] * OWN, 8)
-    others = pl.multiple_of((1 - idx[0]) * OWN, 8)
-    for p in range(EXT):
-        ext[p, pl.ds(mine, OWN), :] = own_ref[pl.ds(p * OWN, OWN), :]
-        ext[p, pl.ds(others, OWN), :] = other_ref[pl.ds(p * OWN, OWN), :]
+SIDE = 6 * OWN
+CENTRE = 6 * OWN + CC_ROWS
+
+
+def smooth_kernel(
+    idx, own_ref, twin_ref, other_ref, iown_ref, iother_ref, u_ref, adv_ref, m_ref, st_ref,
+    ext, mext, image, prod,
+):
+    core, sub, xh = idx[0], idx[4], idx[5]
+    mine = pl.multiple_of(core * OWN, 8)
+    others = pl.multiple_of((1 - core) * OWN, 8)
+
+    def centre(rows, ref):
+        for j in range(3):
+            ext[5 + j, rows, :] = ref[pl.ds(j * OWN, OWN), :]
+            mext[1 + j, rows, :] = ref[pl.ds((3 + j) * OWN, OWN), :]
+
+    def sides(rows, low, high):
+        for d, (ref, at) in enumerate((low, high)):
+            for j in range(5):
+                z = sub * 3 + (j - 5 if d == 0 else j + 3)
+                inside = jnp.logical_and(z >= 0, z < NZ)
+                page = ref[pl.ds(at + j * OWN, OWN), :]
+                ext[j if d == 0 else 8 + j, rows, :] = jnp.where(inside, page, 0.0)
+            z = sub * 3 + (-1 if d == 0 else 3)
+            inside = jnp.logical_and(z >= 0, z < NZ)
+            page = ref[pl.ds(at + 5 * OWN, OWN), :]
+            mext[0 if d == 0 else 4, rows, :] = jnp.where(inside, page, 0.0)
+
+    my_rows, other_rows = pl.ds(mine, OWN), pl.ds(others, OWN)
+    centre(my_rows, own_ref)
+    centre(other_rows, other_ref)
+
+    @pl.when(xh == 0)
+    def _():
+        sides(my_rows, (own_ref, CENTRE), (twin_ref, 0))
+        sides(other_rows, (other_ref, CENTRE), (other_ref, CENTRE + SIDE))
+
+    @pl.when(xh == 1)
+    def _():
+        sides(my_rows, (twin_ref, 0), (own_ref, CENTRE))
+        sides(other_rows, (other_ref, CENTRE + SIDE), (other_ref, CENTRE))
+
     for p in range(15):
-        image[p, pl.ds(mine, OWN), :] = iown_ref[p]
-        image[p, pl.ds(others, OWN), :] = iother_ref[p]
+        image[p, my_rows, :] = iown_ref[p]
+        image[p, other_rows, :] = iother_ref[p].astype(F32)
 
     weights = [math.exp(-o * o / (2.0 * VARIANCE)) for o in range(-REACH, REACH + 1)]
     norm = sum(weights)
@@ -368,9 +413,9 @@
     image_square = jnp.zeros((NX, NY), F32)
     mean = 1.0 / DEVICES
     for j in range(3):
-        m = ext[14 + j] * mean
+        m = mext[1 + j] * mean
         sx, sy = twice_slopes(m)
-        slopes = ((ext[15 + j] - ext[13 + j]) * mean, sx, sy)
+        slopes = ((mext[2 + j] - mext[j]) * mean, sx, sy)
         image_square = image_square + m * m
         moved = None
         for d in range(3):
@@ -386,7 +431,7 @@
             moved = term if d == 0 else moved + term
         adv_ref[j] = moved * 0.5
         m_ref[j] = m
-    tail = pl.ds(EXT * OWN, CC_ROWS)
+    tail = pl.ds(6 * OWN, CC_ROWS)
     cc = jnp.sum(own_ref[tail, :] + other_ref[tail, :])
     one = lax.broadcasted_iota(jnp.int32, (1, NY), 1)
     st_ref[...] = jnp.where(
@@ -394,7 +439,7 @@
     )
 
 
-def smooth_slab(idx, own, other, iown, iother):
+def smooth_slab(idx, own, twin, other, iown, iother):
     vm = pl.BlockSpec(memory_space=pltpu.VMEM)
     return pl.pallas_call(
         smooth_kernel,
@@ -404,17 +449,46 @@
             jax.ShapeDtypeStruct((3, NX, NY), F32),
             jax.ShapeDtypeStruct((1, NY), F32),
         ],
-        in_specs=[pl.BlockSpec(memory_space=pltpu.SMEM), vm, vm, vm, vm],
+        in_specs=[pl.BlockSpec(memory_space=pltpu.SMEM), vm, vm, vm, vm, vm],
         out_specs=[vm] * 4,
         scratch_shapes=[
-            pltpu.VMEM((EXT, NX, NY), F32),
+            pltpu.VMEM((13, NX, NY), F32),
+            pltpu.VMEM((5, NX, NY), F32),
             pltpu.VMEM((15, NX, NY), F32),
             pltpu.VMEM((3, 13, NX, NY), F32),
         ],
         compiler_params=pltpu.CompilerParams(vmem_limit_bytes=24 << 20),
         cost_estimate=pl.CostEstimate(flops=10**8, bytes_accessed=3 * 10**6, transcendentals=0),
         name="smooth_slab",
-    )(idx, own, other, iown, iother)
+    )(idx, own, twin, other, iown, iother)
+
+
+def finish_kernel(rows_ref, u_ref, adv_ref, m_ref, v_ref, t_ref, sim_ref):
+    totals = jnp.sum(rows_ref[...], axis=0, keepdims=True)
+    cells = NZ * NX * NY
+    velocity_scale = STEP_LENGTH / jnp.sqrt(totals[:, 0:1] / cells + EPSILON)
+    image_scale = 1.0 / jnp.sqrt(totals[:, 1:2] / cells + EPSILON)
+    sim_ref[...] = totals[:, 2:3] * (0.5 / (DEVICES * cells))
+    for j in range(3):
+        for d in range(3):
+            v_ref[j, d] = u_ref[j, d] * velocity_scale
+        t_ref[j] = (m_ref[j] - adv_ref[j] * velocity_scale) * image_scale
+
+
+def finish(rows, u, advected, m):
+    vm = pl.BlockSpec(memory_space=pltpu.VMEM)
+    return pl.pallas_call(
+        finish_kernel,
+        out_shape=[
+            jax.ShapeDtypeStruct((3, 3, NX, NY), F32),
+            jax.ShapeDtypeStruct((3, NX, NY), F32),
+            jax.ShapeDtypeStruct((1, 1), F32),
+        ],
+        in_specs=[vm] * 4,
+        out_specs=[vm] * 3,
+        compiler_params=pltpu.CompilerParams(vmem_limit_bytes=12 << 20),
+        name="finish",
+    )(rows, u, advected, m)
 
 
 def after(value, *others):
@@ -431,14 +505,14 @@
     return parts[0] + got[0] + got[1] + got[2]
 
 
-def on_device(template, subjects):
+def step(template, subjects):
     grp = lax.axis_index("grp")
     sub = lax.axis_index("sub")
     core = grp % 2
     xl, y, z = sub // 16, (sub // 4) % 4, sub % 4
     first = jnp.where(core == 0, z, y)
     second = jnp.where(core == 0, y, z)
-    idx = jnp.stack([core, first, second, xl, sub]).astype(jnp.int32)
+    idx = jnp.stack([core, first, second, xl, sub, grp // 2]).astype(jnp.int32)
 
     mine = lax.dynamic_slice_in_dim(template, 40 * core, WIN, axis=1)
     copies = jnp.broadcast_to(mine[None], (32, 3, WIN, NY))
@@ -452,14 +526,15 @@
 
     j_blocks = pair_sum(idx, keep, take)
     jplane = moving_planes(after(idx, *j_blocks), keep, take)
-    j_blocks, jplane = lax.optimization_barrier((j_blocks, jplane))
     j_got = round_one(j_blocks)
     *f_blocks, cc, i_half = factors(idx, image, keep, take, jplane)
     f_got = round_one(f_blocks)
     j_own = after(j_blocks[0], cc)
-    j_part = round_two(j_own + j_got[0] + j_got[1] + j_got[2])
-    f_part = round_two(f_blocks[0] + f_got[0] + f_got[1] + f_got[2])
-    i_other = permute(i_half.astype(BF16), CORE_PAIRS).astype(F32)
+    j_total = j_own + j_got[0] + j_got[1] + j_got[2]
+    j_part = round_two(j_total)
+    i_other = permute(i_half.astype(BF16), CORE_PAIRS)
+    f_total = f_blocks[0] + f_got[0] + f_got[1] + f_got[2]
+    f_part = round_two(f_total)
 
     both = jnp.concatenate(
         [
@@ -474,35 +549,30 @@
 
     f_half = half[: 3 * OWN]
     m_half = half[3 * OWN : 6 * OWN]
-    up1 = permute(jnp.concatenate([f_half, m_half[2 * OWN :]], axis=0), slab_shift(1))
-    down1 = permute(jnp.concatenate([f_half, m_half[:OWN]], axis=0), slab_shift(-1))
-    up2 = permute(f_half[OWN:], slab_shift(2))
-    down2 = permute(f_half[: 2 * OWN], slab_shift(-2))
-    ext = jnp.concatenate(
-        [
-            up2, up1[: 3 * OWN], f_half, down1[: 3 * OWN], down2,
-            up1[3 * OWN :], m_half, down1[3 * OWN :], half[6 * OWN :],
-        ],
-        axis=0,
-    )
-    other = permute(ext, CORE_PAIRS)
-    u, advected, m, stats = smooth_slab(idx, ext, other, i_half, i_other)
-
+    low = grp < 2
+    near = jnp.concatenate(
+        [f_half, jnp.where(low, m_half[2 * OWN :], m_half[:OWN])], axis=0
+    )
+    far = jnp.where(low, f_half[OWN:], f_half[: 2 * OWN])
+    near = permute(near, slab_shift(1))
+    far = permute(far, slab_shift(2))
+    near_f, near_m = near[: 3 * OWN], near[3 * OWN :]
+    f_side = jnp.where(
+        low, jnp.concatenate([far, near_f], axis=0), jnp.concatenate([near_f, far], axis=0)
+    )
+    side = jnp.concatenate([f_side, near_m], axis=0)
+    twin = permute(side, TWIN_PAIRS)
+    own = jnp.concatenate([half, side], axis=0)
+    other = permute(jnp.concatenate([own, twin], axis=0), CORE_PAIRS)
+    u, advected, m, stats = smooth_slab(idx, own, twin, other, i_half, i_other)
     rows = lax.all_to_all(jnp.broadcast_to(stats[None], (32, 1, NY)), "sub", 0, 0, tiled=True)
-    totals = jnp.sum(rows[:, 0, :3], axis=0)
-    cells = NZ * NX * NY
-    velocity_norm = jnp.sqrt(totals[0] / cells + EPSILON)
-    image_norm = jnp.sqrt(totals[1] / cells + EPSILON)
-    scale = STEP_LENGTH / velocity_norm
-    velocity = u * scale
-    new_template = (m - advected * scale) / image_norm
-    similarity = totals[2] * 0.5 / (DEVICES * cells)
-    return velocity, new_template, similarity
+    velocity, new_template, similarity = finish(rows.reshape(32, NY), u, advected, m)
+    return velocity, new_template, similarity.reshape(())
 
 
 def solution(mesh):
     return jax.shard_map(
-        on_device,
+        step,
         mesh=mesh,
         in_specs=(P("sub", None, None), P(("grp", "sub"), None, None, None)),
         out_specs=(P("sub", None, None, None), P("sub", None, None), P()),

time: 159 us -> 141 us (0.89)
  blocking collectives: 21.4 us -> 12.2 us
  starting transfers between devices: 52.4 us -> 46.1 us
  between operations: 4.19 us -> 0.96 us
  local copies, waits for them, and re-layouts: 12.7 us -> 10.4 us
  waiting for transfers between devices: 36.3 us -> 38.1 us
    all_to_all x1, blocking collectives: 21.4 us -> 12.2 us  [step(): lax.all_to_all(jnp.broadcast_to(stats[None], (32, 1, NY)), 'sub', 0, 0, t...]
    ppermute x22 -> x21, waiting for transfers between devices: 30 us -> 36.9 us  [permute(): return lax.ppermute(x, BOTH, table)]
    ppermute x22 -> x21, starting transfers between devices: 42.9 us -> 36.7 us  [permute(): return lax.ppermute(x, BOTH, table)]
    all_to_all x1, waiting for transfers between devices: 6.32 us -> 1.2 us  [step(): image = lax.all_to_all(copies, 'sub', 0, 0, tiled=True).reshape(NZ, WIN, NY)]
    pallas_call x1, Pallas kernels: 18.4 us -> 16.7 us  [factors(): pl.pallas_call(factor_kernel, out_shape=[block] * 4 + [jax.ShapeDtypeStru...]
    unnamed x24 -> x10, local copies, waits for them, and re-layouts: 7.26 us -> 5.61 us
  transfers between devices with their start and end apart: 23 -> 22, of which waited for: 13 -> 10; matrix products, arithmetic and copies ran while one was open for 0% -> 1% of each run, Pallas kernels for 5% -> 18%
where the time goes in v3:
time: 141 us; the launch traced here: 140 us
  starting transfers between devices  46.1 us (33%)
  waiting for transfers between devices  38.1 us (27%)
  Pallas kernels  30.6 us (22%)
  blocking collectives  12.2 us (9%)
  local copies, waits for them, and re-layouts  10.4 us (7%)
  other arithmetic  1.83 us (1%)
    ppermute x21, waiting for transfers between devices, permute(): return lax.ppermute(x, BOTH, table)  36.9 us
    ppermute x21, starting transfers between devices, permute(): return lax.ppermute(x, BOTH, table)  36.7 us
    pallas_call x1, Pallas kernels, factors(): pl.pallas_call(factor_kernel, out_shape=[block] * 4 + [jax.ShapeDtypeStru...  16.7 us
    all_to_all x1, blocking collectives, step(): lax.all_to_all(jnp.broadcast_to(stats[None], (32, 1, NY)), 'sub', 0, 0, t...  12.2 us
    all_to_all x1, starting transfers between devices, step(): image = lax.all_to_all(copies, 'sub', 0, 0, tiled=True).reshape(NZ, WIN, NY)  9.49 us
    pallas_call x1, Pallas kernels, moving_planes(): pl.pallas_call(moving_kernel, out_shape=jax.ShapeDtypeStruct((4, PAGES, O...  6.12 us
    unnamed x10, local copies, waits for them, and re-layouts  5.61 us
    pallas_call x1, Pallas kernels, smooth_slab(): pl.pallas_call(smooth_kernel, out_shape=[jax.ShapeDtypeStruct((3, 3, NX,...  3.98 us
  transfers between devices with their start and end apart: 22, of which 10 were waited for; matrix products, arithmetic and copies ran while one was open for 1% of the time, Pallas kernels for 18%

profile of v3, /device:TPU:0, one launch (start us, length us, event | category | flops | bytes accessed | tf_op | source)
XLA Modules:
  0.0 140.3 jit_solution(14507453413933413905)
XLA Ops:
  0.6 0.0 copy-start
  0.7 0.9 copy-done
  1.5 1.3 broadcast_in_dim.8
  2.8 3.3 %dynamic-slice_bitcast_fusion = (bf16[96,56,128]{2,1,0:T(8,128)(2,1)}, bf16[96,56,128]{2,1,0:T(8,128)(2,1)S(1)}) fusion(bf16[1,96,96,128]{3,2,1,0:T(8,128)(2,1)} %param.3, s32[]{:T(128)S(6)} %select_n.71, s32[]{:T(128)S(6)} %select_n.70), kind=kLoop, calls=%fused_computation | loop fusion | bytes 5505032 | tf_op jit(solution)/shard_map/dynamic_slice | solution.py:523
  6.1 0.0 collective-permute-start
  6.1 9.5 %all-to-all-start = ((bf16[32,3,56,128]{3,2,1,0:T(8,128)(2,1)}), bf16[32,3,56,128]{3,2,1,0:T(8,128)(2,1)}, u32[]{:S(2)}, u32[]{:S(2)}) async-start(bf16[32,3,56,128]{3,2,1,0:T(8,128)(2,1)} %broadcast_in_dim.8), calls=%async_computation | async-start | bytes 2752512 | tf_op jit(solution)/shard_map/all_to_all | solution.py:520
  15.7 0.1 stack.27.idx
  15.8 0.0 collective-permute-done.jb_ref
  15.8 0.0 copy-start.1
  15.8 2.8 %pair_sum.1 = (f32[8,3,48,128]{3,2,1,0:T(8,128)S(1)}, f32[8,3,48,128]{3,2,1,0:T(8,128)}, f32[8,3,48,128]{3,2,1,0:T(8,128)}, f32[8,3,48,128]{3,2,1,0:T(8,128)}) custom-call(s32[6]{0:T(128)S(1)} %stack.27.idx, bf16[96,56,128]{2,1,0:T(8,128)(2,1)S(1)} %get-tuple-element.46.ja_ref, bf16[96,56,128]{2,1,0:T(8,128)(2,1)S(1)} %collective-permute-done.jb_ref), custom_call_target="tpu_custom_call" | custom-call | flops 1000000 | bytes 6000000 | tf_op jit(solution)/shard_map/pair_sum/pallas_call | solution.py:105
  18.6 0.0 copy-start.2
  18.6 0.8 copy-done.2
  19.5 1.7 %collective-permute-start.7 = (f32[8,3,48,128]{3,2,1,0:T(8,128)}, f32[8,3,48,128]{3,2,1,0:T(8,128)S(1)}, u32[]{:S(2)}, u32[]{:S(2)}) collective-permute-start(f32[8,3,48,128]{3,2,1,0:T(8,128)} %get-tuple-element.27), channel_id=1, source_target_pairs={{0,1},{1,2},{2,3},{3,0},{4,5},{5,6},{6,7},{7,4},{8,9},{9,10},{10,1... | collective-permute-start | bytes 1769480 | tf_op jit(solution)/shard_map/ppermute | solution.py:76
  21.2 2.7 %collective-permute-start.8 = (f32[8,3,48,128]{3,2,1,0:T(8,128)}, f32[8,3,48,128]{3,2,1,0:T(8,128)}, u32[]{:S(2)}, u32[]{:S(2)}) collective-permute-start(f32[8,3,48,128]{3,2,1,0:T(8,128)} %get-tuple-element.28), channel_id=1, source_target_pairs={{0,2},{1,3},{2,0},{3,1},{4,6},{5,7},{6,4},{7,5},{8,10},{9,11},{10,... | collective-permute-start | bytes 1769480 | tf_op jit(solution)/shard_map/ppermute | solution.py:76
  23.9 1.5 %collective-permute-start.9 = (f32[8,3,48,128]{3,2,1,0:T(8,128)}, f32[8,3,48,128]{3,2,1,0:T(8,128)}, u32[]{:S(2)}, u32[]{:S(2)}) collective-permute-start(f32[8,3,48,128]{3,2,1,0:T(8,128)} %get-tuple-element.29), channel_id=1, source_target_pairs={{0,3},{1,0},{2,1},{3,2},{4,7},{5,4},{6,5},{7,6},{8,11},{9,8},{10,9... | collective-permute-start | bytes 1769480 | tf_op jit(solution)/shard_map/ppermute | solution.py:76
  25.3 0.0 copy-done.1
  25.3 6.1 %moving_planes.1.jplane_ref = f32[4,104,48,128]{3,2,1,0:T(8,128)S(1)} custom-call(s32[6]{0:T(128)S(1)} %stack.27.idx, bf16[96,56,128]{2,1,0:T(8,128)(2,1)S(1)} %get-tuple-element.46.ja_ref, bf16[96,56,128]{2,1,0:T(8,128)(2,1)S(1)} %collective-permute-done.jb_ref), custom_call_target="tpu_custom_call" | custom-call | flops 4000000000 | bytes 13000000 | tf_op jit(solution)/shard_map/moving_planes/pallas_call | solution.py:211
  31.4 0.0 copy-start.4
  31.5 3.9 %copy-done.4 = f32[4,104,48,128]{3,2,1,0:T(8,128)} copy-done((f32[4,104,48,128]{3,2,1,0:T(8,128)}, f32[4,104,48,128]{3,2,1,0:T(8,128)S(1)}, u32[]{:S(2)}) %copy-start.4) | copy-done | bytes 10223640
  35.4 1.2 all-to-all-done
  36.6 16.7 %factors.1 = (f32[8,3,48,128]{3,2,1,0:T(8,128)S(1)}, f32[8,3,48,128]{3,2,1,0:T(8,128)S(1)}, f32[8,3,48,128]{3,2,1,0:T(8,128)S(1)}, f32[8,3,48,128]{3,2,1,0:T(8,1...) custom-call(s32[6]{0:T(128)S(1)} %stack.27.idx, bf16[96,56,128]{2,1,0:T(8,128)(2,1)} %bitcast.6.i_ref, ...), custom_call_target="tpu_custom_call" | custom-call | flops 4000000000 | bytes 18000000 | tf_op jit(solution)/shard_map/factors/pallas_call | solution.py:315
  53.3 1.2 collective-permute-start.1
  54.5 1.7 %collective-permute-start.2 = (f32[8,3,48,128]{3,2,1,0:T(8,128)S(1)}, f32[8,3,48,128]{3,2,1,0:T(8,128)S(1)}, u32[]{:S(2)}, u32[]{:S(2)}) collective-permute-start(f32[8,3,48,128]{3,2,1,0:T(8,128)S(1)} %get-tuple-element.33), channel_id=1, source_target_pairs={{0,2},{1,3},{2,0},{3,1},{4,6},{5,7},{6,4},{7,5},{8,10},{9,11},{10,... | collective-permute-start | bytes 1769480 | tf_op jit(solution)/shard_map/ppermute | solution.py:76
  56.1 0.0 collective-permute-done.7
  56.1 1.8 %collective-permute-start.3 = (f32[8,3,48,128]{3,2,1,0:T(8,128)S(1)}, f32[8,3,48,128]{3,2,1,0:T(8,128)S(1)}, u32[]{:S(2)}, u32[]{:S(2)}) collective-permute-start(f32[8,3,48,128]{3,2,1,0:T(8,128)S(1)} %get-tuple-element.34), channel_id=1, source_target_pairs={{0,3},{1,0},{2,1},{3,2},{4,7},{5,4},{6,5},{7,6},{8,11},{9,8},{10,9... | collective-permute-start | bytes 1769480 | tf_op jit(solution)/shard_map/ppermute | solution.py:76
  58.0 0.0 collective-permute-done.8
  58.0 0.0 collective-permute-done.9
  58.0 0.0 copy-done.3
  58.0 1.4 %add_add_fusion = f32[8,3,48,128]{3,2,1,0:T(8,128)S(1)} fusion(f32[8,3,48,128]{3,2,1,0:T(8,128)} %collective-permute-done.9, f32[8,3,48,128]{3,2,1,0:T(8,128)} %collective-permute-done.8, f32[8,3,48,128]{3,2,1,0:T(8,128)S(1)} %copy-done.3, f32[8,3,48,128]{3,2,1,0:T(8,128)S(1)} %collective-permute-done.7), kind=kLoop, calls=%fused_computation.2 | loop fusion | flops 442368 | bytes 2949120 | tf_op jit(solution)/shard_map/add | solution.py:533
  59.4 6.1 %collective-permute-start.10 = (f32[2,3,48,128]{3,2,1,0:T(8,128)S(1)}, f32[2,3,48,128]{3,2,1,0:T(8,128)S(1)}, u32[]{:S(2)}, u32[]{:S(2)}) collective-permute-start(f32[2,3,48,128]{3,2,1,0:T(8,128)S(1)} %get-tuple-element.50), channel_id=1, source_target_pairs={{0,4},{1,5},{2,6},{3,7},{4,8},{5,9},{6,10},{7,11},{8,12},{9,13},{1... | collective-permute-start | bytes 442376 | tf_op jit(solution)/shard_map/ppermute | solution.py:76
  65.6 0.0 collective-permute-start.12
  65.6 6.8 %collective-permute-done.1 = f32[8,3,48,128]{3,2,1,0:T(8,128)S(1)} collective-permute-done((f32[8,3,48,128]{3,2,1,0:T(8,128)S(1)}, f32[8,3,48,128]{3,2,1,0:T(8,128)S(1)}, u32[]{:S(2)}, u32[]{:S(2)}) %collective-permute-start.1) | collective-permute-done | bytes 589856 | tf_op jit(solution)/shard_map/ppermute | solution.py:76
  72.3 3.9 %collective-permute-start.11 = (f32[2,3,48,128]{3,2,1,0:T(8,128)S(1)}, f32[2,3,48,128]{3,2,1,0:T(8,128)S(1)}, u32[]{:S(2)}, u32[]{:S(2)}) collective-permute-start(f32[2,3,48,128]{3,2,1,0:T(8,128)S(1)} %get-tuple-element.52), channel_id=1, source_target_pairs={{0,8},{1,9},{2,10},{3,11},{4,12},{5,13},{6,14},{7,15},{8,0},{9,1},... | collective-permute-start | bytes 442376 | tf_op jit(solution)/shard_map/ppermute | solution.py:76
  76.2 0.0 collective-permute-done.2
  76.2 0.0 collective-permute-done.3
  76.2 0.2 add_add_fusion.1
  76.5 6.2 %collective-permute-start.4 = (f32[2,3,48,128]{3,2,1,0:T(8,128)S(1)}, f32[2,3,48,128]{3,2,1,0:T(8,128)S(1)}, u32[]{:S(2)}, u32[]{:S(2)}) collective-permute-start(f32[2,3,48,128]{3,2,1,0:T(8,128)S(1)} %get-tuple-element.47), channel_id=1, source_target_pairs={{0,4},{1,5},{2,6},{3,7},{4,8},{5,9},{6,10},{7,11},{8,12},{9,13},{1... | collective-permute-start | bytes 442376 | tf_op jit(solution)/shard_map/ppermute | solution.py:76
  82.7 2.7 %collective-permute-start.6 = (f32[2,3,48,128]{3,2,1,0:T(8,128)S(1)}, f32[2,3,48,128]{3,2,1,0:T(8,128)S(1)}, u32[]{:S(2)}, u32[]{:S(2)}) collective-permute-start(f32[2,3,48,128]{3,2,1,0:T(8,128)S(1)} %get-tuple-element.48), channel_id=1, source_target_pairs={{0,12},{1,13},{2,14},{3,15},{4,0},{5,1},{6,2},{7,3},{8,4},{9,5},{1... | collective-permute-start | bytes 442376 | tf_op jit(solution)/shard_map/ppermute | solution.py:76
  85.4 0.0 collective-permute-done.10
  85.4 1.4 collective-permute-start.5
  86.8 0.0 collective-permute-done.12
  86.8 0.0 collective-permute-done.11
  86.9 1.6 %collective-permute-done.4 = f32[2,3,48,128]{3,2,1,0:T(8,128)S(1)} collective-permute-done((f32[2,3,48,128]{3,2,1,0:T(8,128)S(1)}, f32[2,3,48,128]{3,2,1,0:T(8,128)S(1)}, u32[]{:S(2)}, u32[]{:S(2)}) %collective-permute-start.4) | collective-permute-done | bytes 147488 | tf_op jit(solution)/shard_map/ppermute | solution.py:76
  88.5 0.0 collective-permute-done.6
  88.5 3.6 %collective-permute-done.5 = f32[2,3,48,128]{3,2,1,0:T(8,128)S(1)} collective-permute-done((f32[2,3,48,128]{3,2,1,0:T(8,128)S(1)}, f32[2,3,48,128]{3,2,1,0:T(8,128)S(1)}, u32[]{:S(2)}, u32[]{:S(2)}) %collective-permute-start.5) | collective-permute-done | bytes 147488 | tf_op jit(solution)/shard_map/ppermute | solution.py:76
  92.2 2.8 %collective-permute-start.13 = (f32[296,128]{1,0:T(8,128)S(1)}, f32[296,128]{1,0:T(8,128)S(1)}, u32[]{:S(2)}, u32[]{:S(2)}) collective-permute-start(f32[296,128]{1,0:T(8,128)S(1)} %get-tuple-element.53), channel_id=1, source_target_pairs={{0,64},{1,65},{2,66},{3,67},{4,68},{5,69},{6,70},{7,71},{8,72},{9,... | collective-permute-start | bytes 454664 | tf_op jit(solution)/shard_map/ppermute | solution.py:76
  95.0 2.0 %collective-permute-start.15 = (f32[296,128]{1,0:T(8,128)S(1)}, f32[296,128]{1,0:T(8,128)S(1)}, u32[]{:S(2)}, u32[]{:S(2)}) collective-permute-start(f32[296,128]{1,0:T(8,128)S(1)} %get-tuple-element.54), channel_id=1, source_target_pairs={{0,80},{1,81},{2,82},{3,83},{4,84},{5,85},{6,86},{7,87},{8,88},{9,... | collective-permute-start | bytes 454664 | tf_op jit(solution)/shard_map/ppermute | solution.py:76
  96.9 0.1 collective-permute-start.14
  97.0 2.0 %collective-permute-done.13 = f32[296,128]{1,0:T(8,128)S(1)} collective-permute-done((f32[296,128]{1,0:T(8,128)S(1)}, f32[296,128]{1,0:T(8,128)S(1)}, u32[]{:S(2)}, u32[]{:S(2)}) %collective-permute-start.13) | collective-permute-done | bytes 151584 | tf_op jit(solution)/shard_map/ppermute | solution.py:76
  99.0 3.8 %collective-permute-done.15 = f32[296,128]{1,0:T(8,128)S(1)} collective-permute-done((f32[296,128]{1,0:T(8,128)S(1)}, f32[296,128]{1,0:T(8,128)S(1)}, u32[]{:S(2)}, u32[]{:S(2)}) %collective-permute-start.15) | collective-permute-done | bytes 151584 | tf_op jit(solution)/shard_map/ppermute | solution.py:76
  102.8 1.8 %collective-permute-done.14 = f32[296,128]{1,0:T(8,128)S(1)} collective-permute-done((f32[296,128]{1,0:T(8,128)S(1)}, f32[296,128]{1,0:T(8,128)S(1)}, u32[]{:S(2)}, u32[]{:S(2)}) %collective-permute-start.14) | collective-permute-done | bytes 151584 | tf_op jit(solution)/shard_map/ppermute | solution.py:76
  104.7 0.1 collective-permute-start.17
  104.8 0.1 collective-permute-start.16
  104.9 9.2 %collective-permute-done.17 = f32[192,128]{1,0:T(8,128)S(1)} collective-permute-done((f32[192,128]{1,0:T(8,128)S(1)}, f32[192,128]{1,0:T(8,128)S(1)}, u32[]{:S(2)}, u32[]{:S(2)}) %collective-permute-start.17) | collective-permute-done | bytes 98336 | tf_op jit(solution)/shard_map/ppermute | solution.py:76
  114.1 0.0 collective-permute-done.16
  114.2 0.1 collective-permute-start.18
  114.3 6.6 %collective-permute-done.18.twin_ref = f32[288,128]{1,0:T(8,128)S(1)} collective-permute-done((f32[288,128]{1,0:T(8,128)S(1)}, f32[288,128]{1,0:T(8,128)S(1)}, u32[]{:S(2)}, u32[]{:S(2)}) %collective-permute-start.18) | collective-permute-done | bytes 147488 | tf_op jit(solution)/shard_map/ppermute | solution.py:76
  120.9 0.1 collective-permute-start.19
  121.1 0.6 collective-permute-start.20
  121.7 1.4 %collective-permute-done.20.iother_ref = bf16[15,48,128]{2,1,0:T(8,128)(2,1)S(1)} collective-permute-done((bf16[15,48,128]{2,1,0:T(8,128)(2,1)S(1)}, bf16[15,48,128]{2,1,0:T(8,128)(2,1)S(1)}, u32[]{:S(2)}, u32[]{:S(2)}) %collective-permute-start.20) | collective-permute-done | bytes 184352 | tf_op jit(solution)/shard_map/ppermute | solution.py:76
  123.1 0.0 collective-permute-done.19.other_ref
  123.1 4.0 %smooth_slab.1 = (f32[3,3,96,128]{3,2,1,0:T(8,128)S(1)}, f32[3,96,128]{2,1,0:T(8,128)S(1)}, f32[3,96,128]{2,1,0:T(8,128)S(1)}, f32[1,128]{1,0:T(1,128)S(1)}) custom-call(s32[6]{0:T(128)S(1)} %stack.27.idx, f32[584,128]{1,0:T(8,128)S(1)} %pad_maximum_fusion.2.own_ref, f32[288,128]{1,0:T(8,128)S(1)} %collective-permute-done.18.twin_ref, ...), custom_call_target="tpu_custom_call" | custom-call | flops 100000000 | bytes 3000000 | tf_op jit(solution)/shard_map/smooth_slab/pallas_call | solution.py:444
  127.1 12.2 %all_to_all.10 = f32[32,1,128]{2,1,0:T(1,128)S(1)} all-to-all(f32[32,1,128]{2,1,0:T(1,128)S(1)} %broadcast_in_dim.11), channel_id=1, replica_groups=mesh['grp'=4,'sub'=32] {'sub'}, dimensions={0} | all-to-all | bytes 32768 | tf_op jit(solution)/shard_map/all_to_all | solution.py:568
  139.3 0.9 finish.1
  (22 shorter events, 0.4 us)
Async XLA Ops:
  0.6 0.9 copy-start
  6.1 9.7 %collective-permute-start = (bf16[96,56,128]{2,1,0:T(8,128)(2,1)}, bf16[96,56,128]{2,1,0:T(8,128)(2,1)S(1)}, u32[]{:S(2)}, u32[]{:S(2)}) collective-permute-start(bf16[96,56,128]{2,1,0:T(8,128)(2,1)} %get-tuple-element.45), channel_id=1, source_target_pairs={{0,32},{1,33},{2,34},{3,35},{4,36},{5,37},{6,38},{7,39},{8,40},{9,... | collective-permute-start | bytes 4128776 | tf_op jit(solution)/shard_map/ppermute | solution.py:76
  6.1 30.4 %all-to-all-start = ((bf16[32,3,56,128]{3,2,1,0:T(8,128)(2,1)}), bf16[32,3,56,128]{3,2,1,0:T(8,128)(2,1)}, u32[]{:S(2)}, u32[]{:S(2)}) async-start(bf16[32,3,56,128]{3,2,1,0:T(8,128)(2,1)} %broadcast_in_dim.8), calls=%async_computation | async-start | bytes 2752512 | tf_op jit(solution)/shard_map/all_to_all | solution.py:520
  15.8 9.5 %copy-start.1 = (bf16[96,56,128]{2,1,0:T(8,128)(2,1)}, bf16[96,56,128]{2,1,0:T(8,128)(2,1)S(1)}, u32[]{:S(2)}) copy-start(bf16[96,56,128]{2,1,0:T(8,128)(2,1)S(1)} %collective-permute-done.jb_ref) | copy-start | bytes 4128772
  18.6 0.8 copy-start.2
  19.5 36.7 %collective-permute-start.7 = (f32[8,3,48,128]{3,2,1,0:T(8,128)}, f32[8,3,48,128]{3,2,1,0:T(8,128)S(1)}, u32[]{:S(2)}, u32[]{:S(2)}) collective-permute-start(f32[8,3,48,128]{3,2,1,0:T(8,128)} %get-tuple-element.27), channel_id=1, source_target_pairs={{0,1},{1,2},{2,3},{3,0},{4,5},{5,6},{6,7},{7,4},{8,9},{9,10},{10,1... | collective-permute-start | bytes 1769480 | tf_op jit(solution)/shard_map/ppermute | solution.py:76
  21.2 36.8 %collective-permute-start.8 = (f32[8,3,48,128]{3,2,1,0:T(8,128)}, f32[8,3,48,128]{3,2,1,0:T(8,128)}, u32[]{:S(2)}, u32[]{:S(2)}) collective-permute-start(f32[8,3,48,128]{3,2,1,0:T(8,128)} %get-tuple-element.28), channel_id=1, source_target_pairs={{0,2},{1,3},{2,0},{3,1},{4,6},{5,7},{6,4},{7,5},{8,10},{9,11},{10,... | collective-permute-start | bytes 1769480 | tf_op jit(solution)/shard_map/ppermute | solution.py:76
  23.9 34.1 %collective-permute-start.9 = (f32[8,3,48,128]{3,2,1,0:T(8,128)}, f32[8,3,48,128]{3,2,1,0:T(8,128)}, u32[]{:S(2)}, u32[]{:S(2)}) collective-permute-start(f32[8,3,48,128]{3,2,1,0:T(8,128)} %get-tuple-element.29), channel_id=1, source_target_pairs={{0,3},{1,0},{2,1},{3,2},{4,7},{5,4},{6,5},{7,6},{8,11},{9,8},{10,9... | collective-permute-start | bytes 1769480 | tf_op jit(solution)/shard_map/ppermute | solution.py:76
  31.4 3.9 %copy-start.4 = (f32[4,104,48,128]{3,2,1,0:T(8,128)}, f32[4,104,48,128]{3,2,1,0:T(8,128)S(1)}, u32[]{:S(2)}) copy-start(f32[4,104,48,128]{3,2,1,0:T(8,128)S(1)} %moving_planes.1.jplane_ref) | copy-start | bytes 30670852
  36.6 21.4 %copy-start.3 = (f32[8,3,48,128]{3,2,1,0:T(8,128)S(1)}, f32[8,3,48,128]{3,2,1,0:T(8,128)}, u32[]{:S(2)}) copy-start(f32[8,3,48,128]{3,2,1,0:T(8,128)} %copy-done.2) | copy-start | bytes 1769476
  53.3 19.1 %collective-permute-start.1 = (f32[8,3,48,128]{3,2,1,0:T(8,128)S(1)}, f32[8,3,48,128]{3,2,1,0:T(8,128)S(1)}, u32[]{:S(2)}, u32[]{:S(2)}) collective-permute-start(f32[8,3,48,128]{3,2,1,0:T(8,128)S(1)} %get-tuple-element.32), channel_id=1, source_target_pairs={{0,1},{1,2},{2,3},{3,0},{4,5},{5,6},{6,7},{7,4},{8,9},{9,10},{10,1... | collective-permute-start | bytes 1769480 | tf_op jit(solution)/shard_map/ppermute | solution.py:76
  54.5 21.8 %collective-permute-start.2 = (f32[8,3,48,128]{3,2,1,0:T(8,128)S(1)}, f32[8,3,48,128]{3,2,1,0:T(8,128)S(1)}, u32[]{:S(2)}, u32[]{:S(2)}) collective-permute-start(f32[8,3,48,128]{3,2,1,0:T(8,128)S(1)} %get-tuple-element.33), channel_id=1, source_target_pairs={{0,2},{1,3},{2,0},{3,1},{4,6},{5,7},{6,4},{7,5},{8,10},{9,11},{10,... | collective-permute-start | bytes 1769480 | tf_op jit(solution)/shard_map/ppermute | solution.py:76
  56.1 20.1 %collective-permute-start.3 = (f32[8,3,48,128]{3,2,1,0:T(8,128)S(1)}, f32[8,3,48,128]{3,2,1,0:T(8,128)S(1)}, u32[]{:S(2)}, u32[]{:S(2)}) collective-permute-start(f32[8,3,48,128]{3,2,1,0:T(8,128)S(1)} %get-tuple-element.34), channel_id=1, source_target_pairs={{0,3},{1,0},{2,1},{3,2},{4,7},{5,4},{6,5},{7,6},{8,11},{9,8},{10,9... | collective-permute-start | bytes 1769480 | tf_op jit(solution)/shard_map/ppermute | solution.py:76
  59.4 26.0 %collective-permute-start.10 = (f32[2,3,48,128]{3,2,1,0:T(8,128)S(1)}, f32[2,3,48,128]{3,2,1,0:T(8,128)S(1)}, u32[]{:S(2)}, u32[]{:S(2)}) collective-permute-start(f32[2,3,48,128]{3,2,1,0:T(8,128)S(1)} %get-tuple-element.50), channel_id=1, source_target_pairs={{0,4},{1,5},{2,6},{3,7},{4,8},{5,9},{6,10},{7,11},{8,12},{9,13},{1... | collective-permute-start | bytes 442376 | tf_op jit(solution)/shard_map/ppermute | solution.py:76
  65.6 21.2 %collective-permute-start.12 = (f32[2,3,48,128]{3,2,1,0:T(8,128)S(1)}, f32[2,3,48,128]{3,2,1,0:T(8,128)S(1)}, u32[]{:S(2)}, u32[]{:S(2)}) collective-permute-start(f32[2,3,48,128]{3,2,1,0:T(8,128)S(1)} %get-tuple-element.51), channel_id=1, source_target_pairs={{0,12},{1,13},{2,14},{3,15},{4,0},{5,1},{6,2},{7,3},{8,4},{9,5},{1... | collective-permute-start | bytes 442376 | tf_op jit(solution)/shard_map/ppermute | solution.py:76
  72.3 14.5 %collective-permute-start.11 = (f32[2,3,48,128]{3,2,1,0:T(8,128)S(1)}, f32[2,3,48,128]{3,2,1,0:T(8,128)S(1)}, u32[]{:S(2)}, u32[]{:S(2)}) collective-permute-start(f32[2,3,48,128]{3,2,1,0:T(8,128)S(1)} %get-tuple-element.52), channel_id=1, source_target_pairs={{0,8},{1,9},{2,10},{3,11},{4,12},{5,13},{6,14},{7,15},{8,0},{9,1},... | collective-permute-start | bytes 442376 | tf_op jit(solution)/shard_map/ppermute | solution.py:76
  76.5 12.0 %collective-permute-start.4 = (f32[2,3,48,128]{3,2,1,0:T(8,128)S(1)}, f32[2,3,48,128]{3,2,1,0:T(8,128)S(1)}, u32[]{:S(2)}, u32[]{:S(2)}) collective-permute-start(f32[2,3,48,128]{3,2,1,0:T(8,128)S(1)} %get-tuple-element.47), channel_id=1, source_target_pairs={{0,4},{1,5},{2,6},{3,7},{4,8},{5,9},{6,10},{7,11},{8,12},{9,13},{1... | collective-permute-start | bytes 442376 | tf_op jit(solution)/shard_map/ppermute | solution.py:76
  82.7 5.8 %collective-permute-start.6 = (f32[2,3,48,128]{3,2,1,0:T(8,128)S(1)}, f32[2,3,48,128]{3,2,1,0:T(8,128)S(1)}, u32[]{:S(2)}, u32[]{:S(2)}) collective-permute-start(f32[2,3,48,128]{3,2,1,0:T(8,128)S(1)} %get-tuple-element.48), channel_id=1, source_target_pairs={{0,12},{1,13},{2,14},{3,15},{4,0},{5,1},{6,2},{7,3},{8,4},{9,5},{1... | collective-permute-start | bytes 442376 | tf_op jit(solution)/shard_map/ppermute | solution.py:76
  85.4 6.6 %collective-permute-start.5 = (f32[2,3,48,128]{3,2,1,0:T(8,128)S(1)}, f32[2,3,48,128]{3,2,1,0:T(8,128)S(1)}, u32[]{:S(2)}, u32[]{:S(2)}) collective-permute-start(f32[2,3,48,128]{3,2,1,0:T(8,128)S(1)} %get-tuple-element.49), channel_id=1, source_target_pairs={{0,8},{1,9},{2,10},{3,11},{4,12},{5,13},{6,14},{7,15},{8,0},{9,1},... | collective-permute-start | bytes 442376 | tf_op jit(solution)/shard_map/ppermute | solution.py:76
  92.2 6.8 %collective-permute-start.13 = (f32[296,128]{1,0:T(8,128)S(1)}, f32[296,128]{1,0:T(8,128)S(1)}, u32[]{:S(2)}, u32[]{:S(2)}) collective-permute-start(f32[296,128]{1,0:T(8,128)S(1)} %get-tuple-element.53), channel_id=1, source_target_pairs={{0,64},{1,65},{2,66},{3,67},{4,68},{5,69},{6,70},{7,71},{8,72},{9,... | collective-permute-start | bytes 454664 | tf_op jit(solution)/shard_map/ppermute | solution.py:76
  95.0 7.8 %collective-permute-start.15 = (f32[296,128]{1,0:T(8,128)S(1)}, f32[296,128]{1,0:T(8,128)S(1)}, u32[]{:S(2)}, u32[]{:S(2)}) collective-permute-start(f32[296,128]{1,0:T(8,128)S(1)} %get-tuple-element.54), channel_id=1, source_target_pairs={{0,80},{1,81},{2,82},{3,83},{4,84},{5,85},{6,86},{7,87},{8,88},{9,... | collective-permute-start | bytes 454664 | tf_op jit(solution)/shard_map/ppermute | solution.py:76
  96.9 7.7 %collective-permute-start.14 = (f32[296,128]{1,0:T(8,128)S(1)}, f32[296,128]{1,0:T(8,128)S(1)}, u32[]{:S(2)}, u32[]{:S(2)}) collective-permute-start(f32[296,128]{1,0:T(8,128)S(1)} %get-tuple-element.54), channel_id=1, source_target_pairs={{0,16},{1,17},{2,18},{3,19},{4,20},{5,21},{6,22},{7,23},{8,24},{9,... | collective-permute-start | bytes 454664 | tf_op jit(solution)/shard_map/ppermute | solution.py:76
  104.7 9.4 %collective-permute-start.17 = (f32[192,128]{1,0:T(8,128)S(1)}, f32[192,128]{1,0:T(8,128)S(1)}, u32[]{:S(2)}, u32[]{:S(2)}) collective-permute-start(f32[192,128]{1,0:T(8,128)S(1)} %pad_maximum_fusion.4), channel_id=1, source_target_pairs={{0,1},{1,2},{2,3},{3,4},{4,5},{5,6},{6,7},{7,8},{8,9},{9,10},{10,1... | collective-permute-start | bytes 294920 | tf_op jit(solution)/shard_map/ppermute | solution.py:76
  104.8 9.3 %collective-permute-start.16 = (f32[96,128]{1,0:T(8,128)S(1)}, f32[96,128]{1,0:T(8,128)S(1)}, u32[]{:S(2)}, u32[]{:S(2)}) collective-permute-start(f32[96,128]{1,0:T(8,128)S(1)} %slice_select_fusion), channel_id=1, source_target_pairs={{0,2},{1,3},{2,4},{3,5},{4,6},{5,7},{6,8},{7,9},{8,10},{9,11},{10,... | collective-permute-start | bytes 147464 | tf_op jit(solution)/shard_map/ppermute | solution.py:76
  114.2 6.7 %collective-permute-start.18 = (f32[288,128]{1,0:T(8,128)S(1)}, f32[288,128]{1,0:T(8,128)S(1)}, u32[]{:S(2)}, u32[]{:S(2)}) collective-permute-start(f32[288,128]{1,0:T(8,128)S(1)} %pad_maximum_fusion.3), channel_id=1, source_target_pairs={{0,64},{1,65},{2,66},{3,67},{4,68},{5,69},{6,70},{7,71},{8,72},{9,... | collective-permute-start | bytes 442376 | tf_op jit(solution)/shard_map/ppermute | solution.py:76
  120.9 2.1 %collective-permute-start.19 = (f32[872,128]{1,0:T(8,128)S(1)}, f32[872,128]{1,0:T(8,128)S(1)}, u32[]{:S(2)}, u32[]{:S(2)}) collective-permute-start(f32[872,128]{1,0:T(8,128)S(1)} %pad_maximum_fusion), channel_id=1, source_target_pairs={{0,32},{1,33},{2,34},{3,35},{4,36},{5,37},{6,38},{7,39},{8,40},{9,... | collective-permute-start | bytes 1339400 | tf_op jit(solution)/shard_map/ppermute | solution.py:76
  121.1 2.0 %collective-permute-start.20 = (bf16[15,48,128]{2,1,0:T(8,128)(2,1)S(1)}, bf16[15,48,128]{2,1,0:T(8,128)(2,1)S(1)}, u32[]{:S(2)}, u32[]{:S(2)}) collective-permute-start(bf16[15,48,128]{2,1,0:T(8,128)(2,1)S(1)} %convert_element_type.3), channel_id=1, source_target_pairs={{0,32},{1,33},{2,34},{3,35},{4,36},{5,37},{6,38},{7,39},{8,40},{9,... | collective-permute-start | bytes 552968 | tf_op jit(solution)/shard_map/ppermute | solution.py:76

commit v4 on v3

--- a/solution.py
+++ b/solution.py
@@ -13,7 +13,6 @@
 EPSILON = 1e-05
 STEP_LENGTH = 0.5
 VARIANCE = 3.0
-HIGH = lax.Precision.HIGHEST
 F32 = jnp.float32
 BF16 = jnp.bfloat16
 
@@ -115,7 +114,11 @@
 
 
 TOP = 16
-PAGES = NZ + 8
+MOVING_CHUNK = 4
+FACTOR_CHUNK = 2
+MOVING_PAGES = NZ + 2 * MOVING_CHUNK
+FACTOR_PAGES = NZ + 6
+FIRST_ORDER = 1.0 / 27.0
 
 
 def split(product):
@@ -132,14 +135,21 @@
     return band2[:NY], band2
 
 
-def plane_sums(makers, shift, even, odd, three, plane):
+def dot(lhs, rhs):
+    return jnp.dot(lhs, rhs, preferred_element_type=F32)
+
+
+def load(ref, base, chunk):
+    return ref[pl.ds(base, chunk)].reshape(chunk * WIN, NY)
+
+
+def triple_sums(makers, scales, shift, even, odd, three, ring, begin, emit, end):
     band1, band2 = bands()
     volumes, chunk = three.shape[:2]
+    slots = ring.shape[1]
     even[...] = jnp.zeros(even.shape, F32)
     odd[...] = jnp.zeros(odd.shape, F32)
-    for v in range(volumes):
-        for p in range(4):
-            plane[v, NZ + 4 + p] = jnp.zeros((OWN, NY), F32)
+    ring[...] = jnp.zeros(ring.shape, F32)
 
     def along_y(thunk, v, line):
         sums = thunk(band1, band2)
@@ -154,7 +164,7 @@
                 + line[v, j, pl.ds(TOP - 7 + shift, 64), :]
             )
         for j in range(chunk):
-            plane[v, base + j + 4] = (
+            ring[v, (base + j) & (slots - 1)] = (
                 three[v, j, pl.ds(5, OWN), :]
                 + three[v, j, pl.ds(8, OWN), :]
                 + three[v, j, pl.ds(11, OWN), :]
@@ -166,30 +176,37 @@
             along_y(thunks[v], v, line)
             along_x(v, other, (i - 1) * chunk)
 
+    def along_z(n):
+        begin(n)
+        for v in range(volumes):
+            for q in range(2 * chunk):
+                z = 2 * chunk * n - chunk - 1 + q
+                page = (
+                    ring[v, (z - 1) & (slots - 1)]
+                    + ring[v, z & (slots - 1)]
+                    + ring[v, (z + 1) & (slots - 1)]
+                )
+                emit(v, n, q, page * scales[v] if scales[v] is not None else page)
+        end(n)
+
     def step(n, carry):
         both(2 * n, even, odd)
         both(2 * n + 1, odd, even)
+        along_z(n)
         return carry
 
-    lax.fori_loop(0, NZ // chunk // 2, step, 0)
+    steps = NZ // (2 * chunk)
+    lax.fori_loop(0, steps, step, 0)
     for v in range(volumes):
         along_x(v, odd, NZ - chunk)
-
-
-MOVING_CHUNK = 4
-FACTOR_CHUNK = 2
-
-
-def dot(lhs, rhs):
-    return jnp.dot(lhs, rhs, preferred_element_type=F32)
-
-
-def load(ref, base, chunk):
-    return ref[pl.ds(base, chunk)].reshape(chunk * WIN, NY)
-
-
-def moving_kernel(idx, ja_ref, jb_ref, plane, even, odd, three):
+        for j in range(chunk):
+            ring[v, (NZ + j) & (slots - 1)] = jnp.zeros((OWN, NY), F32)
+    along_z(jnp.int32(steps))
+
+
+def moving_kernel(idx, ja_ref, jb_ref, out_ref, even, odd, three, ring, ready, sem):
     shift = pl.multiple_of(idx[0] * 8, 8)
+    length = 2 * MOVING_CHUNK
 
     def makers(base):
         out = []
@@ -203,20 +220,43 @@
             out.append(square)
         return out
 
-    plane_sums(makers, shift, even, odd, three, plane)
+    def copy(n):
+        slot = n & 1
+        return pltpu.make_async_copy(
+            ready.at[slot], out_ref.at[:, pl.ds(n * length, length)], sem.at[slot]
+        )
+
+    def begin(n):
+        @pl.when(n >= 2)
+        def _():
+            copy(n - 2).wait()
+
+    def emit(v, n, q, page):
+        ready[n & 1, v, q] = page
+
+    triple_sums(
+        makers, (FIRST_ORDER, None) * 2, shift, even, odd, three, ring,
+        begin, emit, lambda n: copy(n).start(),
+    )
+    last = jnp.int32(NZ // length)
+    copy(last - 1).wait()
+    copy(last).wait()
 
 
 def moving_planes(idx, ja, jb):
     vm = pl.BlockSpec(memory_space=pltpu.VMEM)
     return pl.pallas_call(
         moving_kernel,
-        out_shape=jax.ShapeDtypeStruct((4, PAGES, OWN, NY), F32),
+        out_shape=jax.ShapeDtypeStruct((4, MOVING_PAGES, OWN, NY), F32),
         in_specs=[pl.BlockSpec(memory_space=pltpu.SMEM), vm, vm],
-        out_specs=vm,
+        out_specs=pl.BlockSpec(memory_space=pltpu.HBM),
         scratch_shapes=[
             pltpu.VMEM((4, MOVING_CHUNK, 88, NY), F32),
             pltpu.VMEM((4, MOVING_CHUNK, 88, NY), F32),
             pltpu.VMEM((4, MOVING_CHUNK, 64, NY), F32),
+            pltpu.VMEM((4, 4 * MOVING_CHUNK, OWN, NY), F32),
+            pltpu.VMEM((2, 4, 2 * MOVING_CHUNK, OWN, NY), F32),
+            pltpu.SemaphoreType.DMA((2,)),
         ],
         compiler_params=pltpu.CompilerParams(vmem_limit_bytes=24 << 20),
         cost_estimate=pl.CostEstimate(flops=4 * 10**9, bytes_accessed=13 * 10**6, transcendentals=0),
@@ -226,11 +266,14 @@
 
 def factor_kernel(
     idx, i_ref, ja_ref, jb_ref, jplane_ref, o0, o1, o2, o3, cc_ref, iext_ref,
-    raw, even, odd, three, iplane, jplane, sem,
+    raw, even, odd, three, ring, iplane, jplane, sem,
 ):
     shift = pl.multiple_of(idx[0] * 8, 8)
     fetch = pltpu.make_async_copy(jplane_ref, jplane, sem)
     fetch.start()
+    for v in range(4):
+        for z in (NZ + 1, NZ + 2):
+            iplane[v, z + 3] = jnp.zeros((OWN, NY), F32)
 
     def makers(base):
         def wide(n, keep):
@@ -250,11 +293,18 @@
             lambda b1, b2: dot(split(wide(0, False) * wide(2, True)), b2),
         ]
 
-    plane_sums(makers, shift, even, odd, three, iplane)
+    def emit(v, n, q, page):
+        iplane[v, 2 * FACTOR_CHUNK * n + q] = page
+
+    nothing = lambda n: None
+    triple_sums(
+        makers, (FIRST_ORDER, None, None, None), shift, even, odd, three, ring,
+        nothing, emit, nothing,
+    )
     fetch.wait()
 
-    eps_b = EPSILON * COUNT**2
-    eps_bc = EPSILON * COUNT**4
+    eps_b = EPSILON * COUNT
+    eps_bc = EPSILON * COUNT**2
 
     def block(out, kb, t, cc):
         slab = slab_of(idx, kb, t // 2, t % 2)
@@ -262,38 +312,31 @@
         for r in range(OWN // 8):
             part = pl.ds(r * 8, 8)
 
-            def boxes(ref, v):
-                pages = [ref[v, first + p, part, :] for p in range(11)]
-                mid = pages[2]
-                for p in range(3, 9):
-                    mid = mid + pages[p]
-                return (
-                    mid + (pages[0] + pages[1]),
-                    mid + (pages[1] + pages[9]),
-                    mid + (pages[9] + pages[10]),
-                )
+            def boxes(ref, v, at):
+                pages = [ref[v, first + at + p, part, :] for p in range(9)]
+                return [pages[j] + pages[j + 3] + pages[j + 6] for j in range(3)]
 
             own = pl.ds(shift + r * 8, 8)
-            si, sii = boxes(iplane, 0), boxes(iplane, 1)
-            var_i = [COUNT * sii[j] - si[j] * si[j] for j in range(3)]
+            si, sii = boxes(iplane, 0, 0), boxes(iplane, 1, 0)
+            var_i = [sii[j] - si[j] * si[j] for j in range(3)]
             slope = [
-                (raw[0, first + j, own, :] - si[j] * (1.0 / COUNT)) / (var_i[j] + eps_b)
+                (raw[0, first + j, own, :] - si[j] * FIRST_ORDER) / (var_i[j] + eps_b)
                 for j in range(3)
             ]
             total = [None] * 3
             for n in range(2):
-                sj, sjj = boxes(jplane, 2 * n), boxes(jplane, 2 * n + 1)
-                sij = boxes(iplane, 2 + n)
+                sj, sjj = boxes(jplane, 2 * n, 2), boxes(jplane, 2 * n + 1, 2)
+                sij = boxes(iplane, 2 + n, 0)
                 for j in range(3):
-                    var_j = COUNT * sjj[j] - sj[j] * sj[j]
-                    cross = COUNT * sij[j] - si[j] * sj[j]
+                    var_j = sjj[j] - sj[j] * sj[j]
+                    cross = sij[j] - si[j] * sj[j]
                     gain = cross / (var_i[j] * var_j + eps_bc)
                     cc = cc + cross * gain
-                    moved = raw[1 + n, first + j, own, :] - sj[j] * (1.0 / COUNT) - cross * slope[j]
+                    moved = raw[1 + n, first + j, own, :] - sj[j] * FIRST_ORDER - cross * slope[j]
                     term = gain * moved
                     total[j] = term if n == 0 else total[j] + term
             for j in range(3):
-                out[t, j, part, :] = total[j] * (2.0 * COUNT**2)
+                out[t, j, part, :] = total[j]
         return cc
 
     cc = jnp.zeros((8, NY), F32)
@@ -317,18 +360,19 @@
         out_shape=[block] * 4
         + [jax.ShapeDtypeStruct((8, NY), F32), jax.ShapeDtypeStruct((15, OWN, NY), F32)],
         in_specs=[pl.BlockSpec(memory_space=pltpu.SMEM), vm, vm, vm]
-        + [pl.BlockSpec(memory_space=pl.ANY)],
+        + [pl.BlockSpec(memory_space=pltpu.HBM)],
         out_specs=[vm] * 6,
         scratch_shapes=[
             pltpu.VMEM((3, NZ, WIN, NY), F32),
             pltpu.VMEM((4, FACTOR_CHUNK, 88, NY), F32),
             pltpu.VMEM((4, FACTOR_CHUNK, 88, NY), F32),
             pltpu.VMEM((4, FACTOR_CHUNK, 64, NY), F32),
-            pltpu.VMEM((4, PAGES, OWN, NY), F32),
-            pltpu.VMEM((4, PAGES, OWN, NY), F32),
+            pltpu.VMEM((4, 4 * FACTOR_CHUNK, OWN, NY), F32),
+            pltpu.VMEM((4, FACTOR_PAGES, OWN, NY), F32),
+            pltpu.VMEM((4, MOVING_PAGES, OWN, NY), F32),
             pltpu.SemaphoreType.DMA,
         ],
-        compiler_params=pltpu.CompilerParams(vmem_limit_bytes=48 << 20),
+        compiler_params=pltpu.CompilerParams(vmem_limit_bytes=44 << 20),
         cost_estimate=pl.CostEstimate(flops=4 * 10**9, bytes_accessed=18 * 10**6, transcendentals=0),
         name="factors",
     )(idx, image, ja, jb, jplane)
@@ -392,7 +436,14 @@
         d = (r - c).astype(F32)
         return jnp.where(jnp.abs(r - c) <= REACH, jnp.exp(-d * d / (2.0 * VARIANCE)) / norm, 0.0)
 
-    gx, gy = matrix(NX), matrix(NY)
+    def halves(x):
+        high = x.astype(BF16)
+        return high, (x - high.astype(F32)).astype(BF16)
+
+    high, low = halves(matrix(NX))
+    gx3 = jnp.concatenate([high, high, low], axis=1)
+    high, low = halves(matrix(NY))
+    gy3 = jnp.concatenate([high, high, low], axis=0)
     row = lax.broadcasted_iota(jnp.int32, (NX, NY), 0)
     lane = lax.broadcasted_iota(jnp.int32, (NX, NY), 1)
 
@@ -404,7 +455,7 @@
         return below - above, right - left
 
     for p in range(13):
-        f = ext[p] * 0.5
+        f = ext[p] * COUNT
         sx, sy = twice_slopes(image[p + 1])
         prod[0, p] = f * (image[p + 2] - image[p])
         prod[1, p] = f * sx
@@ -422,8 +473,9 @@
             acc = prod[d, j] * weights[0]
             for o in range(1, 11):
                 acc = acc + prod[d, j + o] * weights[o]
-            acc = jnp.dot(acc, gy, precision=HIGH, preferred_element_type=F32)
-            acc = jnp.dot(gx, acc, precision=HIGH, preferred_element_type=F32)
+            acc = dot(jnp.concatenate([*halves(acc), halves(acc)[0]], axis=1), gy3)
+            high, low = halves(acc)
+            acc = dot(gx3, jnp.concatenate([high, low, high], axis=0))
             u = acc * mean
             u_ref[j, d] = u
             square = square + u * u
@@ -521,8 +573,8 @@
 
     moving = moving[0]
     give = lax.dynamic_slice_in_dim(moving, 40 * (1 - core), WIN, axis=1)
+    keep = lax.dynamic_slice_in_dim(moving, 40 * core, WIN, axis=1)
     take = permute(give, CORE_PAIRS)
-    keep = lax.dynamic_slice_in_dim(moving, 40 * core, WIN, axis=1)
 
     j_blocks = pair_sum(idx, keep, take)
     jplane = moving_planes(after(idx, *j_blocks), keep, take)
@@ -531,18 +583,11 @@
     f_got = round_one(f_blocks)
     j_own = after(j_blocks[0], cc)
     j_total = j_own + j_got[0] + j_got[1] + j_got[2]
-    j_part = round_two(j_total)
     i_other = permute(i_half.astype(BF16), CORE_PAIRS)
     f_total = f_blocks[0] + f_got[0] + f_got[1] + f_got[2]
-    f_part = round_two(f_total)
-
+    part = round_two(jnp.concatenate([f_total, j_total], axis=1))
     both = jnp.concatenate(
-        [
-            f_part.reshape(2, 3 * OWN, NY),
-            j_part.reshape(2, 3 * OWN, NY),
-            jnp.broadcast_to(cc[None], (2, CC_ROWS, NY)),
-        ],
-        axis=1,
+        [part.reshape(2, 6 * OWN, NY), jnp.broadcast_to(cc[None], (2, CC_ROWS, NY))], axis=1
     )
     half = both[0] + permute(both[0], third_round(2))
     half = half + permute(both[1], third_round(1)) + permute(both[1], third_round(3))

time: 141 us -> 139 us (0.986)
  waiting for transfers between devices: 38.1 us -> 35.8 us
  blocking collectives: 12.2 us -> 14.3 us
    all_to_all x1, blocking collectives: 12.2 us -> 14.3 us  [step(): lax.all_to_all(jnp.broadcast_to(stats[None], (32, 1, NY)), 'sub', 0, 0, t...]
    pallas_call x1, Pallas kernels: 6.12 us -> 8.05 us  [moving_planes(): pl.pallas_call(moving_kernel, out_shape=jax.ShapeDtypeStruct((4, MOVING_P...]
    ppermute x21 -> x18, starting transfers between devices: 36.7 us -> 35.4 us  [permute(): return lax.ppermute(x, BOTH, table)]
    ppermute x21 -> x18, waiting for transfers between devices: 36.9 us -> 35.8 us  [permute(): return lax.ppermute(x, BOTH, table)]
    unnamed x10 -> x8, local copies, waits for them, and re-layouts: 5.61 us -> 5.59 us
  transfers between devices with their start and end apart: 22 -> 19, of which waited for: 10 -> 12; matrix products, arithmetic and copies ran while one was open for 1% -> 1% of each run, Pallas kernels for 18% -> 19%
where the time goes in v4:
time: 139 us; the launch traced here: 138 us
  starting transfers between devices  44.8 us (32%)
  waiting for transfers between devices  35.8 us (26%)
  Pallas kernels  30.2 us (22%)
  blocking collectives  14.3 us (10%)
  local copies, waits for them, and re-layouts  10.3 us (7%)
  other arithmetic  2.03 us (1%)
    ppermute x18, waiting for transfers between devices, permute(): return lax.ppermute(x, BOTH, table)  35.8 us
    ppermute x18, starting transfers between devices, permute(): return lax.ppermute(x, BOTH, table)  35.4 us
    pallas_call x1, Pallas kernels, factors(): pl.pallas_call(factor_kernel, out_shape=[block] * 4 + [jax.ShapeDtypeStru...  15.7 us
    all_to_all x1, blocking collectives, step(): lax.all_to_all(jnp.broadcast_to(stats[None], (32, 1, NY)), 'sub', 0, 0, t...  14.3 us
    all_to_all x1, starting transfers between devices, step(): image = lax.all_to_all(copies, 'sub', 0, 0, tiled=True).reshape(NZ, WIN, NY)  9.49 us
    pallas_call x1, Pallas kernels, moving_planes(): pl.pallas_call(moving_kernel, out_shape=jax.ShapeDtypeStruct((4, MOVING_P...  8.05 us
    unnamed x8, local copies, waits for them, and re-layouts  5.59 us
    dynamic_slice x1, local copies, waits for them, and re-layouts, step(): give = lax.dynamic_slice_in_dim(moving, 40 * (1 - core), WIN, axis=1)  3.34 us
  transfers between devices with their start and end apart: 19, of which 12 were waited for; matrix products, arithmetic and copies ran while one was open for 1% of the time, Pallas kernels for 19%

profile of v4, /device:TPU:0, one launch (start us, length us, event | category | flops | bytes accessed | tf_op | source)
XLA Modules:
  0.0 138.5 jit_solution(9028963137946541725)
XLA Ops:
  0.6 0.0 copy-start
  0.7 0.9 copy-done
  1.5 1.3 broadcast_in_dim.8
  2.8 3.3 %dynamic-slice_bitcast_fusion = (bf16[96,56,128]{2,1,0:T(8,128)(2,1)}, bf16[96,56,128]{2,1,0:T(8,128)(2,1)S(1)}) fusion(bf16[1,96,96,128]{3,2,1,0:T(8,128)(2,1)} %param.3, s32[]{:T(128)S(6)} %select_n.71, s32[]{:T(128)S(6)} %select_n.70), kind=kLoop, calls=%fused_computation.6 | loop fusion | bytes 5505032 | tf_op jit(solution)/shard_map/dynamic_slice | solution.py:575
  6.1 0.0 collective-permute-start
  6.1 9.5 %all-to-all-start = ((bf16[32,3,56,128]{3,2,1,0:T(8,128)(2,1)}), bf16[32,3,56,128]{3,2,1,0:T(8,128)(2,1)}, u32[]{:S(2)}, u32[]{:S(2)}) async-start(bf16[32,3,56,128]{3,2,1,0:T(8,128)(2,1)} %broadcast_in_dim.8), calls=%async_computation | async-start | bytes 2752512 | tf_op jit(solution)/shard_map/all_to_all | solution.py:572
  15.7 0.1 stack.27.idx
  15.8 0.0 collective-permute-done.jb_ref
  15.8 2.8 %pair_sum.1 = (f32[8,3,48,128]{3,2,1,0:T(8,128)S(1)}, f32[8,3,48,128]{3,2,1,0:T(8,128)}, f32[8,3,48,128]{3,2,1,0:T(8,128)}, f32[8,3,48,128]{3,2,1,0:T(8,128)}) custom-call(s32[6]{0:T(128)S(1)} %stack.27.idx, bf16[96,56,128]{2,1,0:T(8,128)(2,1)S(1)} %get-tuple-element.46.ja_ref, bf16[96,56,128]{2,1,0:T(8,128)(2,1)S(1)} %collective-permute-done.jb_ref), custom_call_target="tpu_custom_call" | custom-call | flops 1000000 | bytes 6000000 | tf_op jit(solution)/shard_map/pair_sum/pallas_call | solution.py:104
  18.6 0.0 copy-start.1
  18.6 0.8 copy-done.1
  19.4 1.7 %collective-permute-start.4 = (f32[8,3,48,128]{3,2,1,0:T(8,128)}, f32[8,3,48,128]{3,2,1,0:T(8,128)}, u32[]{:S(2)}, u32[]{:S(2)}) collective-permute-start(f32[8,3,48,128]{3,2,1,0:T(8,128)} %get-tuple-element.27), channel_id=1, source_target_pairs={{0,1},{1,2},{2,3},{3,0},{4,5},{5,6},{6,7},{7,4},{8,9},{9,10},{10,1... | collective-permute-start | bytes 1769480 | tf_op jit(solution)/shard_map/ppermute | solution.py:75
  21.2 2.7 %collective-permute-start.5 = (f32[8,3,48,128]{3,2,1,0:T(8,128)}, f32[8,3,48,128]{3,2,1,0:T(8,128)}, u32[]{:S(2)}, u32[]{:S(2)}) collective-permute-start(f32[8,3,48,128]{3,2,1,0:T(8,128)} %get-tuple-element.28), channel_id=1, source_target_pairs={{0,2},{1,3},{2,0},{3,1},{4,6},{5,7},{6,4},{7,5},{8,10},{9,11},{10,... | collective-permute-start | bytes 1769480 | tf_op jit(solution)/shard_map/ppermute | solution.py:75
  23.8 1.5 %collective-permute-start.6 = (f32[8,3,48,128]{3,2,1,0:T(8,128)}, f32[8,3,48,128]{3,2,1,0:T(8,128)}, u32[]{:S(2)}, u32[]{:S(2)}) collective-permute-start(f32[8,3,48,128]{3,2,1,0:T(8,128)} %get-tuple-element.29), channel_id=1, source_target_pairs={{0,3},{1,0},{2,1},{3,2},{4,7},{5,4},{6,5},{7,6},{8,11},{9,8},{10,9... | collective-permute-start | bytes 1769480 | tf_op jit(solution)/shard_map/ppermute | solution.py:75
  25.3 8.0 %moving_planes.1.jplane_ref = f32[4,104,48,128]{3,2,1,0:T(8,128)S(1)} custom-call(s32[6]{0:T(128)S(1)} %stack.27.idx, bf16[96,56,128]{2,1,0:T(8,128)(2,1)S(1)} %get-tuple-element.46.ja_ref, bf16[96,56,128]{2,1,0:T(8,128)(2,1)S(1)} %collective-permute-done.jb_ref), custom_call_target="tpu_custom_call" | custom-call | flops 4000000000 | bytes 13000000 | tf_op jit(solution)/shard_map/moving_planes/pallas_call | solution.py:248
  33.4 0.0 copy-start.3
  33.4 3.9 %copy-done.3 = f32[4,104,48,128]{3,2,1,0:T(8,128)} copy-done((f32[4,104,48,128]{3,2,1,0:T(8,128)}, f32[4,104,48,128]{3,2,1,0:T(8,128)S(1)}, u32[]{:S(2)}) %copy-start.3) | copy-done | bytes 10223640
  37.3 0.0 all-to-all-done
  37.3 0.0 copy-start.2
  37.3 15.7 %factors.1 = (f32[8,3,48,128]{3,2,1,0:T(8,128)S(1)}, f32[8,3,48,128]{3,2,1,0:T(8,128)S(1)}, f32[8,3,48,128]{3,2,1,0:T(8,128)S(1)}, f32[8,3,48,128]{3,2,1,0:T(8,1...) custom-call(s32[6]{0:T(128)S(1)} %stack.27.idx, bf16[96,56,128]{2,1,0:T(8,128)(2,1)} %bitcast.6.i_ref, ...), custom_call_target="tpu_custom_call" | custom-call | flops 4000000000 | bytes 18000000 | tf_op jit(solution)/shard_map/factors/pallas_call | solution.py:358
  52.9 0.6 collective-permute-start.1
  53.6 1.6 %collective-permute-start.2 = (f32[8,3,48,128]{3,2,1,0:T(8,128)S(1)}, f32[8,3,48,128]{3,2,1,0:T(8,128)S(1)}, u32[]{:S(2)}, u32[]{:S(2)}) collective-permute-start(f32[8,3,48,128]{3,2,1,0:T(8,128)S(1)} %get-tuple-element.33), channel_id=1, source_target_pairs={{0,2},{1,3},{2,0},{3,1},{4,6},{5,7},{6,4},{7,5},{8,10},{9,11},{10,... | collective-permute-start | bytes 1769480 | tf_op jit(solution)/shard_map/ppermute | solution.py:75
  55.1 0.0 collective-permute-done.4
  55.1 1.8 %collective-permute-start.3 = (f32[8,3,48,128]{3,2,1,0:T(8,128)S(1)}, f32[8,3,48,128]{3,2,1,0:T(8,128)S(1)}, u32[]{:S(2)}, u32[]{:S(2)}) collective-permute-start(f32[8,3,48,128]{3,2,1,0:T(8,128)S(1)} %get-tuple-element.34), channel_id=1, source_target_pairs={{0,3},{1,0},{2,1},{3,2},{4,7},{5,4},{6,5},{7,6},{8,11},{9,8},{10,9... | collective-permute-start | bytes 1769480 | tf_op jit(solution)/shard_map/ppermute | solution.py:75
  57.0 0.0 collective-permute-done.5
  57.0 0.0 collective-permute-done.6
  57.0 0.0 copy-done.2
  57.0 1.6 %add_add_fusion = f32[8,3,48,128]{3,2,1,0:T(8,128)S(1)} fusion(f32[8,3,48,128]{3,2,1,0:T(8,128)} %collective-permute-done.6, f32[8,3,48,128]{3,2,1,0:T(8,128)} %collective-permute-done.5, f32[8,3,48,128]{3,2,1,0:T(8,128)S(1)} %copy-done.2, f32[8,3,48,128]{3,2,1,0:T(8,128)} %collective-permute-done.4), kind=kLoop, calls=%fused_computation.8 | loop fusion | flops 442368 | bytes 2949120 | tf_op jit(solution)/shard_map/add | solution.py:585
  58.6 11.9 %collective-permute-done.1 = f32[8,3,48,128]{3,2,1,0:T(8,128)S(1)} collective-permute-done((f32[8,3,48,128]{3,2,1,0:T(8,128)S(1)}, f32[8,3,48,128]{3,2,1,0:T(8,128)S(1)}, u32[]{:S(2)}, u32[]{:S(2)}) %collective-permute-start.1) | collective-permute-done | bytes 589856 | tf_op jit(solution)/shard_map/ppermute | solution.py:75
  70.4 0.0 collective-permute-done.2
  70.4 0.9 collective-permute-done.3
  71.3 0.1 add_add_fusion.1
  71.5 0.1 fusion.5
  71.5 11.1 %collective-permute-start.7 = (f32[2,6,48,128]{3,2,1,0:T(8,128)S(1)}, f32[2,6,48,128]{3,2,1,0:T(8,128)S(1)}, u32[]{:S(2)}, u32[]{:S(2)}) collective-permute-start(f32[2,6,48,128]{3,2,1,0:T(8,128)S(1)} %get-tuple-element.47), channel_id=1, source_target_pairs={{0,4},{1,5},{2,6},{3,7},{4,8},{5,9},{6,10},{7,11},{8,12},{9,13},{1... | collective-permute-start | bytes 884744 | tf_op jit(solution)/shard_map/ppermute | solution.py:75
  82.7 0.0 collective-permute-start.9
  82.7 2.1 %collective-permute-start.8 = (f32[2,6,48,128]{3,2,1,0:T(8,128)S(1)}, f32[2,6,48,128]{3,2,1,0:T(8,128)S(1)}, u32[]{:S(2)}, u32[]{:S(2)}) collective-permute-start(f32[2,6,48,128]{3,2,1,0:T(8,128)S(1)} %get-tuple-element.49), channel_id=1, source_target_pairs={{0,8},{1,9},{2,10},{3,11},{4,12},{5,13},{6,14},{7,15},{8,0},{9,1},... | collective-permute-start | bytes 884744 | tf_op jit(solution)/shard_map/ppermute | solution.py:75
  84.8 2.1 %collective-permute-done.7 = f32[2,6,48,128]{3,2,1,0:T(8,128)S(1)} collective-permute-done((f32[2,6,48,128]{3,2,1,0:T(8,128)S(1)}, f32[2,6,48,128]{3,2,1,0:T(8,128)S(1)}, u32[]{:S(2)}, u32[]{:S(2)}) %collective-permute-start.7) | collective-permute-done | bytes 294944 | tf_op jit(solution)/shard_map/ppermute | solution.py:75
  86.9 2.5 %collective-permute-done.9 = f32[2,6,48,128]{3,2,1,0:T(8,128)S(1)} collective-permute-done((f32[2,6,48,128]{3,2,1,0:T(8,128)S(1)}, f32[2,6,48,128]{3,2,1,0:T(8,128)S(1)}, u32[]{:S(2)}, u32[]{:S(2)}) %collective-permute-start.9) | collective-permute-done | bytes 294944 | tf_op jit(solution)/shard_map/ppermute | solution.py:75
  89.4 1.5 %collective-permute-done.8 = f32[2,6,48,128]{3,2,1,0:T(8,128)S(1)} collective-permute-done((f32[2,6,48,128]{3,2,1,0:T(8,128)S(1)}, f32[2,6,48,128]{3,2,1,0:T(8,128)S(1)}, u32[]{:S(2)}, u32[]{:S(2)}) %collective-permute-start.8) | collective-permute-done | bytes 294944 | tf_op jit(solution)/shard_map/ppermute | solution.py:75
  90.9 0.1 fusion.4
  91.0 2.9 %collective-permute-start.10 = (f32[296,128]{1,0:T(8,128)S(1)}, f32[296,128]{1,0:T(8,128)S(1)}, u32[]{:S(2)}, u32[]{:S(2)}) collective-permute-start(f32[296,128]{1,0:T(8,128)S(1)} %get-tuple-element.50), channel_id=1, source_target_pairs={{0,64},{1,65},{2,66},{3,67},{4,68},{5,69},{6,70},{7,71},{8,72},{9,... | collective-permute-start | bytes 454664 | tf_op jit(solution)/shard_map/ppermute | solution.py:75
  93.9 1.7 %collective-permute-start.12 = (f32[296,128]{1,0:T(8,128)S(1)}, f32[296,128]{1,0:T(8,128)S(1)}, u32[]{:S(2)}, u32[]{:S(2)}) collective-permute-start(f32[296,128]{1,0:T(8,128)S(1)} %get-tuple-element.51), channel_id=1, source_target_pairs={{0,80},{1,81},{2,82},{3,83},{4,84},{5,85},{6,86},{7,87},{8,88},{9,... | collective-permute-start | bytes 454664 | tf_op jit(solution)/shard_map/ppermute | solution.py:75
  95.6 0.3 collective-permute-start.11
  95.9 3.1 %collective-permute-done.10 = f32[296,128]{1,0:T(8,128)S(1)} collective-permute-done((f32[296,128]{1,0:T(8,128)S(1)}, f32[296,128]{1,0:T(8,128)S(1)}, u32[]{:S(2)}, u32[]{:S(2)}) %collective-permute-start.10) | collective-permute-done | bytes 151584 | tf_op jit(solution)/shard_map/ppermute | solution.py:75
  99.0 0.8 collective-permute-done.12
  99.7 2.2 %collective-permute-done.11 = f32[296,128]{1,0:T(8,128)S(1)} collective-permute-done((f32[296,128]{1,0:T(8,128)S(1)}, f32[296,128]{1,0:T(8,128)S(1)}, u32[]{:S(2)}, u32[]{:S(2)}) %collective-permute-start.11) | collective-permute-done | bytes 151584 | tf_op jit(solution)/shard_map/ppermute | solution.py:75
  102.1 0.1 collective-permute-start.14
  102.2 3.3 %collective-permute-start.13 = (f32[96,128]{1,0:T(8,128)S(1)}, f32[96,128]{1,0:T(8,128)S(1)}, u32[]{:S(2)}, u32[]{:S(2)}) collective-permute-start(f32[96,128]{1,0:T(8,128)S(1)} %slice_select_fusion), channel_id=1, source_target_pairs={{0,2},{1,3},{2,4},{3,5},{4,6},{5,7},{6,8},{7,9},{8,10},{9,11},{10,... | collective-permute-start | bytes 147464 | tf_op jit(solution)/shard_map/ppermute | solution.py:75
  105.5 5.7 %collective-permute-done.14 = f32[192,128]{1,0:T(8,128)S(1)} collective-permute-done((f32[192,128]{1,0:T(8,128)S(1)}, f32[192,128]{1,0:T(8,128)S(1)}, u32[]{:S(2)}, u32[]{:S(2)}) %collective-permute-start.14) | collective-permute-done | bytes 98336 | tf_op jit(solution)/shard_map/ppermute | solution.py:75
  111.2 0.3 collective-permute-done.13
  111.5 3.2 %collective-permute-start.15 = (f32[288,128]{1,0:T(8,128)S(1)}, f32[288,128]{1,0:T(8,128)S(1)}, u32[]{:S(2)}, u32[]{:S(2)}) collective-permute-start(f32[288,128]{1,0:T(8,128)S(1)} %pad_maximum_fusion.4), channel_id=1, source_target_pairs={{0,64},{1,65},{2,66},{3,67},{4,68},{5,69},{6,70},{7,71},{8,72},{9,... | collective-permute-start | bytes 442376 | tf_op jit(solution)/shard_map/ppermute | solution.py:75
  114.8 3.5 %collective-permute-done.15.twin_ref = f32[288,128]{1,0:T(8,128)S(1)} collective-permute-done((f32[288,128]{1,0:T(8,128)S(1)}, f32[288,128]{1,0:T(8,128)S(1)}, u32[]{:S(2)}, u32[]{:S(2)}) %collective-permute-start.15) | collective-permute-done | bytes 147488 | tf_op jit(solution)/shard_map/ppermute | solution.py:75
  118.3 0.1 collective-permute-start.16
  118.4 0.6 collective-permute-start.17
  119.0 1.4 %collective-permute-done.17.iother_ref = bf16[15,48,128]{2,1,0:T(8,128)(2,1)S(1)} collective-permute-done((bf16[15,48,128]{2,1,0:T(8,128)(2,1)S(1)}, bf16[15,48,128]{2,1,0:T(8,128)(2,1)S(1)}, u32[]{:S(2)}, u32[]{:S(2)}) %collective-permute-start.17) | collective-permute-done | bytes 184352 | tf_op jit(solution)/shard_map/ppermute | solution.py:75
  120.4 0.0 collective-permute-done.16.other_ref
  120.4 2.7 %smooth_slab.1 = (f32[3,3,96,128]{3,2,1,0:T(8,128)S(1)}, f32[3,96,128]{2,1,0:T(8,128)S(1)}, f32[3,96,128]{2,1,0:T(8,128)S(1)}, f32[1,128]{1,0:T(1,128)S(1)}) custom-call(s32[6]{0:T(128)S(1)} %stack.27.idx, f32[584,128]{1,0:T(8,128)S(1)} %pad_maximum_fusion.1.own_ref, f32[288,128]{1,0:T(8,128)S(1)} %collective-permute-done.15.twin_ref, ...), custom_call_target="tpu_custom_call" | custom-call | flops 100000000 | bytes 3000000 | tf_op jit(solution)/shard_map/smooth_slab/pallas_call | solution.py:496
  123.2 14.3 %all_to_all.10 = f32[32,1,128]{2,1,0:T(1,128)S(1)} all-to-all(f32[32,1,128]{2,1,0:T(1,128)S(1)} %broadcast_in_dim.11), channel_id=1, replica_groups=mesh['grp'=4,'sub'=32] {'sub'}, dimensions={0} | all-to-all | bytes 32768 | tf_op jit(solution)/shard_map/all_to_all | solution.py:613
  137.5 0.9 finish.1
  (16 shorter events, 0.2 us)
Async XLA Ops:
  0.6 0.9 copy-start
  6.1 9.7 %collective-permute-start = (bf16[96,56,128]{2,1,0:T(8,128)(2,1)}, bf16[96,56,128]{2,1,0:T(8,128)(2,1)S(1)}, u32[]{:S(2)}, u32[]{:S(2)}) collective-permute-start(bf16[96,56,128]{2,1,0:T(8,128)(2,1)} %get-tuple-element.45), channel_id=1, source_target_pairs={{0,32},{1,33},{2,34},{3,35},{4,36},{5,37},{6,38},{7,39},{8,40},{9,... | collective-permute-start | bytes 4128776 | tf_op jit(solution)/shard_map/ppermute | solution.py:75
  6.1 31.1 %all-to-all-start = ((bf16[32,3,56,128]{3,2,1,0:T(8,128)(2,1)}), bf16[32,3,56,128]{3,2,1,0:T(8,128)(2,1)}, u32[]{:S(2)}, u32[]{:S(2)}) async-start(bf16[32,3,56,128]{3,2,1,0:T(8,128)(2,1)} %broadcast_in_dim.8), calls=%async_computation | async-start | bytes 2752512 | tf_op jit(solution)/shard_map/all_to_all | solution.py:572
  18.6 0.8 copy-start.1
  19.4 35.7 %collective-permute-start.4 = (f32[8,3,48,128]{3,2,1,0:T(8,128)}, f32[8,3,48,128]{3,2,1,0:T(8,128)}, u32[]{:S(2)}, u32[]{:S(2)}) collective-permute-start(f32[8,3,48,128]{3,2,1,0:T(8,128)} %get-tuple-element.27), channel_id=1, source_target_pairs={{0,1},{1,2},{2,3},{3,0},{4,5},{5,6},{6,7},{7,4},{8,9},{9,10},{10,1... | collective-permute-start | bytes 1769480 | tf_op jit(solution)/shard_map/ppermute | solution.py:75
  21.2 35.8 %collective-permute-start.5 = (f32[8,3,48,128]{3,2,1,0:T(8,128)}, f32[8,3,48,128]{3,2,1,0:T(8,128)}, u32[]{:S(2)}, u32[]{:S(2)}) collective-permute-start(f32[8,3,48,128]{3,2,1,0:T(8,128)} %get-tuple-element.28), channel_id=1, source_target_pairs={{0,2},{1,3},{2,0},{3,1},{4,6},{5,7},{6,4},{7,5},{8,10},{9,11},{10,... | collective-permute-start | bytes 1769480 | tf_op jit(solution)/shard_map/ppermute | solution.py:75
  23.8 33.1 %collective-permute-start.6 = (f32[8,3,48,128]{3,2,1,0:T(8,128)}, f32[8,3,48,128]{3,2,1,0:T(8,128)}, u32[]{:S(2)}, u32[]{:S(2)}) collective-permute-start(f32[8,3,48,128]{3,2,1,0:T(8,128)} %get-tuple-element.29), channel_id=1, source_target_pairs={{0,3},{1,0},{2,1},{3,2},{4,7},{5,4},{6,5},{7,6},{8,11},{9,8},{10,9... | collective-permute-start | bytes 1769480 | tf_op jit(solution)/shard_map/ppermute | solution.py:75
  33.4 3.9 %copy-start.3 = (f32[4,104,48,128]{3,2,1,0:T(8,128)}, f32[4,104,48,128]{3,2,1,0:T(8,128)S(1)}, u32[]{:S(2)}) copy-start(f32[4,104,48,128]{3,2,1,0:T(8,128)S(1)} %moving_planes.1.jplane_ref) | copy-start | bytes 30670852
  37.3 19.7 %copy-start.2 = (f32[8,3,48,128]{3,2,1,0:T(8,128)S(1)}, f32[8,3,48,128]{3,2,1,0:T(8,128)}, u32[]{:S(2)}) copy-start(f32[8,3,48,128]{3,2,1,0:T(8,128)} %copy-done.1) | copy-start | bytes 1769476
  52.9 17.5 %collective-permute-start.1 = (f32[8,3,48,128]{3,2,1,0:T(8,128)S(1)}, f32[8,3,48,128]{3,2,1,0:T(8,128)S(1)}, u32[]{:S(2)}, u32[]{:S(2)}) collective-permute-start(f32[8,3,48,128]{3,2,1,0:T(8,128)S(1)} %get-tuple-element.32), channel_id=1, source_target_pairs={{0,1},{1,2},{2,3},{3,0},{4,5},{5,6},{6,7},{7,4},{8,9},{9,10},{10,1... | collective-permute-start | bytes 1769480 | tf_op jit(solution)/shard_map/ppermute | solution.py:75
  53.6 16.9 %collective-permute-start.2 = (f32[8,3,48,128]{3,2,1,0:T(8,128)S(1)}, f32[8,3,48,128]{3,2,1,0:T(8,128)S(1)}, u32[]{:S(2)}, u32[]{:S(2)}) collective-permute-start(f32[8,3,48,128]{3,2,1,0:T(8,128)S(1)} %get-tuple-element.33), channel_id=1, source_target_pairs={{0,2},{1,3},{2,0},{3,1},{4,6},{5,7},{6,4},{7,5},{8,10},{9,11},{10,... | collective-permute-start | bytes 1769480 | tf_op jit(solution)/shard_map/ppermute | solution.py:75
  55.1 16.2 %collective-permute-start.3 = (f32[8,3,48,128]{3,2,1,0:T(8,128)S(1)}, f32[8,3,48,128]{3,2,1,0:T(8,128)S(1)}, u32[]{:S(2)}, u32[]{:S(2)}) collective-permute-start(f32[8,3,48,128]{3,2,1,0:T(8,128)S(1)} %get-tuple-element.34), channel_id=1, source_target_pairs={{0,3},{1,0},{2,1},{3,2},{4,7},{5,4},{6,5},{7,6},{8,11},{9,8},{10,9... | collective-permute-start | bytes 1769480 | tf_op jit(solution)/shard_map/ppermute | solution.py:75
  71.5 15.4 %collective-permute-start.7 = (f32[2,6,48,128]{3,2,1,0:T(8,128)S(1)}, f32[2,6,48,128]{3,2,1,0:T(8,128)S(1)}, u32[]{:S(2)}, u32[]{:S(2)}) collective-permute-start(f32[2,6,48,128]{3,2,1,0:T(8,128)S(1)} %get-tuple-element.47), channel_id=1, source_target_pairs={{0,4},{1,5},{2,6},{3,7},{4,8},{5,9},{6,10},{7,11},{8,12},{9,13},{1... | collective-permute-start | bytes 884744 | tf_op jit(solution)/shard_map/ppermute | solution.py:75
  82.7 6.7 %collective-permute-start.9 = (f32[2,6,48,128]{3,2,1,0:T(8,128)S(1)}, f32[2,6,48,128]{3,2,1,0:T(8,128)S(1)}, u32[]{:S(2)}, u32[]{:S(2)}) collective-permute-start(f32[2,6,48,128]{3,2,1,0:T(8,128)S(1)} %get-tuple-element.48), channel_id=1, source_target_pairs={{0,12},{1,13},{2,14},{3,15},{4,0},{5,1},{6,2},{7,3},{8,4},{9,5},{1... | collective-permute-start | bytes 884744 | tf_op jit(solution)/shard_map/ppermute | solution.py:75
  82.7 8.2 %collective-permute-start.8 = (f32[2,6,48,128]{3,2,1,0:T(8,128)S(1)}, f32[2,6,48,128]{3,2,1,0:T(8,128)S(1)}, u32[]{:S(2)}, u32[]{:S(2)}) collective-permute-start(f32[2,6,48,128]{3,2,1,0:T(8,128)S(1)} %get-tuple-element.49), channel_id=1, source_target_pairs={{0,8},{1,9},{2,10},{3,11},{4,12},{5,13},{6,14},{7,15},{8,0},{9,1},... | collective-permute-start | bytes 884744 | tf_op jit(solution)/shard_map/ppermute | solution.py:75
  91.0 7.9 %collective-permute-start.10 = (f32[296,128]{1,0:T(8,128)S(1)}, f32[296,128]{1,0:T(8,128)S(1)}, u32[]{:S(2)}, u32[]{:S(2)}) collective-permute-start(f32[296,128]{1,0:T(8,128)S(1)} %get-tuple-element.50), channel_id=1, source_target_pairs={{0,64},{1,65},{2,66},{3,67},{4,68},{5,69},{6,70},{7,71},{8,72},{9,... | collective-permute-start | bytes 454664 | tf_op jit(solution)/shard_map/ppermute | solution.py:75
  93.9 5.9 %collective-permute-start.12 = (f32[296,128]{1,0:T(8,128)S(1)}, f32[296,128]{1,0:T(8,128)S(1)}, u32[]{:S(2)}, u32[]{:S(2)}) collective-permute-start(f32[296,128]{1,0:T(8,128)S(1)} %get-tuple-element.51), channel_id=1, source_target_pairs={{0,80},{1,81},{2,82},{3,83},{4,84},{5,85},{6,86},{7,87},{8,88},{9,... | collective-permute-start | bytes 454664 | tf_op jit(solution)/shard_map/ppermute | solution.py:75
  95.6 6.4 %collective-permute-start.11 = (f32[296,128]{1,0:T(8,128)S(1)}, f32[296,128]{1,0:T(8,128)S(1)}, u32[]{:S(2)}, u32[]{:S(2)}) collective-permute-start(f32[296,128]{1,0:T(8,128)S(1)} %get-tuple-element.51), channel_id=1, source_target_pairs={{0,16},{1,17},{2,18},{3,19},{4,20},{5,21},{6,22},{7,23},{8,24},{9,... | collective-permute-start | bytes 454664 | tf_op jit(solution)/shard_map/ppermute | solution.py:75
  102.1 9.2 %collective-permute-start.14 = (f32[192,128]{1,0:T(8,128)S(1)}, f32[192,128]{1,0:T(8,128)S(1)}, u32[]{:S(2)}, u32[]{:S(2)}) collective-permute-start(f32[192,128]{1,0:T(8,128)S(1)} %pad_maximum_fusion.5), channel_id=1, source_target_pairs={{0,1},{1,2},{2,3},{3,4},{4,5},{5,6},{6,7},{7,8},{8,9},{9,10},{10,1... | collective-permute-start | bytes 294920 | tf_op jit(solution)/shard_map/ppermute | solution.py:75
  102.2 9.3 %collective-permute-start.13 = (f32[96,128]{1,0:T(8,128)S(1)}, f32[96,128]{1,0:T(8,128)S(1)}, u32[]{:S(2)}, u32[]{:S(2)}) collective-permute-start(f32[96,128]{1,0:T(8,128)S(1)} %slice_select_fusion), channel_id=1, source_target_pairs={{0,2},{1,3},{2,4},{3,5},{4,6},{5,7},{6,8},{7,9},{8,10},{9,11},{10,... | collective-permute-start | bytes 147464 | tf_op jit(solution)/shard_map/ppermute | solution.py:75
  111.5 6.7 %collective-permute-start.15 = (f32[288,128]{1,0:T(8,128)S(1)}, f32[288,128]{1,0:T(8,128)S(1)}, u32[]{:S(2)}, u32[]{:S(2)}) collective-permute-start(f32[288,128]{1,0:T(8,128)S(1)} %pad_maximum_fusion.4), channel_id=1, source_target_pairs={{0,64},{1,65},{2,66},{3,67},{4,68},{5,69},{6,70},{7,71},{8,72},{9,... | collective-permute-start | bytes 442376 | tf_op jit(solution)/shard_map/ppermute | solution.py:75
  118.3 2.1 %collective-permute-start.16 = (f32[872,128]{1,0:T(8,128)S(1)}, f32[872,128]{1,0:T(8,128)S(1)}, u32[]{:S(2)}, u32[]{:S(2)}) collective-permute-start(f32[872,128]{1,0:T(8,128)S(1)} %pad_maximum_fusion), channel_id=1, source_target_pairs={{0,32},{1,33},{2,34},{3,35},{4,36},{5,37},{6,38},{7,39},{8,40},{9,... | collective-permute-start | bytes 1339400 | tf_op jit(solution)/shard_map/ppermute | solution.py:75
  118.4 2.0 %collective-permute-start.17 = (bf16[15,48,128]{2,1,0:T(8,128)(2,1)S(1)}, bf16[15,48,128]{2,1,0:T(8,128)(2,1)S(1)}, u32[]{:S(2)}, u32[]{:S(2)}) collective-permute-start(bf16[15,48,128]{2,1,0:T(8,128)(2,1)S(1)} %convert_element_type.3), channel_id=1, source_target_pairs={{0,32},{1,33},{2,34},{3,35},{4,36},{5,37},{6,38},{7,39},{8,40},{9,... | collective-permute-start | bytes 552968 | tf_op jit(solution)/shard_map/ppermute | solution.py:75

commit v5 on v4

--- a/solution.py
+++ b/solution.py
@@ -85,34 +85,6 @@
     return xl * 16 + y * 4 + z
 
 
-def pair_sum_kernel(idx, ja_ref, jb_ref, o0, o1, o2, o3, page):
-    shift = pl.multiple_of(idx[0] * 8, 8)
-    for kb, out in enumerate((o0, o1, o2, o3)):
-
-        def step(t, carry):
-            slab = slab_of(idx, kb, t // 2, t % 2)
-            for j in range(3):
-                page[...] = ja_ref[slab * 3 + j].astype(F32) + jb_ref[slab * 3 + j].astype(F32)
-                out[t, j] = page[pl.ds(shift, OWN), :]
-            return carry
-
-        lax.fori_loop(0, 8, step, 0)
-
-
-def pair_sum(idx, ja, jb):
-    vm = pl.BlockSpec(memory_space=pltpu.VMEM)
-    return pl.pallas_call(
-        pair_sum_kernel,
-        out_shape=[jax.ShapeDtypeStruct((8, 3, OWN, NY), F32)] * 4,
-        in_specs=[pl.BlockSpec(memory_space=pltpu.SMEM), vm, vm],
-        out_specs=[vm] * 4,
-        scratch_shapes=[pltpu.VMEM((WIN, NY), F32)],
-        compiler_params=pltpu.CompilerParams(vmem_limit_bytes=24 << 20),
-        cost_estimate=pl.CostEstimate(flops=10**6, bytes_accessed=6 * 10**6, transcendentals=0),
-        name="pair_sum",
-    )(idx, ja, jb)
-
-
 TOP = 16
 MOVING_CHUNK = 4
 FACTOR_CHUNK = 2
@@ -143,7 +115,7 @@
     return ref[pl.ds(base, chunk)].reshape(chunk * WIN, NY)
 
 
-def triple_sums(makers, scales, shift, even, odd, three, ring, begin, emit, end):
+def triple_sums(makers, scales, shift, even, odd, three, ring, enter, begin, emit, end):
     band1, band2 = bands()
     volumes, chunk = three.shape[:2]
     slots = ring.shape[1]
@@ -190,6 +162,7 @@
         end(n)
 
     def step(n, carry):
+        enter(n)
         both(2 * n, even, odd)
         both(2 * n + 1, odd, even)
         along_z(n)
@@ -204,21 +177,65 @@
     along_z(jnp.int32(steps))
 
 
-def moving_kernel(idx, ja_ref, jb_ref, out_ref, even, odd, three, ring, ready, sem):
+PARTS = 4
+PART = NZ // PARTS
+
+
+def window_fetches(core, pairs_of_refs, sems):
+    rows = pl.ds(pl.multiple_of(core * (NX - WIN), 8), WIN)
+    return [
+        [
+            pltpu.make_async_copy(
+                ref.at[pl.ds(p * PART, PART), rows], held.at[pl.ds(p * PART, PART)], sems.at[i, p]
+            )
+            for i, (ref, held) in enumerate(pairs_of_refs)
+        ]
+        for p in range(PARTS)
+    ]
+
+
+def wait_part(fetches, n, steps):
+    for p in range(PARTS):
+
+        @pl.when(n == p * (steps // PARTS))
+        def _():
+            for fetch in fetches[p]:
+                fetch.wait()
+
+
+def in_hbm(x):
+    return pltpu.with_memory_space_constraint(x, pltpu.HBM)
+
+
+def moving_kernel(
+    idx, ja_hbm, jb_hbm, out_ref, o0, o1, o2, o3,
+    ja_ref, jb_ref, pair, even, odd, three, ring, ready, sem, in_sem, pair_sem,
+):
     shift = pl.multiple_of(idx[0] * 8, 8)
     length = 2 * MOVING_CHUNK
+    steps = NZ // length
+    fetches = window_fetches(idx[0], ((ja_hbm, ja_ref), (jb_hbm, jb_ref)), in_sem)
+    for part in fetches:
+        for fetch in part:
+            fetch.start()
 
     def makers(base):
-        out = []
-        for ref in (ja_ref, jb_ref):
-
-            def square(b1, b2, ref=ref):
-                f = load(ref, base, MOVING_CHUNK).astype(F32)
-                return dot(split(f * f), b2)
-
-            out.append(lambda b1, b2, ref=ref: dot(load(ref, base, MOVING_CHUNK), b1))
-            out.append(square)
-        return out
+        def square(ref, b2):
+            f = load(ref, base, MOVING_CHUNK).astype(F32)
+            return dot(split(f * f), b2)
+
+        def first(b1, b2):
+            fa = load(ja_ref, base, MOVING_CHUNK).astype(F32)
+            fb = load(jb_ref, base, MOVING_CHUNK).astype(F32)
+            pair[pl.ds(base, MOVING_CHUNK)] = (fa + fb).reshape(MOVING_CHUNK, WIN, NY)
+            return dot(load(ja_ref, base, MOVING_CHUNK), b1)
+
+        return [
+            first,
+            lambda b1, b2: square(ja_ref, b2),
+            lambda b1, b2: dot(load(jb_ref, base, MOVING_CHUNK), b1),
+            lambda b1, b2: square(jb_ref, b2),
+        ]
 
     def copy(n):
         slot = n & 1
@@ -236,39 +253,64 @@
 
     triple_sums(
         makers, (FIRST_ORDER, None) * 2, shift, even, odd, three, ring,
-        begin, emit, lambda n: copy(n).start(),
-    )
-    last = jnp.int32(NZ // length)
+        lambda n: wait_part(fetches, n, steps), begin, emit, lambda n: copy(n).start(),
+    )
+    outs = []
+    for kb, out in enumerate((o0, o1, o2, o3)):
+        for t in range(8):
+            slab = slab_of(idx, kb, t // 2, t % 2)
+            outs.append(
+                pltpu.make_async_copy(
+                    pair.at[pl.ds(slab * 3, 3), pl.ds(shift, OWN)], out.at[t], pair_sem.at[kb * 8 + t]
+                )
+            )
+    for out in outs:
+        out.start()
+    last = jnp.int32(steps)
     copy(last - 1).wait()
     copy(last).wait()
+    for out in outs:
+        out.wait()
 
 
 def moving_planes(idx, ja, jb):
-    vm = pl.BlockSpec(memory_space=pltpu.VMEM)
+    hbm = pl.BlockSpec(memory_space=pltpu.HBM)
     return pl.pallas_call(
         moving_kernel,
-        out_shape=jax.ShapeDtypeStruct((4, MOVING_PAGES, OWN, NY), F32),
-        in_specs=[pl.BlockSpec(memory_space=pltpu.SMEM), vm, vm],
-        out_specs=pl.BlockSpec(memory_space=pltpu.HBM),
+        out_shape=[pltpu.HBM((4, MOVING_PAGES, OWN, NY), F32)]
+        + [pltpu.HBM((8, 3, OWN, NY), F32)] * 4,
+        in_specs=[pl.BlockSpec(memory_space=pltpu.SMEM), hbm, hbm],
+        out_specs=[hbm] * 5,
         scratch_shapes=[
+            pltpu.VMEM((NZ, WIN, NY), BF16),
+            pltpu.VMEM((NZ, WIN, NY), BF16),
+            pltpu.VMEM((NZ, WIN, NY), F32),
             pltpu.VMEM((4, MOVING_CHUNK, 88, NY), F32),
             pltpu.VMEM((4, MOVING_CHUNK, 88, NY), F32),
             pltpu.VMEM((4, MOVING_CHUNK, 64, NY), F32),
             pltpu.VMEM((4, 4 * MOVING_CHUNK, OWN, NY), F32),
             pltpu.VMEM((2, 4, 2 * MOVING_CHUNK, OWN, NY), F32),
             pltpu.SemaphoreType.DMA((2,)),
+            pltpu.SemaphoreType.DMA((2, PARTS)),
+            pltpu.SemaphoreType.DMA((32,)),
         ],
-        compiler_params=pltpu.CompilerParams(vmem_limit_bytes=24 << 20),
-        cost_estimate=pl.CostEstimate(flops=4 * 10**9, bytes_accessed=13 * 10**6, transcendentals=0),
+        compiler_params=pltpu.CompilerParams(vmem_limit_bytes=28 << 20),
+        cost_estimate=pl.CostEstimate(flops=4 * 10**9, bytes_accessed=17 * 10**6, transcendentals=0),
         name="moving_planes",
-    )(idx, ja, jb)
+    )(idx, in_hbm(ja), in_hbm(jb))
 
 
 def factor_kernel(
-    idx, i_ref, ja_ref, jb_ref, jplane_ref, o0, o1, o2, o3, cc_ref, iext_ref,
-    raw, even, odd, three, ring, iplane, jplane, sem,
+    idx, i_hbm, ja_hbm, jb_hbm, jplane_ref, o0, o1, o2, o3, cc_ref, iext_ref,
+    i_ref, ja_ref, jb_ref, raw, even, odd, three, ring, iplane, jplane, sem, in_sem, i_sem,
 ):
     shift = pl.multiple_of(idx[0] * 8, 8)
+    fetches = window_fetches(idx[0], ((ja_hbm, ja_ref), (jb_hbm, jb_ref)), in_sem)
+    for p in range(PARTS):
+        part = pl.ds(p * PART, PART)
+        fetches[p].append(pltpu.make_async_copy(i_hbm.at[part], i_ref.at[part], i_sem.at[p]))
+        for fetch in fetches[p]:
+            fetch.start()
     fetch = pltpu.make_async_copy(jplane_ref, jplane, sem)
     fetch.start()
     for v in range(4):
@@ -297,9 +339,10 @@
         iplane[v, 2 * FACTOR_CHUNK * n + q] = page
 
     nothing = lambda n: None
+    steps = NZ // (2 * FACTOR_CHUNK)
     triple_sums(
         makers, (FIRST_ORDER, None, None, None), shift, even, odd, three, ring,
-        nothing, emit, nothing,
+        lambda n: wait_part(fetches, n, steps), nothing, emit, nothing,
     )
     fetch.wait()
 
@@ -359,10 +402,12 @@
         factor_kernel,
         out_shape=[block] * 4
         + [jax.ShapeDtypeStruct((8, NY), F32), jax.ShapeDtypeStruct((15, OWN, NY), F32)],
-        in_specs=[pl.BlockSpec(memory_space=pltpu.SMEM), vm, vm, vm]
-        + [pl.BlockSpec(memory_space=pltpu.HBM)],
+        in_specs=[pl.BlockSpec(memory_space=pltpu.SMEM)] + [pl.BlockSpec(memory_space=pltpu.HBM)] * 4,
         out_specs=[vm] * 6,
         scratch_shapes=[
+            pltpu.VMEM((NZ, WIN, NY), BF16),
+            pltpu.VMEM((NZ, WIN, NY), BF16),
+            pltpu.VMEM((NZ, WIN, NY), BF16),
             pltpu.VMEM((3, NZ, WIN, NY), F32),
             pltpu.VMEM((4, FACTOR_CHUNK, 88, NY), F32),
             pltpu.VMEM((4, FACTOR_CHUNK, 88, NY), F32),
@@ -371,11 +416,13 @@
             pltpu.VMEM((4, FACTOR_PAGES, OWN, NY), F32),
             pltpu.VMEM((4, MOVING_PAGES, OWN, NY), F32),
             pltpu.SemaphoreType.DMA,
+            pltpu.SemaphoreType.DMA((2, PARTS)),
+            pltpu.SemaphoreType.DMA((PARTS,)),
         ],
         compiler_params=pltpu.CompilerParams(vmem_limit_bytes=44 << 20),
         cost_estimate=pl.CostEstimate(flops=4 * 10**9, bytes_accessed=18 * 10**6, transcendentals=0),
         name="factors",
-    )(idx, image, ja, jb, jplane)
+    )(idx, image, in_hbm(ja), in_hbm(jb), in_hbm(jplane))
 
 
 CC_ROWS = 8
@@ -566,18 +613,13 @@
     second = jnp.where(core == 0, y, z)
     idx = jnp.stack([core, first, second, xl, sub, grp // 2]).astype(jnp.int32)
 
+    keep = subjects[0]
+    take = permute(keep, CORE_PAIRS)
     mine = lax.dynamic_slice_in_dim(template, 40 * core, WIN, axis=1)
     copies = jnp.broadcast_to(mine[None], (32, 3, WIN, NY))
-    copies, moving = lax.optimization_barrier((copies, subjects))
     image = lax.all_to_all(copies, "sub", 0, 0, tiled=True).reshape(NZ, WIN, NY)
 
-    moving = moving[0]
-    give = lax.dynamic_slice_in_dim(moving, 40 * (1 - core), WIN, axis=1)
-    keep = lax.dynamic_slice_in_dim(moving, 40 * core, WIN, axis=1)
-    take = permute(give, CORE_PAIRS)
-
-    j_blocks = pair_sum(idx, keep, take)
-    jplane = moving_planes(after(idx, *j_blocks), keep, take)
+    jplane, *j_blocks = moving_planes(idx, keep, take)
     j_got = round_one(j_blocks)
     *f_blocks, cc, i_half = factors(idx, image, keep, take, jplane)
     f_got = round_one(f_blocks)

time: 139 us -> 138 us (level)
  waiting for transfers between devices: 35.8 us -> 56.3 us
  starting transfers between devices: 44.8 us -> 33.9 us
  local copies, waits for them, and re-layouts: 10.3 us -> 2.18 us
  other arithmetic: 2.03 us -> 0.61 us
    ppermute x18, waiting for transfers between devices: 35.8 us -> 47.1 us  [permute(): return lax.ppermute(x, BOTH, table)]
    ppermute x18, starting transfers between devices: 35.4 us -> 24.5 us  [permute(): return lax.ppermute(x, BOTH, table)]
    all_to_all x1, waiting for transfers between devices: 0.01 us -> 9.2 us  [step(): image = lax.all_to_all(copies, 'sub', 0, 0, tiled=True).reshape(NZ, WIN, NY)]
    unnamed x8 -> x10, local copies, waits for them, and re-layouts: 5.59 us -> 0.78 us
    dynamic_slice x1 -> x0, local copies, waits for them, and re-layouts: 3.34 us -> none  [step(): give = lax.dynamic_slice_in_dim(moving, 40 * (1 - core), WIN, axis=1)]
    add x1, other arithmetic: 1.57 us -> 0.13 us  [step(): j_total = j_own + j_got[0] + j_got[1] + j_got[2]]
    pallas_call x2 -> x1, Pallas kernels: 10.9 us -> 10.3 us  [moving_planes(): pl.pallas_call(moving_kernel, out_shape=[pltpu.HBM((4, MOVING_PAGES, OWN,...]
  transfers between devices with their start and end apart: 19 -> 19, of which waited for: 12 -> 17; matrix products, arithmetic and copies ran while one was open for 1% -> 1% of each run, Pallas kernels for 19% -> 8%
where the time goes in v5:
time: 138 us; the launch traced here: 137 us
  waiting for transfers between devices  56.3 us (41%)
  starting transfers between devices  33.9 us (25%)
  Pallas kernels  29.7 us (22%)
  blocking collectives  13.2 us (10%)
  local copies, waits for them, and re-layouts  2.18 us (2%)
    ppermute x18, waiting for transfers between devices, permute(): return lax.ppermute(x, BOTH, table)  47.1 us
    ppermute x18, starting transfers between devices, permute(): return lax.ppermute(x, BOTH, table)  24.5 us
    pallas_call x1, Pallas kernels, factors(): pl.pallas_call(factor_kernel, out_shape=[block] * 4 + [jax.ShapeDtypeStru...  15.7 us
    all_to_all x1, blocking collectives, step(): lax.all_to_all(jnp.broadcast_to(stats[None], (32, 1, NY)), 'sub', 0, 0, t...  13.2 us
    pallas_call x1, Pallas kernels, moving_planes(): pl.pallas_call(moving_kernel, out_shape=[pltpu.HBM((4, MOVING_PAGES, OWN,...  10.3 us
    all_to_all x1, starting transfers between devices, step(): image = lax.all_to_all(copies, 'sub', 0, 0, tiled=True).reshape(NZ, WIN, NY)  9.37 us
    all_to_all x1, waiting for transfers between devices, step(): image = lax.all_to_all(copies, 'sub', 0, 0, tiled=True).reshape(NZ, WIN, NY)  9.2 us
  transfers between devices with their start and end apart: 19, of which 17 were waited for; matrix products, arithmetic and copies ran while one was open for 1% of the time, Pallas kernels for 8%

profile of v5, /device:TPU:0, one launch (start us, length us, event | category | flops | bytes accessed | tf_op | source)
XLA Modules:
  0.0 136.8 jit_solution(18382087838093755011)
XLA Ops:
  0.6 0.0 copy-start
  0.6 0.1 collective-permute-start
  0.8 0.8 copy-done
  1.5 1.3 broadcast_in_dim.8
  2.8 9.4 %all-to-all-start = ((bf16[32,3,56,128]{3,2,1,0:T(8,128)(2,1)}), bf16[32,3,56,128]{3,2,1,0:T(8,128)(2,1)S(1)}, u32[]{:S(2)}, u32[]{:S(2)}) async-start(bf16[32,3,56,128]{3,2,1,0:T(8,128)(2,1)} %broadcast_in_dim.8), calls=%async_computation | async-start | bytes 2752512 | tf_op jit(solution)/shard_map/all_to_all | solution.py:620
  12.2 0.1 stack.27.idx
  12.3 0.0 collective-permute-done.jb_hbm
  12.3 10.3 %moving_planes.1 = (f32[4,104,48,128]{3,2,1,0:T(8,128)}, f32[8,3,48,128]{3,2,1,0:T(8,128)}, f32[8,3,48,128]{3,2,1,0:T(8,128)}, f32[8,3,48,128]{3,2,1,0:T(8,128)}, f32[8,3,48,128]{3,2,1,0:T(8,128)}) custom-call(s32[6]{0:T(128)S(1)} %stack.27.idx, bf16[96,96,128]{2,1,0:T(8,128)(2,1)} %bitcast.24, bf16[96,96,128]{2,1,0:T(8,128)(2,1)} %collective-permute-done.jb_hbm), custom_call_target="tpu_custom_call" | custom-call | flops 4000000000 | bytes 17000000 | tf_op jit(solution)/shard_map/moving_planes/pallas_call | solution.py:278
  22.7 9.2 %all-to-all-done = bf16[32,3,56,128]{3,2,1,0:T(8,128)(2,1)S(1)} async-done(((bf16[32,3,56,128]{3,2,1,0:T(8,128)(2,1)}), bf16[32,3,56,128]{3,2,1,0:T(8,128)(2,1)S(1)}, u32[]{:S(2)}, u32[]{:S(2)}) %all-to-all-start) | async-done | bytes 1376288 | tf_op jit(solution)/shard_map/all_to_all | solution.py:620
  31.9 0.0 copy-start.4
  31.9 0.0 copy-start.3
  31.9 0.0 copy-start.2
  31.9 15.7 %factors.1 = (f32[8,3,48,128]{3,2,1,0:T(8,128)S(1)}, f32[8,3,48,128]{3,2,1,0:T(8,128)S(1)}, f32[8,3,48,128]{3,2,1,0:T(8,128)S(1)}, f32[8,3,48,128]{3,2,1,0:T(8,1...) custom-call(s32[6]{0:T(128)S(1)} %stack.27.idx, bf16[96,56,128]{2,1,0:T(8,128)(2,1)S(1)} %bitcast.18, ...), custom_call_target="tpu_custom_call" | custom-call | flops 4000000000 | bytes 18000000 | tf_op jit(solution)/shard_map/factors/pallas_call | solution.py:401
  47.5 1.5 %collective-permute-start.1 = (f32[8,3,48,128]{3,2,1,0:T(8,128)S(1)}, f32[8,3,48,128]{3,2,1,0:T(8,128)S(1)}, u32[]{:S(2)}, u32[]{:S(2)}) collective-permute-start(f32[8,3,48,128]{3,2,1,0:T(8,128)S(1)} %get-tuple-element.24), channel_id=1, source_target_pairs={{0,1},{1,2},{2,3},{3,0},{4,5},{5,6},{6,7},{7,4},{8,9},{9,10},{10,1... | collective-permute-start | bytes 1769480 | tf_op jit(solution)/shard_map/ppermute | solution.py:75
  49.0 2.0 %collective-permute-start.2 = (f32[8,3,48,128]{3,2,1,0:T(8,128)S(1)}, f32[8,3,48,128]{3,2,1,0:T(8,128)S(1)}, u32[]{:S(2)}, u32[]{:S(2)}) collective-permute-start(f32[8,3,48,128]{3,2,1,0:T(8,128)S(1)} %get-tuple-element.25), channel_id=1, source_target_pairs={{0,2},{1,3},{2,0},{3,1},{4,6},{5,7},{6,4},{7,5},{8,10},{9,11},{10,... | collective-permute-start | bytes 1769480 | tf_op jit(solution)/shard_map/ppermute | solution.py:75
  51.1 1.8 %collective-permute-start.3 = (f32[8,3,48,128]{3,2,1,0:T(8,128)S(1)}, f32[8,3,48,128]{3,2,1,0:T(8,128)S(1)}, u32[]{:S(2)}, u32[]{:S(2)}) collective-permute-start(f32[8,3,48,128]{3,2,1,0:T(8,128)S(1)} %get-tuple-element.26), channel_id=1, source_target_pairs={{0,3},{1,0},{2,1},{3,2},{4,7},{5,4},{6,5},{7,6},{8,11},{9,8},{10,9... | collective-permute-start | bytes 1769480 | tf_op jit(solution)/shard_map/ppermute | solution.py:75
  52.9 0.0 copy-done.4
  52.9 0.2 collective-permute-start.4
  53.1 0.0 copy-done.3
  53.1 1.5 %collective-permute-start.5 = (f32[8,3,48,128]{3,2,1,0:T(8,128)S(1)}, f32[8,3,48,128]{3,2,1,0:T(8,128)S(1)}, u32[]{:S(2)}, u32[]{:S(2)}) collective-permute-start(f32[8,3,48,128]{3,2,1,0:T(8,128)S(1)} %copy-done.3), channel_id=1, source_target_pairs={{0,2},{1,3},{2,0},{3,1},{4,6},{5,7},{6,4},{7,5},{8,10},{9,11},{10,... | collective-permute-start | bytes 1769480 | tf_op jit(solution)/shard_map/ppermute | solution.py:75
  54.6 4.1 %collective-permute-done.1 = f32[8,3,48,128]{3,2,1,0:T(8,128)S(1)} collective-permute-done((f32[8,3,48,128]{3,2,1,0:T(8,128)S(1)}, f32[8,3,48,128]{3,2,1,0:T(8,128)S(1)}, u32[]{:S(2)}, u32[]{:S(2)}) %collective-permute-start.1) | collective-permute-done | bytes 589856 | tf_op jit(solution)/shard_map/ppermute | solution.py:75
  58.7 0.0 copy-done.2
  58.7 0.8 collective-permute-start.6
  59.5 5.9 %collective-permute-done.2 = f32[8,3,48,128]{3,2,1,0:T(8,128)S(1)} collective-permute-done((f32[8,3,48,128]{3,2,1,0:T(8,128)S(1)}, f32[8,3,48,128]{3,2,1,0:T(8,128)S(1)}, u32[]{:S(2)}, u32[]{:S(2)}) %collective-permute-start.2) | collective-permute-done | bytes 589856 | tf_op jit(solution)/shard_map/ppermute | solution.py:75
  65.3 0.6 collective-permute-done.3
  65.9 0.0 copy-start.1
  65.9 0.1 add_add_fusion.1
  66.1 5.3 %collective-permute-done.4 = f32[8,3,48,128]{3,2,1,0:T(8,128)S(1)} collective-permute-done((f32[8,3,48,128]{3,2,1,0:T(8,128)S(1)}, f32[8,3,48,128]{3,2,1,0:T(8,128)S(1)}, u32[]{:S(2)}, u32[]{:S(2)}) %collective-permute-start.4) | collective-permute-done | bytes 589856 | tf_op jit(solution)/shard_map/ppermute | solution.py:75
  71.3 6.6 %collective-permute-done.5 = f32[8,3,48,128]{3,2,1,0:T(8,128)S(1)} collective-permute-done((f32[8,3,48,128]{3,2,1,0:T(8,128)S(1)}, f32[8,3,48,128]{3,2,1,0:T(8,128)S(1)}, u32[]{:S(2)}, u32[]{:S(2)}) %collective-permute-start.5) | collective-permute-done | bytes 589856 | tf_op jit(solution)/shard_map/ppermute | solution.py:75
  77.9 0.7 collective-permute-done.6
  78.6 0.0 copy-done.1
  78.6 0.1 add_add_fusion
  78.7 0.1 fusion.5
  78.8 1.5 %collective-permute-start.7 = (f32[2,6,48,128]{3,2,1,0:T(8,128)S(1)}, f32[2,6,48,128]{3,2,1,0:T(8,128)S(1)}, u32[]{:S(2)}, u32[]{:S(2)}) collective-permute-start(f32[2,6,48,128]{3,2,1,0:T(8,128)S(1)} %get-tuple-element.41), channel_id=1, source_target_pairs={{0,4},{1,5},{2,6},{3,7},{4,8},{5,9},{6,10},{7,11},{8,12},{9,13},{1... | collective-permute-start | bytes 884744 | tf_op jit(solution)/shard_map/ppermute | solution.py:75
  80.3 1.8 %collective-permute-start.9 = (f32[2,6,48,128]{3,2,1,0:T(8,128)S(1)}, f32[2,6,48,128]{3,2,1,0:T(8,128)S(1)}, u32[]{:S(2)}, u32[]{:S(2)}) collective-permute-start(f32[2,6,48,128]{3,2,1,0:T(8,128)S(1)} %get-tuple-element.42), channel_id=1, source_target_pairs={{0,12},{1,13},{2,14},{3,15},{4,0},{5,1},{6,2},{7,3},{8,4},{9,5},{1... | collective-permute-start | bytes 884744 | tf_op jit(solution)/shard_map/ppermute | solution.py:75
  82.1 1.2 collective-permute-start.8
  83.3 3.5 %collective-permute-done.7 = f32[2,6,48,128]{3,2,1,0:T(8,128)S(1)} collective-permute-done((f32[2,6,48,128]{3,2,1,0:T(8,128)S(1)}, f32[2,6,48,128]{3,2,1,0:T(8,128)S(1)}, u32[]{:S(2)}, u32[]{:S(2)}) %collective-permute-start.7) | collective-permute-done | bytes 294944 | tf_op jit(solution)/shard_map/ppermute | solution.py:75
  86.8 2.7 %collective-permute-done.9 = f32[2,6,48,128]{3,2,1,0:T(8,128)S(1)} collective-permute-done((f32[2,6,48,128]{3,2,1,0:T(8,128)S(1)}, f32[2,6,48,128]{3,2,1,0:T(8,128)S(1)}, u32[]{:S(2)}, u32[]{:S(2)}) %collective-permute-start.9) | collective-permute-done | bytes 294944 | tf_op jit(solution)/shard_map/ppermute | solution.py:75
  89.6 1.0 collective-permute-done.8
  90.5 0.1 fusion.4
  90.7 2.8 %collective-permute-start.10 = (f32[296,128]{1,0:T(8,128)S(1)}, f32[296,128]{1,0:T(8,128)S(1)}, u32[]{:S(2)}, u32[]{:S(2)}) collective-permute-start(f32[296,128]{1,0:T(8,128)S(1)} %get-tuple-element.44), channel_id=1, source_target_pairs={{0,64},{1,65},{2,66},{3,67},{4,68},{5,69},{6,70},{7,71},{8,72},{9,... | collective-permute-start | bytes 454664 | tf_op jit(solution)/shard_map/ppermute | solution.py:75
  93.5 1.3 collective-permute-start.12
  94.8 0.7 collective-permute-start.11
  95.5 1.9 %collective-permute-done.10 = f32[296,128]{1,0:T(8,128)S(1)} collective-permute-done((f32[296,128]{1,0:T(8,128)S(1)}, f32[296,128]{1,0:T(8,128)S(1)}, u32[]{:S(2)}, u32[]{:S(2)}) %collective-permute-start.10) | collective-permute-done | bytes 151584 | tf_op jit(solution)/shard_map/ppermute | solution.py:75
  97.4 1.6 %collective-permute-done.12 = f32[296,128]{1,0:T(8,128)S(1)} collective-permute-done((f32[296,128]{1,0:T(8,128)S(1)}, f32[296,128]{1,0:T(8,128)S(1)}, u32[]{:S(2)}, u32[]{:S(2)}) %collective-permute-start.12) | collective-permute-done | bytes 151584 | tf_op jit(solution)/shard_map/ppermute | solution.py:75
  99.0 2.2 %collective-permute-done.11 = f32[296,128]{1,0:T(8,128)S(1)} collective-permute-done((f32[296,128]{1,0:T(8,128)S(1)}, f32[296,128]{1,0:T(8,128)S(1)}, u32[]{:S(2)}, u32[]{:S(2)}) %collective-permute-start.11) | collective-permute-done | bytes 151584 | tf_op jit(solution)/shard_map/ppermute | solution.py:75
  101.2 0.1 add_add_fusion.2
  101.3 1.0 collective-permute-start.14
  102.3 3.1 %collective-permute-start.13 = (f32[96,128]{1,0:T(8,128)S(1)}, f32[96,128]{1,0:T(8,128)S(1)}, u32[]{:S(2)}, u32[]{:S(2)}) collective-permute-start(f32[96,128]{1,0:T(8,128)S(1)} %slice_select_fusion), channel_id=1, source_target_pairs={{0,2},{1,3},{2,4},{3,5},{4,6},{5,7},{6,8},{7,9},{8,10},{9,11},{10,... | collective-permute-start | bytes 147464 | tf_op jit(solution)/shard_map/ppermute | solution.py:75
  105.4 4.7 %collective-permute-done.14 = f32[192,128]{1,0:T(8,128)S(1)} collective-permute-done((f32[192,128]{1,0:T(8,128)S(1)}, f32[192,128]{1,0:T(8,128)S(1)}, u32[]{:S(2)}, u32[]{:S(2)}) %collective-permute-start.14) | collective-permute-done | bytes 98336 | tf_op jit(solution)/shard_map/ppermute | solution.py:75
  110.2 0.7 collective-permute-done.13
  110.9 2.5 %collective-permute-start.15 = (f32[288,128]{1,0:T(8,128)S(1)}, f32[288,128]{1,0:T(8,128)S(1)}, u32[]{:S(2)}, u32[]{:S(2)}) collective-permute-start(f32[288,128]{1,0:T(8,128)S(1)} %pad_maximum_fusion.4), channel_id=1, source_target_pairs={{0,64},{1,65},{2,66},{3,67},{4,68},{5,69},{6,70},{7,71},{8,72},{9,... | collective-permute-start | bytes 442376 | tf_op jit(solution)/shard_map/ppermute | solution.py:75
  113.4 4.3 %collective-permute-done.15.twin_ref = f32[288,128]{1,0:T(8,128)S(1)} collective-permute-done((f32[288,128]{1,0:T(8,128)S(1)}, f32[288,128]{1,0:T(8,128)S(1)}, u32[]{:S(2)}, u32[]{:S(2)}) %collective-permute-start.15) | collective-permute-done | bytes 147488 | tf_op jit(solution)/shard_map/ppermute | solution.py:75
  117.7 0.1 collective-permute-start.16
  117.8 0.6 collective-permute-start.17
  118.4 1.4 %collective-permute-done.17.iother_ref = bf16[15,48,128]{2,1,0:T(8,128)(2,1)S(1)} collective-permute-done((bf16[15,48,128]{2,1,0:T(8,128)(2,1)S(1)}, bf16[15,48,128]{2,1,0:T(8,128)(2,1)S(1)}, u32[]{:S(2)}, u32[]{:S(2)}) %collective-permute-start.17) | collective-permute-done | bytes 184352 | tf_op jit(solution)/shard_map/ppermute | solution.py:75
  119.9 0.0 collective-permute-done.16.other_ref
  119.9 2.7 %smooth_slab.1 = (f32[3,3,96,128]{3,2,1,0:T(8,128)S(1)}, f32[3,96,128]{2,1,0:T(8,128)S(1)}, f32[3,96,128]{2,1,0:T(8,128)S(1)}, f32[1,128]{1,0:T(1,128)S(1)}) custom-call(s32[6]{0:T(128)S(1)} %stack.27.idx, f32[584,128]{1,0:T(8,128)S(1)} %pad_maximum_fusion.1.own_ref, f32[288,128]{1,0:T(8,128)S(1)} %collective-permute-done.15.twin_ref, ...), custom_call_target="tpu_custom_call" | custom-call | flops 100000000 | bytes 3000000 | tf_op jit(solution)/shard_map/smooth_slab/pallas_call | solution.py:543
  122.6 13.2 %all_to_all.10 = f32[32,1,128]{2,1,0:T(1,128)S(1)} all-to-all(f32[32,1,128]{2,1,0:T(1,128)S(1)} %broadcast_in_dim.11), channel_id=1, replica_groups=mesh['grp'=4,'sub'=32] {'sub'}, dimensions={0} | all-to-all | bytes 32768 | tf_op jit(solution)/shard_map/all_to_all | solution.py:655
  135.9 0.9 finish.1
  (15 shorter events, 0.2 us)
Async XLA Ops:
  0.6 0.9 copy-start
  0.6 11.7 %collective-permute-start = (bf16[96,96,128]{2,1,0:T(8,128)(2,1)}, bf16[96,96,128]{2,1,0:T(8,128)(2,1)}, u32[]{:S(2)}, u32[]{:S(2)}) collective-permute-start(bf16[96,96,128]{2,1,0:T(8,128)(2,1)} %bitcast.23), channel_id=1, source_target_pairs={{0,32},{1,33},{2,34},{3,35},{4,36},{5,37},{6,38},{7,39},{8,40},{9,... | collective-permute-start | bytes 7077896 | tf_op jit(solution)/shard_map/ppermute | solution.py:75
  2.8 29.1 %all-to-all-start = ((bf16[32,3,56,128]{3,2,1,0:T(8,128)(2,1)}), bf16[32,3,56,128]{3,2,1,0:T(8,128)(2,1)S(1)}, u32[]{:S(2)}, u32[]{:S(2)}) async-start(bf16[32,3,56,128]{3,2,1,0:T(8,128)(2,1)} %broadcast_in_dim.8), calls=%async_computation | async-start | bytes 2752512 | tf_op jit(solution)/shard_map/all_to_all | solution.py:620
  31.9 21.0 %copy-start.4 = (f32[8,3,48,128]{3,2,1,0:T(8,128)S(1)}, f32[8,3,48,128]{3,2,1,0:T(8,128)}, u32[]{:S(2)}) copy-start(f32[8,3,48,128]{3,2,1,0:T(8,128)} %get-tuple-element.30) | copy-start | bytes 1769476
  31.9 21.2 %copy-start.3 = (f32[8,3,48,128]{3,2,1,0:T(8,128)S(1)}, f32[8,3,48,128]{3,2,1,0:T(8,128)}, u32[]{:S(2)}) copy-start(f32[8,3,48,128]{3,2,1,0:T(8,128)} %get-tuple-element.31) | copy-start | bytes 1769476
  31.9 26.8 %copy-start.2 = (f32[8,3,48,128]{3,2,1,0:T(8,128)S(1)}, f32[8,3,48,128]{3,2,1,0:T(8,128)}, u32[]{:S(2)}) copy-start(f32[8,3,48,128]{3,2,1,0:T(8,128)} %get-tuple-element.32) | copy-start | bytes 1769476
  47.5 11.2 %collective-permute-start.1 = (f32[8,3,48,128]{3,2,1,0:T(8,128)S(1)}, f32[8,3,48,128]{3,2,1,0:T(8,128)S(1)}, u32[]{:S(2)}, u32[]{:S(2)}) collective-permute-start(f32[8,3,48,128]{3,2,1,0:T(8,128)S(1)} %get-tuple-element.24), channel_id=1, source_target_pairs={{0,1},{1,2},{2,3},{3,0},{4,5},{5,6},{6,7},{7,4},{8,9},{9,10},{10,1... | collective-permute-start | bytes 1769480 | tf_op jit(solution)/shard_map/ppermute | solution.py:75
  49.0 16.3 %collective-permute-start.2 = (f32[8,3,48,128]{3,2,1,0:T(8,128)S(1)}, f32[8,3,48,128]{3,2,1,0:T(8,128)S(1)}, u32[]{:S(2)}, u32[]{:S(2)}) collective-permute-start(f32[8,3,48,128]{3,2,1,0:T(8,128)S(1)} %get-tuple-element.25), channel_id=1, source_target_pairs={{0,2},{1,3},{2,0},{3,1},{4,6},{5,7},{6,4},{7,5},{8,10},{9,11},{10,... | collective-permute-start | bytes 1769480 | tf_op jit(solution)/shard_map/ppermute | solution.py:75
  51.1 14.9 %collective-permute-start.3 = (f32[8,3,48,128]{3,2,1,0:T(8,128)S(1)}, f32[8,3,48,128]{3,2,1,0:T(8,128)S(1)}, u32[]{:S(2)}, u32[]{:S(2)}) collective-permute-start(f32[8,3,48,128]{3,2,1,0:T(8,128)S(1)} %get-tuple-element.26), channel_id=1, source_target_pairs={{0,3},{1,0},{2,1},{3,2},{4,7},{5,4},{6,5},{7,6},{8,11},{9,8},{10,9... | collective-permute-start | bytes 1769480 | tf_op jit(solution)/shard_map/ppermute | solution.py:75
  52.9 18.5 %collective-permute-start.4 = (f32[8,3,48,128]{3,2,1,0:T(8,128)S(1)}, f32[8,3,48,128]{3,2,1,0:T(8,128)S(1)}, u32[]{:S(2)}, u32[]{:S(2)}) collective-permute-start(f32[8,3,48,128]{3,2,1,0:T(8,128)S(1)} %copy-done.4), channel_id=1, source_target_pairs={{0,1},{1,2},{2,3},{3,0},{4,5},{5,6},{6,7},{7,4},{8,9},{9,10},{10,1... | collective-permute-start | bytes 1769480 | tf_op jit(solution)/shard_map/ppermute | solution.py:75
  53.1 24.8 %collective-permute-start.5 = (f32[8,3,48,128]{3,2,1,0:T(8,128)S(1)}, f32[8,3,48,128]{3,2,1,0:T(8,128)S(1)}, u32[]{:S(2)}, u32[]{:S(2)}) collective-permute-start(f32[8,3,48,128]{3,2,1,0:T(8,128)S(1)} %copy-done.3), channel_id=1, source_target_pairs={{0,2},{1,3},{2,0},{3,1},{4,6},{5,7},{6,4},{7,5},{8,10},{9,11},{10,... | collective-permute-start | bytes 1769480 | tf_op jit(solution)/shard_map/ppermute | solution.py:75
  58.7 19.9 %collective-permute-start.6 = (f32[8,3,48,128]{3,2,1,0:T(8,128)S(1)}, f32[8,3,48,128]{3,2,1,0:T(8,128)S(1)}, u32[]{:S(2)}, u32[]{:S(2)}) collective-permute-start(f32[8,3,48,128]{3,2,1,0:T(8,128)S(1)} %copy-done.2), channel_id=1, source_target_pairs={{0,3},{1,0},{2,1},{3,2},{4,7},{5,4},{6,5},{7,6},{8,11},{9,8},{10,9... | collective-permute-start | bytes 1769480 | tf_op jit(solution)/shard_map/ppermute | solution.py:75
  65.9 12.7 %copy-start.1 = (f32[8,3,48,128]{3,2,1,0:T(8,128)S(1)}, f32[8,3,48,128]{3,2,1,0:T(8,128)}, u32[]{:S(2)}) copy-start(f32[8,3,48,128]{3,2,1,0:T(8,128)} %get-tuple-element.29) | copy-start | bytes 1769476
  78.8 8.0 %collective-permute-start.7 = (f32[2,6,48,128]{3,2,1,0:T(8,128)S(1)}, f32[2,6,48,128]{3,2,1,0:T(8,128)S(1)}, u32[]{:S(2)}, u32[]{:S(2)}) collective-permute-start(f32[2,6,48,128]{3,2,1,0:T(8,128)S(1)} %get-tuple-element.41), channel_id=1, source_target_pairs={{0,4},{1,5},{2,6},{3,7},{4,8},{5,9},{6,10},{7,11},{8,12},{9,13},{1... | collective-permute-start | bytes 884744 | tf_op jit(solution)/shard_map/ppermute | solution.py:75
  80.3 9.2 %collective-permute-start.9 = (f32[2,6,48,128]{3,2,1,0:T(8,128)S(1)}, f32[2,6,48,128]{3,2,1,0:T(8,128)S(1)}, u32[]{:S(2)}, u32[]{:S(2)}) collective-permute-start(f32[2,6,48,128]{3,2,1,0:T(8,128)S(1)} %get-tuple-element.42), channel_id=1, source_target_pairs={{0,12},{1,13},{2,14},{3,15},{4,0},{5,1},{6,2},{7,3},{8,4},{9,5},{1... | collective-permute-start | bytes 884744 | tf_op jit(solution)/shard_map/ppermute | solution.py:75
  82.1 8.4 %collective-permute-start.8 = (f32[2,6,48,128]{3,2,1,0:T(8,128)S(1)}, f32[2,6,48,128]{3,2,1,0:T(8,128)S(1)}, u32[]{:S(2)}, u32[]{:S(2)}) collective-permute-start(f32[2,6,48,128]{3,2,1,0:T(8,128)S(1)} %get-tuple-element.43), channel_id=1, source_target_pairs={{0,8},{1,9},{2,10},{3,11},{4,12},{5,13},{6,14},{7,15},{8,0},{9,1},... | collective-permute-start | bytes 884744 | tf_op jit(solution)/shard_map/ppermute | solution.py:75
  90.7 6.8 %collective-permute-start.10 = (f32[296,128]{1,0:T(8,128)S(1)}, f32[296,128]{1,0:T(8,128)S(1)}, u32[]{:S(2)}, u32[]{:S(2)}) collective-permute-start(f32[296,128]{1,0:T(8,128)S(1)} %get-tuple-element.44), channel_id=1, source_target_pairs={{0,64},{1,65},{2,66},{3,67},{4,68},{5,69},{6,70},{7,71},{8,72},{9,... | collective-permute-start | bytes 454664 | tf_op jit(solution)/shard_map/ppermute | solution.py:75
  93.5 5.6 %collective-permute-start.12 = (f32[296,128]{1,0:T(8,128)S(1)}, f32[296,128]{1,0:T(8,128)S(1)}, u32[]{:S(2)}, u32[]{:S(2)}) collective-permute-start(f32[296,128]{1,0:T(8,128)S(1)} %get-tuple-element.45), channel_id=1, source_target_pairs={{0,80},{1,81},{2,82},{3,83},{4,84},{5,85},{6,86},{7,87},{8,88},{9,... | collective-permute-start | bytes 454664 | tf_op jit(solution)/shard_map/ppermute | solution.py:75
  94.8 6.4 %collective-permute-start.11 = (f32[296,128]{1,0:T(8,128)S(1)}, f32[296,128]{1,0:T(8,128)S(1)}, u32[]{:S(2)}, u32[]{:S(2)}) collective-permute-start(f32[296,128]{1,0:T(8,128)S(1)} %get-tuple-element.45), channel_id=1, source_target_pairs={{0,16},{1,17},{2,18},{3,19},{4,20},{5,21},{6,22},{7,23},{8,24},{9,... | collective-permute-start | bytes 454664 | tf_op jit(solution)/shard_map/ppermute | solution.py:75
  101.3 8.9 %collective-permute-start.14 = (f32[192,128]{1,0:T(8,128)S(1)}, f32[192,128]{1,0:T(8,128)S(1)}, u32[]{:S(2)}, u32[]{:S(2)}) collective-permute-start(f32[192,128]{1,0:T(8,128)S(1)} %pad_maximum_fusion.5), channel_id=1, source_target_pairs={{0,1},{1,2},{2,3},{3,4},{4,5},{5,6},{6,7},{7,8},{8,9},{9,10},{10,1... | collective-permute-start | bytes 294920 | tf_op jit(solution)/shard_map/ppermute | solution.py:75
  102.3 8.6 %collective-permute-start.13 = (f32[96,128]{1,0:T(8,128)S(1)}, f32[96,128]{1,0:T(8,128)S(1)}, u32[]{:S(2)}, u32[]{:S(2)}) collective-permute-start(f32[96,128]{1,0:T(8,128)S(1)} %slice_select_fusion), channel_id=1, source_target_pairs={{0,2},{1,3},{2,4},{3,5},{4,6},{5,7},{6,8},{7,9},{8,10},{9,11},{10,... | collective-permute-start | bytes 147464 | tf_op jit(solution)/shard_map/ppermute | solution.py:75
  110.9 6.7 %collective-permute-start.15 = (f32[288,128]{1,0:T(8,128)S(1)}, f32[288,128]{1,0:T(8,128)S(1)}, u32[]{:S(2)}, u32[]{:S(2)}) collective-permute-start(f32[288,128]{1,0:T(8,128)S(1)} %pad_maximum_fusion.4), channel_id=1, source_target_pairs={{0,64},{1,65},{2,66},{3,67},{4,68},{5,69},{6,70},{7,71},{8,72},{9,... | collective-permute-start | bytes 442376 | tf_op jit(solution)/shard_map/ppermute | solution.py:75
  117.7 2.1 %collective-permute-start.16 = (f32[872,128]{1,0:T(8,128)S(1)}, f32[872,128]{1,0:T(8,128)S(1)}, u32[]{:S(2)}, u32[]{:S(2)}) collective-permute-start(f32[872,128]{1,0:T(8,128)S(1)} %pad_maximum_fusion), channel_id=1, source_target_pairs={{0,32},{1,33},{2,34},{3,35},{4,36},{5,37},{6,38},{7,39},{8,40},{9,... | collective-permute-start | bytes 1339400 | tf_op jit(solution)/shard_map/ppermute | solution.py:75
  117.8 2.0 %collective-permute-start.17 = (bf16[15,48,128]{2,1,0:T(8,128)(2,1)S(1)}, bf16[15,48,128]{2,1,0:T(8,128)(2,1)S(1)}, u32[]{:S(2)}, u32[]{:S(2)}) collective-permute-start(bf16[15,48,128]{2,1,0:T(8,128)(2,1)S(1)} %convert_element_type.3), channel_id=1, source_target_pairs={{0,32},{1,33},{2,34},{3,35},{4,36},{5,37},{6,38},{7,39},{8,40},{9,... | collective-permute-start | bytes 552968 | tf_op jit(solution)/shard_map/ppermute | solution.py:75

commit v6 on v5

--- a/solution.py
+++ b/solution.py
@@ -86,10 +86,9 @@
 
 
 TOP = 16
-MOVING_CHUNK = 4
-FACTOR_CHUNK = 2
-MOVING_PAGES = NZ + 2 * MOVING_CHUNK
-FACTOR_PAGES = NZ + 6
+CHUNK = 4
+STEPS = NZ // (2 * CHUNK)
+PAGES = NZ + 2 * CHUNK
 FIRST_ORDER = 1.0 / 27.0
 
 
@@ -115,66 +114,69 @@
     return ref[pl.ds(base, chunk)].reshape(chunk * WIN, NY)
 
 
-def triple_sums(makers, scales, shift, even, odd, three, ring, enter, begin, emit, end):
+def triple_sums(makers, scales, shift, even, odd, three, last, enter, emit, leave):
     band1, band2 = bands()
-    volumes, chunk = three.shape[:2]
-    slots = ring.shape[1]
-    even[...] = jnp.zeros(even.shape, F32)
-    odd[...] = jnp.zeros(odd.shape, F32)
-    ring[...] = jnp.zeros(ring.shape, F32)
-
-    def along_y(thunk, v, line):
-        sums = thunk(band1, band2)
-        for j in range(chunk):
-            line[v, j, pl.ds(TOP, WIN), :] = sums[j * WIN : (j + 1) * WIN]
-
-    def along_x(v, line, base):
-        for j in range(chunk):
-            three[v, j] = (
-                line[v, j, pl.ds(TOP - 9 + shift, 64), :]
-                + line[v, j, pl.ds(TOP - 8 + shift, 64), :]
-                + line[v, j, pl.ds(TOP - 7 + shift, 64), :]
+    volumes = len(three)
+    first = [v for v in range(volumes) if scales[v] is not None]
+    second = [v for v in range(volumes) if scales[v] is None]
+    for v in range(volumes):
+        for ref in (even[v], odd[v], last[v]):
+            ref[...] = jnp.zeros(ref.shape, F32)
+
+    def along_y(lhs, line):
+        size = CHUNK * WIN
+        for members, band in ((first, band1), (second, band2)):
+            sums = dot(jnp.concatenate([lhs[v]() for v in members], axis=0), band)
+            for m, v in enumerate(members):
+                for j in range(CHUNK):
+                    at = m * size + j * WIN
+                    line[v][j, pl.ds(TOP, WIN), :] = sums[at : at + WIN]
+
+    def triples(v, n, q, rows, pages):
+        before, here = last[v][0, rows, :], last[v][1, rows, :]
+        left, right = here + pages[0], pages[1] + pages[2]
+        sums = (before + left, left + pages[1], pages[0] + right, right + pages[3])
+        for j in range(CHUNK):
+            emit(v, n, q + j, rows, sums[j] * scales[v] if scales[v] is not None else sums[j])
+        last[v][0, rows, :] = pages[2]
+        last[v][1, rows, :] = pages[3]
+
+    def along_x(v, line, n, q):
+        for j in range(CHUNK):
+            three[v][j] = (
+                line[v][j, pl.ds(TOP - 9 + shift, 64), :]
+                + line[v][j, pl.ds(TOP - 8 + shift, 64), :]
+                + line[v][j, pl.ds(TOP - 7 + shift, 64), :]
             )
-        for j in range(chunk):
-            ring[v, (base + j) & (slots - 1)] = (
-                three[v, j, pl.ds(5, OWN), :]
-                + three[v, j, pl.ds(8, OWN), :]
-                + three[v, j, pl.ds(11, OWN), :]
-            )
-
-    def both(i, line, other):
-        thunks = makers(i * chunk)
-        for v in range(volumes):
-            along_y(thunks[v], v, line)
-            along_x(v, other, (i - 1) * chunk)
-
-    def along_z(n):
-        begin(n)
-        for v in range(volumes):
-            for q in range(2 * chunk):
-                z = 2 * chunk * n - chunk - 1 + q
-                page = (
-                    ring[v, (z - 1) & (slots - 1)]
-                    + ring[v, z & (slots - 1)]
-                    + ring[v, (z + 1) & (slots - 1)]
-                )
-                emit(v, n, q, page * scales[v] if scales[v] is not None else page)
-        end(n)
+        for r in range(OWN // 8):
+            pages = [
+                three[v][j, pl.ds(5 + 8 * r, 8), :]
+                + three[v][j, pl.ds(8 + 8 * r, 8), :]
+                + three[v][j, pl.ds(11 + 8 * r, 8), :]
+                for j in range(CHUNK)
+            ]
+            triples(v, n, q, pl.ds(8 * r, 8), pages)
 
     def step(n, carry):
         enter(n)
-        both(2 * n, even, odd)
-        both(2 * n + 1, odd, even)
-        along_z(n)
+        along_y(makers(2 * n * CHUNK), even)
+        for v in range(volumes):
+            along_x(v, odd, n, 0)
+        along_y(makers((2 * n + 1) * CHUNK), odd)
+        for v in range(volumes):
+            along_x(v, even, n, CHUNK)
+        leave(n)
         return carry
 
-    steps = NZ // (2 * chunk)
-    lax.fori_loop(0, steps, step, 0)
+    lax.fori_loop(0, STEPS, step, 0)
+    n = jnp.int32(STEPS)
+    enter(n)
+    zeros = jnp.zeros((8, NY), F32)
     for v in range(volumes):
-        along_x(v, odd, NZ - chunk)
-        for j in range(chunk):
-            ring[v, (NZ + j) & (slots - 1)] = jnp.zeros((OWN, NY), F32)
-    along_z(jnp.int32(steps))
+        along_x(v, odd, n, 0)
+        for r in range(OWN // 8):
+            triples(v, n, CHUNK, pl.ds(8 * r, 8), [zeros] * CHUNK)
+    leave(n)
 
 
 PARTS = 4
@@ -194,10 +196,10 @@
     ]
 
 
-def wait_part(fetches, n, steps):
+def wait_part(fetches, n):
     for p in range(PARTS):
 
-        @pl.when(n == p * (steps // PARTS))
+        @pl.when(n == p * (STEPS // PARTS))
         def _():
             for fetch in fetches[p]:
                 fetch.wait()
@@ -209,32 +211,31 @@
 
 def moving_kernel(
     idx, ja_hbm, jb_hbm, out_ref, o0, o1, o2, o3,
-    ja_ref, jb_ref, pair, even, odd, three, ring, ready, sem, in_sem, pair_sem,
+    ja_ref, jb_ref, pair, even, odd, three, last, ready, sem, in_sem, pair_sem,
 ):
     shift = pl.multiple_of(idx[0] * 8, 8)
-    length = 2 * MOVING_CHUNK
-    steps = NZ // length
+    length = 2 * CHUNK
     fetches = window_fetches(idx[0], ((ja_hbm, ja_ref), (jb_hbm, jb_ref)), in_sem)
     for part in fetches:
         for fetch in part:
             fetch.start()
 
     def makers(base):
-        def square(ref, b2):
-            f = load(ref, base, MOVING_CHUNK).astype(F32)
-            return dot(split(f * f), b2)
-
-        def first(b1, b2):
-            fa = load(ja_ref, base, MOVING_CHUNK).astype(F32)
-            fb = load(jb_ref, base, MOVING_CHUNK).astype(F32)
-            pair[pl.ds(base, MOVING_CHUNK)] = (fa + fb).reshape(MOVING_CHUNK, WIN, NY)
-            return dot(load(ja_ref, base, MOVING_CHUNK), b1)
+        def square(ref):
+            f = load(ref, base, CHUNK).astype(F32)
+            return split(f * f)
+
+        def add():
+            fa = load(ja_ref, base, CHUNK).astype(F32)
+            fb = load(jb_ref, base, CHUNK).astype(F32)
+            pair[pl.ds(base, CHUNK)] = (fa + fb).reshape(CHUNK, WIN, NY)
+            return load(ja_ref, base, CHUNK)
 
         return [
-            first,
-            lambda b1, b2: square(ja_ref, b2),
-            lambda b1, b2: dot(load(jb_ref, base, MOVING_CHUNK), b1),
-            lambda b1, b2: square(jb_ref, b2),
+            add,
+            lambda: square(ja_ref),
+            lambda: load(jb_ref, base, CHUNK),
+            lambda: square(jb_ref),
         ]
 
     def copy(n):
@@ -243,17 +244,19 @@
             ready.at[slot], out_ref.at[:, pl.ds(n * length, length)], sem.at[slot]
         )
 
-    def begin(n):
+    def enter(n):
+        wait_part(fetches, n)
+
         @pl.when(n >= 2)
         def _():
             copy(n - 2).wait()
 
-    def emit(v, n, q, page):
-        ready[n & 1, v, q] = page
+    def emit(v, n, q, rows, x):
+        ready[n & 1, v, q, rows, :] = x
 
     triple_sums(
-        makers, (FIRST_ORDER, None) * 2, shift, even, odd, three, ring,
-        lambda n: wait_part(fetches, n, steps), begin, emit, lambda n: copy(n).start(),
+        makers, (FIRST_ORDER, None) * 2, shift, even, odd, three, last,
+        enter, emit, lambda n: copy(n).start(),
     )
     outs = []
     for kb, out in enumerate((o0, o1, o2, o3)):
@@ -266,9 +269,8 @@
             )
     for out in outs:
         out.start()
-    last = jnp.int32(steps)
-    copy(last - 1).wait()
-    copy(last).wait()
+    copy(jnp.int32(STEPS - 1)).wait()
+    copy(jnp.int32(STEPS)).wait()
     for out in outs:
         out.wait()
 
@@ -277,7 +279,7 @@
     hbm = pl.BlockSpec(memory_space=pltpu.HBM)
     return pl.pallas_call(
         moving_kernel,
-        out_shape=[pltpu.HBM((4, MOVING_PAGES, OWN, NY), F32)]
+        out_shape=[pltpu.HBM((4, PAGES, OWN, NY), F32)]
         + [pltpu.HBM((8, 3, OWN, NY), F32)] * 4,
         in_specs=[pl.BlockSpec(memory_space=pltpu.SMEM), hbm, hbm],
         out_specs=[hbm] * 5,
@@ -285,11 +287,11 @@
             pltpu.VMEM((NZ, WIN, NY), BF16),
             pltpu.VMEM((NZ, WIN, NY), BF16),
             pltpu.VMEM((NZ, WIN, NY), F32),
-            pltpu.VMEM((4, MOVING_CHUNK, 88, NY), F32),
-            pltpu.VMEM((4, MOVING_CHUNK, 88, NY), F32),
-            pltpu.VMEM((4, MOVING_CHUNK, 64, NY), F32),
-            pltpu.VMEM((4, 4 * MOVING_CHUNK, OWN, NY), F32),
-            pltpu.VMEM((2, 4, 2 * MOVING_CHUNK, OWN, NY), F32),
+            [pltpu.VMEM((CHUNK, 88, NY), F32)] * 4,
+            [pltpu.VMEM((CHUNK, 88, NY), F32)] * 4,
+            [pltpu.VMEM((CHUNK, 64, NY), F32)] * 4,
+            [pltpu.VMEM((2, OWN, NY), F32)] * 4,
+            pltpu.VMEM((2, 4, 2 * CHUNK, OWN, NY), F32),
             pltpu.SemaphoreType.DMA((2,)),
             pltpu.SemaphoreType.DMA((2, PARTS)),
             pltpu.SemaphoreType.DMA((32,)),
@@ -302,7 +304,7 @@
 
 def factor_kernel(
     idx, i_hbm, ja_hbm, jb_hbm, jplane_ref, o0, o1, o2, o3, cc_ref, iext_ref,
-    i_ref, ja_ref, jb_ref, raw, even, odd, three, ring, iplane, jplane, sem, in_sem, i_sem,
+    i_ref, ja_ref, jb_ref, raw, even, odd, three, last, iplane, jplane, sem, in_sem, i_sem,
 ):
     shift = pl.multiple_of(idx[0] * 8, 8)
     fetches = window_fetches(idx[0], ((ja_hbm, ja_ref), (jb_hbm, jb_ref)), in_sem)
@@ -313,36 +315,31 @@
             fetch.start()
     fetch = pltpu.make_async_copy(jplane_ref, jplane, sem)
     fetch.start()
-    for v in range(4):
-        for z in (NZ + 1, NZ + 2):
-            iplane[v, z + 3] = jnp.zeros((OWN, NY), F32)
 
     def makers(base):
         def wide(n, keep):
-            f = load((i_ref, ja_ref, jb_ref)[n], base, FACTOR_CHUNK).astype(F32)
+            f = load((i_ref, ja_ref, jb_ref)[n], base, CHUNK).astype(F32)
             if keep:
-                raw[n, pl.ds(base, FACTOR_CHUNK)] = f.reshape(FACTOR_CHUNK, WIN, NY)
+                raw[n, pl.ds(base, CHUNK)] = f.reshape(CHUNK, WIN, NY)
             return f
 
-        def square(b1, b2):
+        def square():
             f = wide(0, True)
-            return dot(split(f * f), b2)
+            return split(f * f)
 
         return [
-            lambda b1, b2: dot(load(i_ref, base, FACTOR_CHUNK), b1),
+            lambda: load(i_ref, base, CHUNK),
             square,
-            lambda b1, b2: dot(split(wide(0, False) * wide(1, True)), b2),
-            lambda b1, b2: dot(split(wide(0, False) * wide(2, True)), b2),
+            lambda: split(wide(0, False) * wide(1, True)),
+            lambda: split(wide(0, False) * wide(2, True)),
         ]
 
-    def emit(v, n, q, page):
-        iplane[v, 2 * FACTOR_CHUNK * n + q] = page
-
-    nothing = lambda n: None
-    steps = NZ // (2 * FACTOR_CHUNK)
+    def emit(v, n, q, rows, x):
+        iplane[v, 2 * CHUNK * n + q, rows, :] = x
+
     triple_sums(
-        makers, (FIRST_ORDER, None, None, None), shift, even, odd, three, ring,
-        lambda n: wait_part(fetches, n, steps), nothing, emit, nothing,
+        makers, (FIRST_ORDER, None, None, None), shift, even, odd, three, last,
+        lambda n: wait_part(fetches, n), emit, lambda n: None,
     )
     fetch.wait()
 
@@ -355,12 +352,12 @@
         for r in range(OWN // 8):
             part = pl.ds(r * 8, 8)
 
-            def boxes(ref, v, at):
-                pages = [ref[v, first + at + p, part, :] for p in range(9)]
+            def boxes(ref, v):
+                pages = [ref[v, first + 2 + p, part, :] for p in range(9)]
                 return [pages[j] + pages[j + 3] + pages[j + 6] for j in range(3)]
 
             own = pl.ds(shift + r * 8, 8)
-            si, sii = boxes(iplane, 0, 0), boxes(iplane, 1, 0)
+            si, sii = boxes(iplane, 0), boxes(iplane, 1)
             var_i = [sii[j] - si[j] * si[j] for j in range(3)]
             slope = [
                 (raw[0, first + j, own, :] - si[j] * FIRST_ORDER) / (var_i[j] + eps_b)
@@ -368,8 +365,8 @@
             ]
             total = [None] * 3
             for n in range(2):
-                sj, sjj = boxes(jplane, 2 * n, 2), boxes(jplane, 2 * n + 1, 2)
-                sij = boxes(iplane, 2 + n, 0)
+                sj, sjj = boxes(jplane, 2 * n), boxes(jplane, 2 * n + 1)
+                sij = boxes(iplane, 2 + n)
                 for j in range(3):
                     var_j = sjj[j] - sj[j] * sj[j]
                     cross = sij[j] - si[j] * sj[j]
@@ -409,12 +406,12 @@
             pltpu.VMEM((NZ, WIN, NY), BF16),
             pltpu.VMEM((NZ, WIN, NY), BF16),
             pltpu.VMEM((3, NZ, WIN, NY), F32),
-            pltpu.VMEM((4, FACTOR_CHUNK, 88, NY), F32),
-            pltpu.VMEM((4, FACTOR_CHUNK, 88, NY), F32),
-            pltpu.VMEM((4, FACTOR_CHUNK, 64, NY), F32),
-            pltpu.VMEM((4, 4 * FACTOR_CHUNK, OWN, NY), F32),
-            pltpu.VMEM((4, FACTOR_PAGES, OWN, NY), F32),
-            pltpu.VMEM((4, MOVING_PAGES, OWN, NY), F32),
+            [pltpu.VMEM((CHUNK, 88, NY), F32)] * 4,
+            [pltpu.VMEM((CHUNK, 88, NY), F32)] * 4,
+            [pltpu.VMEM((CHUNK, 64, NY), F32)] * 4,
+            [pltpu.VMEM((2, OWN, NY), F32)] * 4,
+            pltpu.VMEM((4, PAGES, OWN, NY), F32),
+            pltpu.VMEM((4, PAGES, OWN, NY), F32),
             pltpu.SemaphoreType.DMA,
             pltpu.SemaphoreType.DMA((2, PARTS)),
             pltpu.SemaphoreType.DMA((PARTS,)),

time: 138 us -> 135 us (0.978)
  waiting for transfers between devices: 56.3 us -> 54.4 us
    pallas_call x1, Pallas kernels: 15.7 us -> 13 us  [factors(): pl.pallas_call(factor_kernel, out_shape=[block] * 4 + [jax.ShapeDtypeStru...]
    all_to_all x1, waiting for transfers between devices: 9.2 us -> 7.28 us  [step(): image = lax.all_to_all(copies, 'sub', 0, 0, tiled=True).reshape(NZ, WIN, NY)]
    pallas_call x1, Pallas kernels: 10.3 us -> 12.2 us  [moving_planes(): pl.pallas_call(moving_kernel, out_shape=[pltpu.HBM((4, PAGES, OWN, NY), F...]
  transfers between devices with their start and end apart: 19 -> 19, of which waited for: 17 -> 17; matrix products, arithmetic and copies ran while one was open for 1% -> 1% of each run, Pallas kernels for 8% -> 9%
where the time goes in v6:
time: 135 us; the launch traced here: 134 us
  waiting for transfers between devices  54.4 us (40%)
  starting transfers between devices  33.9 us (25%)
  Pallas kernels  28.9 us (21%)
  blocking collectives  13.2 us (10%)
  local copies, waits for them, and re-layouts  2.18 us (2%)
    ppermute x18, waiting for transfers between devices, permute(): return lax.ppermute(x, BOTH, table)  47.1 us
    ppermute x18, starting transfers between devices, permute(): return lax.ppermute(x, BOTH, table)  24.5 us
    all_to_all x1, blocking collectives, step(): lax.all_to_all(jnp.broadcast_to(stats[None], (32, 1, NY)), 'sub', 0, 0, t...  13.2 us
    pallas_call x1, Pallas kernels, factors(): pl.pallas_call(factor_kernel, out_shape=[block] * 4 + [jax.ShapeDtypeStru...  13 us
    pallas_call x1, Pallas kernels, moving_planes(): pl.pallas_call(moving_kernel, out_shape=[pltpu.HBM((4, PAGES, OWN, NY), F...  12.2 us
    all_to_all x1, starting transfers between devices, step(): image = lax.all_to_all(copies, 'sub', 0, 0, tiled=True).reshape(NZ, WIN, NY)  9.37 us
    all_to_all x1, waiting for transfers between devices, step(): image = lax.all_to_all(copies, 'sub', 0, 0, tiled=True).reshape(NZ, WIN, NY)  7.28 us
    pallas_call x1, Pallas kernels, smooth_slab(): pl.pallas_call(smooth_kernel, out_shape=[jax.ShapeDtypeStruct((3, 3, NX,...  2.73 us
  transfers between devices with their start and end apart: 19, of which 17 were waited for; matrix products, arithmetic and copies ran while one was open for 1% of the time, Pallas kernels for 9%

profile of v6, /device:TPU:0, one launch (start us, length us, event | category | flops | bytes accessed | tf_op | source)
XLA Modules:
  0.0 134.1 jit_solution(11233622915196506841)
XLA Ops:
  0.6 0.0 copy-start
  0.6 0.1 collective-permute-start
  0.8 0.8 copy-done
  1.5 1.3 broadcast_in_dim.8
  2.8 9.4 %all-to-all-start = ((bf16[32,3,56,128]{3,2,1,0:T(8,128)(2,1)}), bf16[32,3,56,128]{3,2,1,0:T(8,128)(2,1)S(1)}, u32[]{:S(2)}, u32[]{:S(2)}) async-start(bf16[32,3,56,128]{3,2,1,0:T(8,128)(2,1)} %broadcast_in_dim.8), calls=%async_computation | async-start | bytes 2752512 | tf_op jit(solution)/shard_map/all_to_all | solution.py:617
  12.2 0.1 stack.27.idx
  12.3 0.0 collective-permute-done.jb_hbm
  12.3 12.2 %moving_planes.1 = (f32[4,104,48,128]{3,2,1,0:T(8,128)}, f32[8,3,48,128]{3,2,1,0:T(8,128)}, f32[8,3,48,128]{3,2,1,0:T(8,128)}, f32[8,3,48,128]{3,2,1,0:T(8,128)}, f32[8,3,48,128]{3,2,1,0:T(8,128)}) custom-call(s32[6]{0:T(128)S(1)} %stack.27.idx, bf16[96,96,128]{2,1,0:T(8,128)(2,1)} %bitcast.24, bf16[96,96,128]{2,1,0:T(8,128)(2,1)} %collective-permute-done.jb_hbm), custom_call_target="tpu_custom_call" | custom-call | flops 4000000000 | bytes 17000000 | tf_op jit(solution)/shard_map/moving_planes/pallas_call | solution.py:280
  24.6 7.3 %all-to-all-done = bf16[32,3,56,128]{3,2,1,0:T(8,128)(2,1)S(1)} async-done(((bf16[32,3,56,128]{3,2,1,0:T(8,128)(2,1)}), bf16[32,3,56,128]{3,2,1,0:T(8,128)(2,1)S(1)}, u32[]{:S(2)}, u32[]{:S(2)}) %all-to-all-start) | async-done | bytes 1376288 | tf_op jit(solution)/shard_map/all_to_all | solution.py:617
  31.9 0.0 copy-start.4
  31.9 0.0 copy-start.3
  31.9 0.0 copy-start.2
  31.9 13.0 %factors.1 = (f32[8,3,48,128]{3,2,1,0:T(8,128)S(1)}, f32[8,3,48,128]{3,2,1,0:T(8,128)S(1)}, f32[8,3,48,128]{3,2,1,0:T(8,128)S(1)}, f32[8,3,48,128]{3,2,1,0:T(8,1...) custom-call(s32[6]{0:T(128)S(1)} %stack.27.idx, bf16[96,56,128]{2,1,0:T(8,128)(2,1)S(1)} %bitcast.18, ...), custom_call_target="tpu_custom_call" | custom-call | flops 4000000000 | bytes 18000000 | tf_op jit(solution)/shard_map/factors/pallas_call | solution.py:398
  44.9 1.5 %collective-permute-start.1 = (f32[8,3,48,128]{3,2,1,0:T(8,128)S(1)}, f32[8,3,48,128]{3,2,1,0:T(8,128)S(1)}, u32[]{:S(2)}, u32[]{:S(2)}) collective-permute-start(f32[8,3,48,128]{3,2,1,0:T(8,128)S(1)} %get-tuple-element.24), channel_id=1, source_target_pairs={{0,1},{1,2},{2,3},{3,0},{4,5},{5,6},{6,7},{7,4},{8,9},{9,10},{10,1... | collective-permute-start | bytes 1769480 | tf_op jit(solution)/shard_map/ppermute | solution.py:75
  46.4 2.0 %collective-permute-start.2 = (f32[8,3,48,128]{3,2,1,0:T(8,128)S(1)}, f32[8,3,48,128]{3,2,1,0:T(8,128)S(1)}, u32[]{:S(2)}, u32[]{:S(2)}) collective-permute-start(f32[8,3,48,128]{3,2,1,0:T(8,128)S(1)} %get-tuple-element.25), channel_id=1, source_target_pairs={{0,2},{1,3},{2,0},{3,1},{4,6},{5,7},{6,4},{7,5},{8,10},{9,11},{10,... | collective-permute-start | bytes 1769480 | tf_op jit(solution)/shard_map/ppermute | solution.py:75
  48.4 1.8 %collective-permute-start.3 = (f32[8,3,48,128]{3,2,1,0:T(8,128)S(1)}, f32[8,3,48,128]{3,2,1,0:T(8,128)S(1)}, u32[]{:S(2)}, u32[]{:S(2)}) collective-permute-start(f32[8,3,48,128]{3,2,1,0:T(8,128)S(1)} %get-tuple-element.26), channel_id=1, source_target_pairs={{0,3},{1,0},{2,1},{3,2},{4,7},{5,4},{6,5},{7,6},{8,11},{9,8},{10,9... | collective-permute-start | bytes 1769480 | tf_op jit(solution)/shard_map/ppermute | solution.py:75
  50.2 0.0 copy-done.4
  50.2 0.2 collective-permute-start.4
  50.5 0.0 copy-done.3
  50.5 1.5 %collective-permute-start.5 = (f32[8,3,48,128]{3,2,1,0:T(8,128)S(1)}, f32[8,3,48,128]{3,2,1,0:T(8,128)S(1)}, u32[]{:S(2)}, u32[]{:S(2)}) collective-permute-start(f32[8,3,48,128]{3,2,1,0:T(8,128)S(1)} %copy-done.3), channel_id=1, source_target_pairs={{0,2},{1,3},{2,0},{3,1},{4,6},{5,7},{6,4},{7,5},{8,10},{9,11},{10,... | collective-permute-start | bytes 1769480 | tf_op jit(solution)/shard_map/ppermute | solution.py:75
  52.0 4.1 %collective-permute-done.1 = f32[8,3,48,128]{3,2,1,0:T(8,128)S(1)} collective-permute-done((f32[8,3,48,128]{3,2,1,0:T(8,128)S(1)}, f32[8,3,48,128]{3,2,1,0:T(8,128)S(1)}, u32[]{:S(2)}, u32[]{:S(2)}) %collective-permute-start.1) | collective-permute-done | bytes 589856 | tf_op jit(solution)/shard_map/ppermute | solution.py:75
  56.1 0.0 copy-done.2
  56.1 0.8 collective-permute-start.6
  56.9 5.9 %collective-permute-done.2 = f32[8,3,48,128]{3,2,1,0:T(8,128)S(1)} collective-permute-done((f32[8,3,48,128]{3,2,1,0:T(8,128)S(1)}, f32[8,3,48,128]{3,2,1,0:T(8,128)S(1)}, u32[]{:S(2)}, u32[]{:S(2)}) %collective-permute-start.2) | collective-permute-done | bytes 589856 | tf_op jit(solution)/shard_map/ppermute | solution.py:75
  62.7 0.6 collective-permute-done.3
  63.3 0.0 copy-start.1
  63.3 0.1 add_add_fusion.1
  63.5 5.3 %collective-permute-done.4 = f32[8,3,48,128]{3,2,1,0:T(8,128)S(1)} collective-permute-done((f32[8,3,48,128]{3,2,1,0:T(8,128)S(1)}, f32[8,3,48,128]{3,2,1,0:T(8,128)S(1)}, u32[]{:S(2)}, u32[]{:S(2)}) %collective-permute-start.4) | collective-permute-done | bytes 589856 | tf_op jit(solution)/shard_map/ppermute | solution.py:75
  68.7 6.6 %collective-permute-done.5 = f32[8,3,48,128]{3,2,1,0:T(8,128)S(1)} collective-permute-done((f32[8,3,48,128]{3,2,1,0:T(8,128)S(1)}, f32[8,3,48,128]{3,2,1,0:T(8,128)S(1)}, u32[]{:S(2)}, u32[]{:S(2)}) %collective-permute-start.5) | collective-permute-done | bytes 589856 | tf_op jit(solution)/shard_map/ppermute | solution.py:75
  75.3 0.7 collective-permute-done.6
  76.0 0.0 copy-done.1
  76.0 0.1 add_add_fusion
  76.1 0.1 fusion.5
  76.2 1.5 %collective-permute-start.7 = (f32[2,6,48,128]{3,2,1,0:T(8,128)S(1)}, f32[2,6,48,128]{3,2,1,0:T(8,128)S(1)}, u32[]{:S(2)}, u32[]{:S(2)}) collective-permute-start(f32[2,6,48,128]{3,2,1,0:T(8,128)S(1)} %get-tuple-element.41), channel_id=1, source_target_pairs={{0,4},{1,5},{2,6},{3,7},{4,8},{5,9},{6,10},{7,11},{8,12},{9,13},{1... | collective-permute-start | bytes 884744 | tf_op jit(solution)/shard_map/ppermute | solution.py:75
  77.7 1.8 %collective-permute-start.9 = (f32[2,6,48,128]{3,2,1,0:T(8,128)S(1)}, f32[2,6,48,128]{3,2,1,0:T(8,128)S(1)}, u32[]{:S(2)}, u32[]{:S(2)}) collective-permute-start(f32[2,6,48,128]{3,2,1,0:T(8,128)S(1)} %get-tuple-element.42), channel_id=1, source_target_pairs={{0,12},{1,13},{2,14},{3,15},{4,0},{5,1},{6,2},{7,3},{8,4},{9,5},{1... | collective-permute-start | bytes 884744 | tf_op jit(solution)/shard_map/ppermute | solution.py:75
  79.5 1.2 collective-permute-start.8
  80.7 3.5 %collective-permute-done.7 = f32[2,6,48,128]{3,2,1,0:T(8,128)S(1)} collective-permute-done((f32[2,6,48,128]{3,2,1,0:T(8,128)S(1)}, f32[2,6,48,128]{3,2,1,0:T(8,128)S(1)}, u32[]{:S(2)}, u32[]{:S(2)}) %collective-permute-start.7) | collective-permute-done | bytes 294944 | tf_op jit(solution)/shard_map/ppermute | solution.py:75
  84.2 2.7 %collective-permute-done.9 = f32[2,6,48,128]{3,2,1,0:T(8,128)S(1)} collective-permute-done((f32[2,6,48,128]{3,2,1,0:T(8,128)S(1)}, f32[2,6,48,128]{3,2,1,0:T(8,128)S(1)}, u32[]{:S(2)}, u32[]{:S(2)}) %collective-permute-start.9) | collective-permute-done | bytes 294944 | tf_op jit(solution)/shard_map/ppermute | solution.py:75
  86.9 1.0 collective-permute-done.8
  87.9 0.1 fusion.4
  88.0 2.8 %collective-permute-start.10 = (f32[296,128]{1,0:T(8,128)S(1)}, f32[296,128]{1,0:T(8,128)S(1)}, u32[]{:S(2)}, u32[]{:S(2)}) collective-permute-start(f32[296,128]{1,0:T(8,128)S(1)} %get-tuple-element.44), channel_id=1, source_target_pairs={{0,64},{1,65},{2,66},{3,67},{4,68},{5,69},{6,70},{7,71},{8,72},{9,... | collective-permute-start | bytes 454664 | tf_op jit(solution)/shard_map/ppermute | solution.py:75
  90.8 1.3 collective-permute-start.12
  92.1 0.7 collective-permute-start.11
  92.8 1.9 %collective-permute-done.10 = f32[296,128]{1,0:T(8,128)S(1)} collective-permute-done((f32[296,128]{1,0:T(8,128)S(1)}, f32[296,128]{1,0:T(8,128)S(1)}, u32[]{:S(2)}, u32[]{:S(2)}) %collective-permute-start.10) | collective-permute-done | bytes 151584 | tf_op jit(solution)/shard_map/ppermute | solution.py:75
  94.8 1.6 %collective-permute-done.12 = f32[296,128]{1,0:T(8,128)S(1)} collective-permute-done((f32[296,128]{1,0:T(8,128)S(1)}, f32[296,128]{1,0:T(8,128)S(1)}, u32[]{:S(2)}, u32[]{:S(2)}) %collective-permute-start.12) | collective-permute-done | bytes 151584 | tf_op jit(solution)/shard_map/ppermute | solution.py:75
  96.4 2.2 %collective-permute-done.11 = f32[296,128]{1,0:T(8,128)S(1)} collective-permute-done((f32[296,128]{1,0:T(8,128)S(1)}, f32[296,128]{1,0:T(8,128)S(1)}, u32[]{:S(2)}, u32[]{:S(2)}) %collective-permute-start.11) | collective-permute-done | bytes 151584 | tf_op jit(solution)/shard_map/ppermute | solution.py:75
  98.5 0.1 add_add_fusion.2
  98.6 1.0 collective-permute-start.14
  99.7 3.1 %collective-permute-start.13 = (f32[96,128]{1,0:T(8,128)S(1)}, f32[96,128]{1,0:T(8,128)S(1)}, u32[]{:S(2)}, u32[]{:S(2)}) collective-permute-start(f32[96,128]{1,0:T(8,128)S(1)} %slice_select_fusion), channel_id=1, source_target_pairs={{0,2},{1,3},{2,4},{3,5},{4,6},{5,7},{6,8},{7,9},{8,10},{9,11},{10,... | collective-permute-start | bytes 147464 | tf_op jit(solution)/shard_map/ppermute | solution.py:75
  102.8 4.7 %collective-permute-done.14 = f32[192,128]{1,0:T(8,128)S(1)} collective-permute-done((f32[192,128]{1,0:T(8,128)S(1)}, f32[192,128]{1,0:T(8,128)S(1)}, u32[]{:S(2)}, u32[]{:S(2)}) %collective-permute-start.14) | collective-permute-done | bytes 98336 | tf_op jit(solution)/shard_map/ppermute | solution.py:75
  107.5 0.7 collective-permute-done.13
  108.3 2.5 %collective-permute-start.15 = (f32[288,128]{1,0:T(8,128)S(1)}, f32[288,128]{1,0:T(8,128)S(1)}, u32[]{:S(2)}, u32[]{:S(2)}) collective-permute-start(f32[288,128]{1,0:T(8,128)S(1)} %pad_maximum_fusion.4), channel_id=1, source_target_pairs={{0,64},{1,65},{2,66},{3,67},{4,68},{5,69},{6,70},{7,71},{8,72},{9,... | collective-permute-start | bytes 442376 | tf_op jit(solution)/shard_map/ppermute | solution.py:75
  110.8 4.3 %collective-permute-done.15.twin_ref = f32[288,128]{1,0:T(8,128)S(1)} collective-permute-done((f32[288,128]{1,0:T(8,128)S(1)}, f32[288,128]{1,0:T(8,128)S(1)}, u32[]{:S(2)}, u32[]{:S(2)}) %collective-permute-start.15) | collective-permute-done | bytes 147488 | tf_op jit(solution)/shard_map/ppermute | solution.py:75
  115.1 0.1 collective-permute-start.16
  115.2 0.6 collective-permute-start.17
  115.8 1.4 %collective-permute-done.17.iother_ref = bf16[15,48,128]{2,1,0:T(8,128)(2,1)S(1)} collective-permute-done((bf16[15,48,128]{2,1,0:T(8,128)(2,1)S(1)}, bf16[15,48,128]{2,1,0:T(8,128)(2,1)S(1)}, u32[]{:S(2)}, u32[]{:S(2)}) %collective-permute-start.17) | collective-permute-done | bytes 184352 | tf_op jit(solution)/shard_map/ppermute | solution.py:75
  117.2 0.0 collective-permute-done.16.other_ref
  117.2 2.7 %smooth_slab.1 = (f32[3,3,96,128]{3,2,1,0:T(8,128)S(1)}, f32[3,96,128]{2,1,0:T(8,128)S(1)}, f32[3,96,128]{2,1,0:T(8,128)S(1)}, f32[1,128]{1,0:T(1,128)S(1)}) custom-call(s32[6]{0:T(128)S(1)} %stack.27.idx, f32[584,128]{1,0:T(8,128)S(1)} %pad_maximum_fusion.1.own_ref, f32[288,128]{1,0:T(8,128)S(1)} %collective-permute-done.15.twin_ref, ...), custom_call_target="tpu_custom_call" | custom-call | flops 100000000 | bytes 3000000 | tf_op jit(solution)/shard_map/smooth_slab/pallas_call | solution.py:540
  120.0 13.2 %all_to_all.10 = f32[32,1,128]{2,1,0:T(1,128)S(1)} all-to-all(f32[32,1,128]{2,1,0:T(1,128)S(1)} %broadcast_in_dim.11), channel_id=1, replica_groups=mesh['grp'=4,'sub'=32] {'sub'}, dimensions={0} | all-to-all | bytes 32768 | tf_op jit(solution)/shard_map/all_to_all | solution.py:652
  133.1 0.9 finish.1
  (15 shorter events, 0.2 us)
Async XLA Ops:
  0.6 0.9 copy-start
  0.6 11.7 %collective-permute-start = (bf16[96,96,128]{2,1,0:T(8,128)(2,1)}, bf16[96,96,128]{2,1,0:T(8,128)(2,1)}, u32[]{:S(2)}, u32[]{:S(2)}) collective-permute-start(bf16[96,96,128]{2,1,0:T(8,128)(2,1)} %bitcast.23), channel_id=1, source_target_pairs={{0,32},{1,33},{2,34},{3,35},{4,36},{5,37},{6,38},{7,39},{8,40},{9,... | collective-permute-start | bytes 7077896 | tf_op jit(solution)/shard_map/ppermute | solution.py:75
  2.8 29.1 %all-to-all-start = ((bf16[32,3,56,128]{3,2,1,0:T(8,128)(2,1)}), bf16[32,3,56,128]{3,2,1,0:T(8,128)(2,1)S(1)}, u32[]{:S(2)}, u32[]{:S(2)}) async-start(bf16[32,3,56,128]{3,2,1,0:T(8,128)(2,1)} %broadcast_in_dim.8), calls=%async_computation | async-start | bytes 2752512 | tf_op jit(solution)/shard_map/all_to_all | solution.py:617
  31.9 18.3 %copy-start.4 = (f32[8,3,48,128]{3,2,1,0:T(8,128)S(1)}, f32[8,3,48,128]{3,2,1,0:T(8,128)}, u32[]{:S(2)}) copy-start(f32[8,3,48,128]{3,2,1,0:T(8,128)} %get-tuple-element.30) | copy-start | bytes 1769476
  31.9 18.6 %copy-start.3 = (f32[8,3,48,128]{3,2,1,0:T(8,128)S(1)}, f32[8,3,48,128]{3,2,1,0:T(8,128)}, u32[]{:S(2)}) copy-start(f32[8,3,48,128]{3,2,1,0:T(8,128)} %get-tuple-element.31) | copy-start | bytes 1769476
  31.9 24.2 %copy-start.2 = (f32[8,3,48,128]{3,2,1,0:T(8,128)S(1)}, f32[8,3,48,128]{3,2,1,0:T(8,128)}, u32[]{:S(2)}) copy-start(f32[8,3,48,128]{3,2,1,0:T(8,128)} %get-tuple-element.32) | copy-start | bytes 1769476
  44.9 11.2 %collective-permute-start.1 = (f32[8,3,48,128]{3,2,1,0:T(8,128)S(1)}, f32[8,3,48,128]{3,2,1,0:T(8,128)S(1)}, u32[]{:S(2)}, u32[]{:S(2)}) collective-permute-start(f32[8,3,48,128]{3,2,1,0:T(8,128)S(1)} %get-tuple-element.24), channel_id=1, source_target_pairs={{0,1},{1,2},{2,3},{3,0},{4,5},{5,6},{6,7},{7,4},{8,9},{9,10},{10,1... | collective-permute-start | bytes 1769480 | tf_op jit(solution)/shard_map/ppermute | solution.py:75
  46.4 16.3 %collective-permute-start.2 = (f32[8,3,48,128]{3,2,1,0:T(8,128)S(1)}, f32[8,3,48,128]{3,2,1,0:T(8,128)S(1)}, u32[]{:S(2)}, u32[]{:S(2)}) collective-permute-start(f32[8,3,48,128]{3,2,1,0:T(8,128)S(1)} %get-tuple-element.25), channel_id=1, source_target_pairs={{0,2},{1,3},{2,0},{3,1},{4,6},{5,7},{6,4},{7,5},{8,10},{9,11},{10,... | collective-permute-start | bytes 1769480 | tf_op jit(solution)/shard_map/ppermute | solution.py:75
  48.4 14.9 %collective-permute-start.3 = (f32[8,3,48,128]{3,2,1,0:T(8,128)S(1)}, f32[8,3,48,128]{3,2,1,0:T(8,128)S(1)}, u32[]{:S(2)}, u32[]{:S(2)}) collective-permute-start(f32[8,3,48,128]{3,2,1,0:T(8,128)S(1)} %get-tuple-element.26), channel_id=1, source_target_pairs={{0,3},{1,0},{2,1},{3,2},{4,7},{5,4},{6,5},{7,6},{8,11},{9,8},{10,9... | collective-permute-start | bytes 1769480 | tf_op jit(solution)/shard_map/ppermute | solution.py:75
  50.2 18.5 %collective-permute-start.4 = (f32[8,3,48,128]{3,2,1,0:T(8,128)S(1)}, f32[8,3,48,128]{3,2,1,0:T(8,128)S(1)}, u32[]{:S(2)}, u32[]{:S(2)}) collective-permute-start(f32[8,3,48,128]{3,2,1,0:T(8,128)S(1)} %copy-done.4), channel_id=1, source_target_pairs={{0,1},{1,2},{2,3},{3,0},{4,5},{5,6},{6,7},{7,4},{8,9},{9,10},{10,1... | collective-permute-start | bytes 1769480 | tf_op jit(solution)/shard_map/ppermute | solution.py:75
  50.5 24.8 %collective-permute-start.5 = (f32[8,3,48,128]{3,2,1,0:T(8,128)S(1)}, f32[8,3,48,128]{3,2,1,0:T(8,128)S(1)}, u32[]{:S(2)}, u32[]{:S(2)}) collective-permute-start(f32[8,3,48,128]{3,2,1,0:T(8,128)S(1)} %copy-done.3), channel_id=1, source_target_pairs={{0,2},{1,3},{2,0},{3,1},{4,6},{5,7},{6,4},{7,5},{8,10},{9,11},{10,... | collective-permute-start | bytes 1769480 | tf_op jit(solution)/shard_map/ppermute | solution.py:75
  56.1 19.9 %collective-permute-start.6 = (f32[8,3,48,128]{3,2,1,0:T(8,128)S(1)}, f32[8,3,48,128]{3,2,1,0:T(8,128)S(1)}, u32[]{:S(2)}, u32[]{:S(2)}) collective-permute-start(f32[8,3,48,128]{3,2,1,0:T(8,128)S(1)} %copy-done.2), channel_id=1, source_target_pairs={{0,3},{1,0},{2,1},{3,2},{4,7},{5,4},{6,5},{7,6},{8,11},{9,8},{10,9... | collective-permute-start | bytes 1769480 | tf_op jit(solution)/shard_map/ppermute | solution.py:75
  63.3 12.7 %copy-start.1 = (f32[8,3,48,128]{3,2,1,0:T(8,128)S(1)}, f32[8,3,48,128]{3,2,1,0:T(8,128)}, u32[]{:S(2)}) copy-start(f32[8,3,48,128]{3,2,1,0:T(8,128)} %get-tuple-element.29) | copy-start | bytes 1769476
  76.2 8.0 %collective-permute-start.7 = (f32[2,6,48,128]{3,2,1,0:T(8,128)S(1)}, f32[2,6,48,128]{3,2,1,0:T(8,128)S(1)}, u32[]{:S(2)}, u32[]{:S(2)}) collective-permute-start(f32[2,6,48,128]{3,2,1,0:T(8,128)S(1)} %get-tuple-element.41), channel_id=1, source_target_pairs={{0,4},{1,5},{2,6},{3,7},{4,8},{5,9},{6,10},{7,11},{8,12},{9,13},{1... | collective-permute-start | bytes 884744 | tf_op jit(solution)/shard_map/ppermute | solution.py:75
  77.7 9.3 %collective-permute-start.9 = (f32[2,6,48,128]{3,2,1,0:T(8,128)S(1)}, f32[2,6,48,128]{3,2,1,0:T(8,128)S(1)}, u32[]{:S(2)}, u32[]{:S(2)}) collective-permute-start(f32[2,6,48,128]{3,2,1,0:T(8,128)S(1)} %get-tuple-element.42), channel_id=1, source_target_pairs={{0,12},{1,13},{2,14},{3,15},{4,0},{5,1},{6,2},{7,3},{8,4},{9,5},{1... | collective-permute-start | bytes 884744 | tf_op jit(solution)/shard_map/ppermute | solution.py:75
  79.5 8.4 %collective-permute-start.8 = (f32[2,6,48,128]{3,2,1,0:T(8,128)S(1)}, f32[2,6,48,128]{3,2,1,0:T(8,128)S(1)}, u32[]{:S(2)}, u32[]{:S(2)}) collective-permute-start(f32[2,6,48,128]{3,2,1,0:T(8,128)S(1)} %get-tuple-element.43), channel_id=1, source_target_pairs={{0,8},{1,9},{2,10},{3,11},{4,12},{5,13},{6,14},{7,15},{8,0},{9,1},... | collective-permute-start | bytes 884744 | tf_op jit(solution)/shard_map/ppermute | solution.py:75
  88.0 6.8 %collective-permute-start.10 = (f32[296,128]{1,0:T(8,128)S(1)}, f32[296,128]{1,0:T(8,128)S(1)}, u32[]{:S(2)}, u32[]{:S(2)}) collective-permute-start(f32[296,128]{1,0:T(8,128)S(1)} %get-tuple-element.44), channel_id=1, source_target_pairs={{0,64},{1,65},{2,66},{3,67},{4,68},{5,69},{6,70},{7,71},{8,72},{9,... | collective-permute-start | bytes 454664 | tf_op jit(solution)/shard_map/ppermute | solution.py:75
  90.8 5.6 %collective-permute-start.12 = (f32[296,128]{1,0:T(8,128)S(1)}, f32[296,128]{1,0:T(8,128)S(1)}, u32[]{:S(2)}, u32[]{:S(2)}) collective-permute-start(f32[296,128]{1,0:T(8,128)S(1)} %get-tuple-element.45), channel_id=1, source_target_pairs={{0,80},{1,81},{2,82},{3,83},{4,84},{5,85},{6,86},{7,87},{8,88},{9,... | collective-permute-start | bytes 454664 | tf_op jit(solution)/shard_map/ppermute | solution.py:75
  92.1 6.4 %collective-permute-start.11 = (f32[296,128]{1,0:T(8,128)S(1)}, f32[296,128]{1,0:T(8,128)S(1)}, u32[]{:S(2)}, u32[]{:S(2)}) collective-permute-start(f32[296,128]{1,0:T(8,128)S(1)} %get-tuple-element.45), channel_id=1, source_target_pairs={{0,16},{1,17},{2,18},{3,19},{4,20},{5,21},{6,22},{7,23},{8,24},{9,... | collective-permute-start | bytes 454664 | tf_op jit(solution)/shard_map/ppermute | solution.py:75
  98.6 8.9 %collective-permute-start.14 = (f32[192,128]{1,0:T(8,128)S(1)}, f32[192,128]{1,0:T(8,128)S(1)}, u32[]{:S(2)}, u32[]{:S(2)}) collective-permute-start(f32[192,128]{1,0:T(8,128)S(1)} %pad_maximum_fusion.5), channel_id=1, source_target_pairs={{0,1},{1,2},{2,3},{3,4},{4,5},{5,6},{6,7},{7,8},{8,9},{9,10},{10,1... | collective-permute-start | bytes 294920 | tf_op jit(solution)/shard_map/ppermute | solution.py:75
  99.7 8.6 %collective-permute-start.13 = (f32[96,128]{1,0:T(8,128)S(1)}, f32[96,128]{1,0:T(8,128)S(1)}, u32[]{:S(2)}, u32[]{:S(2)}) collective-permute-start(f32[96,128]{1,0:T(8,128)S(1)} %slice_select_fusion), channel_id=1, source_target_pairs={{0,2},{1,3},{2,4},{3,5},{4,6},{5,7},{6,8},{7,9},{8,10},{9,11},{10,... | collective-permute-start | bytes 147464 | tf_op jit(solution)/shard_map/ppermute | solution.py:75
  108.3 6.7 %collective-permute-start.15 = (f32[288,128]{1,0:T(8,128)S(1)}, f32[288,128]{1,0:T(8,128)S(1)}, u32[]{:S(2)}, u32[]{:S(2)}) collective-permute-start(f32[288,128]{1,0:T(8,128)S(1)} %pad_maximum_fusion.4), channel_id=1, source_target_pairs={{0,64},{1,65},{2,66},{3,67},{4,68},{5,69},{6,70},{7,71},{8,72},{9,... | collective-permute-start | bytes 442376 | tf_op jit(solution)/shard_map/ppermute | solution.py:75
  115.1 2.1 %collective-permute-start.16 = (f32[872,128]{1,0:T(8,128)S(1)}, f32[872,128]{1,0:T(8,128)S(1)}, u32[]{:S(2)}, u32[]{:S(2)}) collective-permute-start(f32[872,128]{1,0:T(8,128)S(1)} %pad_maximum_fusion), channel_id=1, source_target_pairs={{0,32},{1,33},{2,34},{3,35},{4,36},{5,37},{6,38},{7,39},{8,40},{9,... | collective-permute-start | bytes 1339400 | tf_op jit(solution)/shard_map/ppermute | solution.py:75
  115.2 2.0 %collective-permute-start.17 = (bf16[15,48,128]{2,1,0:T(8,128)(2,1)S(1)}, bf16[15,48,128]{2,1,0:T(8,128)(2,1)S(1)}, u32[]{:S(2)}, u32[]{:S(2)}) collective-permute-start(bf16[15,48,128]{2,1,0:T(8,128)(2,1)S(1)} %convert_element_type.3), channel_id=1, source_target_pairs={{0,32},{1,33},{2,34},{3,35},{4,36},{5,37},{6,38},{7,39},{8,40},{9,... | collective-permute-start | bytes 552968 | tf_op jit(solution)/shard_map/ppermute | solution.py:75

commit v7 on v6

--- a/solution.py
+++ b/solution.py
@@ -1,3 +1,4 @@
+import functools
 import math
 
 import jax
@@ -210,8 +211,8 @@
 
 
 def moving_kernel(
-    idx, ja_hbm, jb_hbm, out_ref, o0, o1, o2, o3,
-    ja_ref, jb_ref, pair, even, odd, three, last, ready, sem, in_sem, pair_sem,
+    idx, ja_hbm, jb_hbm, plane_hbm, o0, o1, o2, o3,
+    ja_ref, jb_ref, pair, even, odd, three, last, ready, in_sem, pair_sem, sem,
 ):
     shift = pl.multiple_of(idx[0] * 8, 8)
     length = 2 * CHUNK
@@ -239,25 +240,11 @@
         ]
 
     def copy(n):
-        slot = n & 1
+        slot = n & (SLOTS - 1)
         return pltpu.make_async_copy(
-            ready.at[slot], out_ref.at[:, pl.ds(n * length, length)], sem.at[slot]
+            ready.at[slot], plane_hbm.at[:, pl.ds(n * length, length)], sem.at[slot]
         )
 
-    def enter(n):
-        wait_part(fetches, n)
-
-        @pl.when(n >= 2)
-        def _():
-            copy(n - 2).wait()
-
-    def emit(v, n, q, rows, x):
-        ready[n & 1, v, q, rows, :] = x
-
-    triple_sums(
-        makers, (FIRST_ORDER, None) * 2, shift, even, odd, three, last,
-        enter, emit, lambda n: copy(n).start(),
-    )
     outs = []
     for kb, out in enumerate((o0, o1, o2, o3)):
         for t in range(8):
@@ -267,44 +254,76 @@
                     pair.at[pl.ds(slab * 3, 3), pl.ds(shift, OWN)], out.at[t], pair_sem.at[kb * 8 + t]
                 )
             )
-    for out in outs:
-        out.start()
-    copy(jnp.int32(STEPS - 1)).wait()
-    copy(jnp.int32(STEPS)).wait()
+
+    def enter(n):
+        wait_part(fetches, n)
+
+        @pl.when(n >= SLOTS)
+        def _():
+            copy(n - SLOTS).wait()
+
+        @pl.when(n == STEPS)
+        def _():
+            for out in outs:
+                out.start()
+
+    def emit(v, n, q, rows, x):
+        ready[n & (SLOTS - 1), v, q, rows, :] = x
+
+    triple_sums(
+        makers, (FIRST_ORDER, None) * 2, shift, even, odd, three, last,
+        enter, emit, lambda n: copy(n).start(),
+    )
+    for n in range(STEPS + 1 - SLOTS, STEPS + 1):
+        copy(jnp.int32(n)).wait()
     for out in outs:
         out.wait()
 
 
+SLOTS = 4
+LINES = [
+    [pltpu.VMEM((CHUNK, 88, NY), F32)] * 4,
+    [pltpu.VMEM((CHUNK, 88, NY), F32)] * 4,
+    [pltpu.VMEM((CHUNK, 64, NY), F32)] * 4,
+    [pltpu.VMEM((2, OWN, NY), F32)] * 4,
+]
+SMALL = pl.BlockSpec(memory_space=pltpu.SMEM)
+FAR = pl.BlockSpec(memory_space=pltpu.HBM)
+NEAR = pl.BlockSpec(memory_space=pltpu.VMEM)
+WINDOW = pltpu.VMEM((NZ, WIN, NY), BF16)
+PLANES = pltpu.VMEM((4, PAGES, OWN, NY), F32)
+RAW = pltpu.VMEM((3, NZ, WIN, NY), F32)
+
+
+def in_vmem(x):
+    return pltpu.with_memory_space_constraint(x, pltpu.VMEM)
+
+
 def moving_planes(idx, ja, jb):
-    hbm = pl.BlockSpec(memory_space=pltpu.HBM)
     return pl.pallas_call(
         moving_kernel,
-        out_shape=[pltpu.HBM((4, PAGES, OWN, NY), F32)]
-        + [pltpu.HBM((8, 3, OWN, NY), F32)] * 4,
-        in_specs=[pl.BlockSpec(memory_space=pltpu.SMEM), hbm, hbm],
-        out_specs=[hbm] * 5,
+        out_shape=[pltpu.HBM((4, PAGES, OWN, NY), F32)] + [pltpu.HBM((8, 3, OWN, NY), F32)] * 4,
+        in_specs=[SMALL, FAR, FAR],
+        out_specs=[FAR] * 5,
         scratch_shapes=[
-            pltpu.VMEM((NZ, WIN, NY), BF16),
-            pltpu.VMEM((NZ, WIN, NY), BF16),
+            WINDOW,
+            WINDOW,
             pltpu.VMEM((NZ, WIN, NY), F32),
-            [pltpu.VMEM((CHUNK, 88, NY), F32)] * 4,
-            [pltpu.VMEM((CHUNK, 88, NY), F32)] * 4,
-            [pltpu.VMEM((CHUNK, 64, NY), F32)] * 4,
-            [pltpu.VMEM((2, OWN, NY), F32)] * 4,
-            pltpu.VMEM((2, 4, 2 * CHUNK, OWN, NY), F32),
-            pltpu.SemaphoreType.DMA((2,)),
+            *LINES,
+            pltpu.VMEM((SLOTS, 4, 2 * CHUNK, OWN, NY), F32),
             pltpu.SemaphoreType.DMA((2, PARTS)),
             pltpu.SemaphoreType.DMA((32,)),
+            pltpu.SemaphoreType.DMA((SLOTS,)),
         ],
-        compiler_params=pltpu.CompilerParams(vmem_limit_bytes=28 << 20),
-        cost_estimate=pl.CostEstimate(flops=4 * 10**9, bytes_accessed=17 * 10**6, transcendentals=0),
+        compiler_params=pltpu.CompilerParams(vmem_limit_bytes=24 << 20),
+        cost_estimate=pl.CostEstimate(flops=4 * 10**9, bytes_accessed=6 * 10**6, transcendentals=0),
         name="moving_planes",
     )(idx, in_hbm(ja), in_hbm(jb))
 
 
-def factor_kernel(
-    idx, i_hbm, ja_hbm, jb_hbm, jplane_ref, o0, o1, o2, o3, cc_ref, iext_ref,
-    i_ref, ja_ref, jb_ref, raw, even, odd, three, last, iplane, jplane, sem, in_sem, i_sem,
+def template_kernel(
+    idx, i_hbm, ja_hbm, jb_hbm, plane, raw, iext_ref,
+    i_ref, ja_ref, jb_ref, even, odd, three, last, in_sem, i_sem,
 ):
     shift = pl.multiple_of(idx[0] * 8, 8)
     fetches = window_fetches(idx[0], ((ja_hbm, ja_ref), (jb_hbm, jb_ref)), in_sem)
@@ -313,8 +332,6 @@
         fetches[p].append(pltpu.make_async_copy(i_hbm.at[part], i_ref.at[part], i_sem.at[p]))
         for fetch in fetches[p]:
             fetch.start()
-    fetch = pltpu.make_async_copy(jplane_ref, jplane, sem)
-    fetch.start()
 
     def makers(base):
         def wide(n, keep):
@@ -335,18 +352,46 @@
         ]
 
     def emit(v, n, q, rows, x):
-        iplane[v, 2 * CHUNK * n + q, rows, :] = x
+        plane[v, 2 * CHUNK * n + q, rows, :] = x
 
     triple_sums(
         makers, (FIRST_ORDER, None, None, None), shift, even, odd, three, last,
         lambda n: wait_part(fetches, n), emit, lambda n: None,
     )
-    fetch.wait()
-
+    start = idx[4] * 3 - 6
+    for j in range(15):
+        z = start + j
+        inside = jnp.logical_and(z >= 0, z < NZ)
+        page = raw[0, jnp.clip(z, 0, NZ - 1), pl.ds(shift, OWN), :]
+        iext_ref[j] = jnp.where(inside, page, 0.0).astype(BF16)
+
+
+def template_planes(idx, image, ja, jb):
+    return pl.pallas_call(
+        template_kernel,
+        out_shape=[PLANES, RAW, jax.ShapeDtypeStruct((15, OWN, NY), BF16)],
+        in_specs=[SMALL, FAR, FAR, FAR],
+        out_specs=[NEAR] * 3,
+        scratch_shapes=[
+            WINDOW,
+            WINDOW,
+            WINDOW,
+            *LINES,
+            pltpu.SemaphoreType.DMA((2, PARTS)),
+            pltpu.SemaphoreType.DMA((PARTS,)),
+        ],
+        compiler_params=pltpu.CompilerParams(vmem_limit_bytes=16 << 20),
+        cost_estimate=pl.CostEstimate(flops=4 * 10**9, bytes_accessed=5 * 10**6, transcendentals=0),
+        name="template_planes",
+    )(idx, image, in_hbm(ja), in_hbm(jb))
+
+
+def factor_kernel(kb, idx, iplane, jplane, raw, out, cc_ref):
+    shift = pl.multiple_of(idx[0] * 8, 8)
     eps_b = EPSILON * COUNT
     eps_bc = EPSILON * COUNT**2
 
-    def block(out, kb, t, cc):
+    def block(t, cc):
         slab = slab_of(idx, kb, t // 2, t % 2)
         first = slab * 3
         for r in range(OWN // 8):
@@ -379,47 +424,22 @@
                 out[t, j, part, :] = total[j]
         return cc
 
-    cc = jnp.zeros((8, NY), F32)
-    for kb, out in enumerate((o0, o1, o2, o3)):
-        cc = lax.fori_loop(0, 8, lambda t, cc, out=out, kb=kb: block(out, kb, t, cc), cc)
-    cc_ref[...] = cc
-
-    start = idx[4] * 3 - 6
-    for j in range(15):
-        z = start + j
-        inside = jnp.logical_and(z >= 0, z < NZ)
-        page = raw[0, jnp.clip(z, 0, NZ - 1), pl.ds(shift, OWN), :]
-        iext_ref[j] = jnp.where(inside, page, 0.0)
-
-
-def factors(idx, image, ja, jb, jplane):
-    vm = pl.BlockSpec(memory_space=pltpu.VMEM)
-    block = jax.ShapeDtypeStruct((8, 3, OWN, NY), F32)
+    cc_ref[...] = lax.fori_loop(0, 8, block, jnp.zeros((8, NY), F32))
+
+
+def factors(kb, idx, iplane, jplane, raw):
     return pl.pallas_call(
-        factor_kernel,
-        out_shape=[block] * 4
-        + [jax.ShapeDtypeStruct((8, NY), F32), jax.ShapeDtypeStruct((15, OWN, NY), F32)],
-        in_specs=[pl.BlockSpec(memory_space=pltpu.SMEM)] + [pl.BlockSpec(memory_space=pltpu.HBM)] * 4,
-        out_specs=[vm] * 6,
-        scratch_shapes=[
-            pltpu.VMEM((NZ, WIN, NY), BF16),
-            pltpu.VMEM((NZ, WIN, NY), BF16),
-            pltpu.VMEM((NZ, WIN, NY), BF16),
-            pltpu.VMEM((3, NZ, WIN, NY), F32),
-            [pltpu.VMEM((CHUNK, 88, NY), F32)] * 4,
-            [pltpu.VMEM((CHUNK, 88, NY), F32)] * 4,
-            [pltpu.VMEM((CHUNK, 64, NY), F32)] * 4,
-            [pltpu.VMEM((2, OWN, NY), F32)] * 4,
-            pltpu.VMEM((4, PAGES, OWN, NY), F32),
-            pltpu.VMEM((4, PAGES, OWN, NY), F32),
-            pltpu.SemaphoreType.DMA,
-            pltpu.SemaphoreType.DMA((2, PARTS)),
-            pltpu.SemaphoreType.DMA((PARTS,)),
+        functools.partial(factor_kernel, kb),
+        out_shape=[
+            jax.ShapeDtypeStruct((8, 3, OWN, NY), F32),
+            jax.ShapeDtypeStruct((8, NY), F32),
         ],
-        compiler_params=pltpu.CompilerParams(vmem_limit_bytes=44 << 20),
-        cost_estimate=pl.CostEstimate(flops=4 * 10**9, bytes_accessed=18 * 10**6, transcendentals=0),
+        in_specs=[SMALL, NEAR, NEAR, NEAR],
+        out_specs=[NEAR] * 2,
+        compiler_params=pltpu.CompilerParams(vmem_limit_bytes=4 << 20),
+        cost_estimate=pl.CostEstimate(flops=4 * 10**8, bytes_accessed=10**6, transcendentals=0),
         name="factors",
-    )(idx, image, in_hbm(ja), in_hbm(jb), in_hbm(jplane))
+    )(idx, in_vmem(iplane), in_vmem(jplane), in_vmem(raw))
 
 
 CC_ROWS = 8
@@ -467,7 +487,7 @@
         sides(other_rows, (other_ref, CENTRE + SIDE), (other_ref, CENTRE))
 
     for p in range(15):
-        image[p, my_rows, :] = iown_ref[p]
+        image[p, my_rows, :] = iown_ref[p].astype(F32)
         image[p, other_rows, :] = iother_ref[p].astype(F32)
 
     weights = [math.exp(-o * o / (2.0 * VARIANCE)) for o in range(-REACH, REACH + 1)]
@@ -618,12 +638,17 @@
 
     jplane, *j_blocks = moving_planes(idx, keep, take)
     j_got = round_one(j_blocks)
-    *f_blocks, cc, i_half = factors(idx, image, keep, take, jplane)
-    f_got = round_one(f_blocks)
+    iplane, raw, i_half = template_planes(idx, image, keep, take)
+    f_blocks, f_got, cc = [None] * 4, [None] * 4, None
+    for k in (2, 1, 3, 0):
+        f_blocks[k], part = factors(k, idx, iplane, jplane, raw)
+        cc = part if cc is None else cc + part
+        if k:
+            f_got[k] = permute(f_blocks[k], first_round(k))
     j_own = after(j_blocks[0], cc)
     j_total = j_own + j_got[0] + j_got[1] + j_got[2]
-    i_other = permute(i_half.astype(BF16), CORE_PAIRS)
-    f_total = f_blocks[0] + f_got[0] + f_got[1] + f_got[2]
+    i_other = permute(i_half, CORE_PAIRS)
+    f_total = f_blocks[0] + f_got[1] + f_got[2] + f_got[3]
     part = round_two(jnp.concatenate([f_total, j_total], axis=1))
     both = jnp.concatenate(
         [part.reshape(2, 6 * OWN, NY), jnp.broadcast_to(cc[None], (2, CC_ROWS, NY))], axis=1

time: 135 us -> 123 us (0.911)
  waiting for transfers between devices: 54.4 us -> 35 us
  starting transfers between devices: 33.9 us -> 40.8 us
    ppermute x18, waiting for transfers between devices: 47.1 us -> 30.4 us  [permute(): return lax.ppermute(x, BOTH, table)]
    ppermute x18, starting transfers between devices: 24.5 us -> 31.5 us  [permute(): return lax.ppermute(x, BOTH, table)]
    all_to_all x1, waiting for transfers between devices: 7.28 us -> 4.68 us  [step(): image = lax.all_to_all(copies, 'sub', 0, 0, tiled=True).reshape(NZ, WIN, NY)]
    pallas_call x1, Pallas kernels: 12.2 us -> 9.67 us  [moving_planes(): pl.pallas_call(moving_kernel, out_shape=[pltpu.HBM((4, PAGES, OWN, NY), F...]
    pallas_call x1 -> x5, Pallas kernels: 13 us -> 15.4 us  [the longest x1 8.1 us: template_planes(): pl.pallas_call(template_kernel, out_shape=[PLANES, RAW, jax.ShapeDtypeStr...]
  transfers between devices with their start and end apart: 19 -> 19, of which waited for: 17 -> 11; matrix products, arithmetic and copies ran while one was open for 1% -> 1% of each run, Pallas kernels for 9% -> 21%
where the time goes in v7:
time: 123 us; the launch traced here: 122 us
  starting transfers between devices  40.8 us (33%)
  waiting for transfers between devices  35 us (28%)
  Pallas kernels  28.8 us (23%)
  blocking collectives  13.2 us (11%)
  local copies, waits for them, and re-layouts  2.16 us (2%)
    ppermute x18, starting transfers between devices, permute(): return lax.ppermute(x, BOTH, table)  31.5 us
    ppermute x18, waiting for transfers between devices, permute(): return lax.ppermute(x, BOTH, table)  30.4 us
    all_to_all x1, blocking collectives, step(): lax.all_to_all(jnp.broadcast_to(stats[None], (32, 1, NY)), 'sub', 0, 0, t...  13.2 us
    pallas_call x1, Pallas kernels, moving_planes(): pl.pallas_call(moving_kernel, out_shape=[pltpu.HBM((4, PAGES, OWN, NY), F...  9.67 us
    all_to_all x1, starting transfers between devices, step(): image = lax.all_to_all(copies, 'sub', 0, 0, tiled=True).reshape(NZ, WIN, NY)  9.37 us
    pallas_call x1, Pallas kernels, template_planes(): pl.pallas_call(template_kernel, out_shape=[PLANES, RAW, jax.ShapeDtypeStr...  8.1 us
    pallas_call x4, Pallas kernels, factors(): pl.pallas_call(functools.partial(factor_kernel, kb), out_shape=[jax.Shape...  7.3 us
    all_to_all x1, waiting for transfers between devices, step(): image = lax.all_to_all(copies, 'sub', 0, 0, tiled=True).reshape(NZ, WIN, NY)  4.68 us
  transfers between devices with their start and end apart: 19, of which 11 were waited for; matrix products, arithmetic and copies ran while one was open for 1% of the time, Pallas kernels for 21%

profile of v7, /device:TPU:0, one launch (start us, length us, event | category | flops | bytes accessed | tf_op | source)
XLA Modules:
  0.0 121.5 jit_solution(10580709863934182568)
XLA Ops:
  0.6 0.0 copy-start
  0.6 0.1 collective-permute-start
  0.8 0.8 copy-done
  1.5 1.3 %broadcast_in_dim.8 = bf16[32,3,56,128]{3,2,1,0:T(8,128)(2,1)} broadcast(bf16[3,56,128]{2,1,0:T(8,128)(2,1)S(1)} %constant_dynamic-slice_fusion), dimensions={1,2,3} | broadcast | bytes 1419264 | tf_op jit(solution)/shard_map/broadcast_in_dim | solution.py:636
  2.8 9.4 %all-to-all-start = ((bf16[32,3,56,128]{3,2,1,0:T(8,128)(2,1)}), bf16[32,3,56,128]{3,2,1,0:T(8,128)(2,1)S(1)}, u32[]{:S(2)}, u32[]{:S(2)}) async-start(bf16[32,3,56,128]{3,2,1,0:T(8,128)(2,1)} %broadcast_in_dim.8), calls=%async_computation | async-start | bytes 2752512 | tf_op jit(solution)/shard_map/all_to_all | solution.py:637
  12.2 0.1 stack.27.idx
  12.3 0.0 collective-permute-done.jb_hbm
  12.3 9.7 %moving_planes.1 = (f32[4,104,48,128]{3,2,1,0:T(8,128)}, f32[8,3,48,128]{3,2,1,0:T(8,128)}, f32[8,3,48,128]{3,2,1,0:T(8,128)}, f32[8,3,48,128]{3,2,1,0:T(8,128)}, f32[8,3,48,128]{3,2,1,0:T(8,128)}) custom-call(s32[6]{0:T(128)S(1)} %stack.27.idx, bf16[96,96,128]{2,1,0:T(8,128)(2,1)} %bitcast.24, bf16[96,96,128]{2,1,0:T(8,128)(2,1)} %collective-permute-done.jb_hbm), custom_call_target="tpu_custom_call" | custom-call | flops 4000000000 | bytes 6000000 | tf_op jit(solution)/shard_map/moving_planes/pallas_call | solution.py:303
  22.0 1.8 %collective-permute-start.4 = (f32[8,3,48,128]{3,2,1,0:T(8,128)}, f32[8,3,48,128]{3,2,1,0:T(8,128)S(1)}, u32[]{:S(2)}, u32[]{:S(2)}) collective-permute-start(f32[8,3,48,128]{3,2,1,0:T(8,128)} %get-tuple-element.40), channel_id=1, source_target_pairs={{0,1},{1,2},{2,3},{3,0},{4,5},{5,6},{6,7},{7,4},{8,9},{9,10},{10,1... | collective-permute-start | bytes 1769480 | tf_op jit(solution)/shard_map/ppermute | solution.py:76
  23.8 2.7 %collective-permute-start.5 = (f32[8,3,48,128]{3,2,1,0:T(8,128)}, f32[8,3,48,128]{3,2,1,0:T(8,128)S(1)}, u32[]{:S(2)}, u32[]{:S(2)}) collective-permute-start(f32[8,3,48,128]{3,2,1,0:T(8,128)} %get-tuple-element.41), channel_id=1, source_target_pairs={{0,2},{1,3},{2,0},{3,1},{4,6},{5,7},{6,4},{7,5},{8,10},{9,11},{10,... | collective-permute-start | bytes 1769480 | tf_op jit(solution)/shard_map/ppermute | solution.py:76
  26.5 1.5 %collective-permute-start.6 = (f32[8,3,48,128]{3,2,1,0:T(8,128)}, f32[8,3,48,128]{3,2,1,0:T(8,128)S(1)}, u32[]{:S(2)}, u32[]{:S(2)}) collective-permute-start(f32[8,3,48,128]{3,2,1,0:T(8,128)} %get-tuple-element.42), channel_id=1, source_target_pairs={{0,3},{1,0},{2,1},{3,2},{4,7},{5,4},{6,5},{7,6},{8,11},{9,8},{10,9... | collective-permute-start | bytes 1769480 | tf_op jit(solution)/shard_map/ppermute | solution.py:76
  28.0 4.7 %all-to-all-done = bf16[32,3,56,128]{3,2,1,0:T(8,128)(2,1)S(1)} async-done(((bf16[32,3,56,128]{3,2,1,0:T(8,128)(2,1)}), bf16[32,3,56,128]{3,2,1,0:T(8,128)(2,1)S(1)}, u32[]{:S(2)}, u32[]{:S(2)}) %all-to-all-start) | async-done | bytes 1376288 | tf_op jit(solution)/shard_map/all_to_all | solution.py:637
  32.7 0.0 copy-start.1
  32.7 8.1 %template_planes.1 = (f32[4,104,48,128]{3,2,1,0:T(8,128)S(1)}, f32[3,96,56,128]{3,2,1,0:T(8,128)S(1)}, bf16[15,48,128]{2,1,0:T(8,128)(2,1)S(1)}) custom-call(s32[6]{0:T(128)S(1)} %stack.27.idx, bf16[96,56,128]{2,1,0:T(8,128)(2,1)S(1)} %bitcast.18, bf16[96,96,128]{2,1,0:T(8,128)(2,1)} %bitcast.25, bf16[96,96,128]{2,1,0:T(8,128)(2,1)} %collective-permute-done.jb_hbm), custom_call_target="tpu_custom_call" | custom-call | flops 4000000000 | bytes 5000000 | tf_op jit(solution)/shard_map/template_planes/pallas_call | solution.py:370
  40.8 0.0 copy-done.1
  40.8 1.9 %factors.5 = (f32[8,3,48,128]{3,2,1,0:T(8,128)S(1)}, f32[8,128]{1,0:T(8,128)S(1)}) custom-call(s32[6]{0:T(128)S(1)} %stack.27.idx, f32[4,104,48,128]{3,2,1,0:T(8,128)S(1)} %get-tuple-element.27.iplane, f32[4,104,48,128]{3,2,1,0:T(8,128)S(1)} %copy-done.1, f32[3,96,56,128]{3,2,1,0:T(8,128)S(1)} %get-tuple-element.29.raw), custom_call_target="tpu_custom_call" | custom-call | flops 400000000 | bytes 1000000 | tf_op jit(solution)/shard_map/factors/pallas_call | solution.py:431
  42.7 1.1 collective-permute-start.1
  43.7 1.8 %factors.6 = (f32[8,3,48,128]{3,2,1,0:T(8,128)S(1)}, f32[8,128]{1,0:T(8,128)S(1)}) custom-call(s32[6]{0:T(128)S(1)} %stack.27.idx, f32[4,104,48,128]{3,2,1,0:T(8,128)S(1)} %get-tuple-element.27.iplane, f32[4,104,48,128]{3,2,1,0:T(8,128)S(1)} %copy-done.1, f32[3,96,56,128]{3,2,1,0:T(8,128)S(1)} %get-tuple-element.29.raw), custom_call_target="tpu_custom_call" | custom-call | flops 400000000 | bytes 1000000 | tf_op jit(solution)/shard_map/factors/pallas_call | solution.py:431
  45.6 1.8 %collective-permute-start.2 = (f32[8,3,48,128]{3,2,1,0:T(8,128)S(1)}, f32[8,3,48,128]{3,2,1,0:T(8,128)S(1)}, u32[]{:S(2)}, u32[]{:S(2)}) collective-permute-start(f32[8,3,48,128]{3,2,1,0:T(8,128)S(1)} %get-tuple-element.32), channel_id=1, source_target_pairs={{0,2},{1,3},{2,0},{3,1},{4,6},{5,7},{6,4},{7,5},{8,10},{9,11},{10,... | collective-permute-start | bytes 1769480 | tf_op jit(solution)/shard_map/ppermute | solution.py:76
  47.4 1.8 %factors.7 = (f32[8,3,48,128]{3,2,1,0:T(8,128)S(1)}, f32[8,128]{1,0:T(8,128)S(1)}) custom-call(s32[6]{0:T(128)S(1)} %stack.27.idx, f32[4,104,48,128]{3,2,1,0:T(8,128)S(1)} %get-tuple-element.27.iplane, f32[4,104,48,128]{3,2,1,0:T(8,128)S(1)} %copy-done.1, f32[3,96,56,128]{3,2,1,0:T(8,128)S(1)} %get-tuple-element.29.raw), custom_call_target="tpu_custom_call" | custom-call | flops 400000000 | bytes 1000000 | tf_op jit(solution)/shard_map/factors/pallas_call | solution.py:431
  49.1 0.0 collective-permute-done.4
  49.1 0.0 copy-start.2
  49.2 1.8 %collective-permute-start.3 = (f32[8,3,48,128]{3,2,1,0:T(8,128)S(1)}, f32[8,3,48,128]{3,2,1,0:T(8,128)S(1)}, u32[]{:S(2)}, u32[]{:S(2)}) collective-permute-start(f32[8,3,48,128]{3,2,1,0:T(8,128)S(1)} %get-tuple-element.33), channel_id=1, source_target_pairs={{0,3},{1,0},{2,1},{3,2},{4,7},{5,4},{6,5},{7,6},{8,11},{9,8},{10,9... | collective-permute-start | bytes 1769480 | tf_op jit(solution)/shard_map/ppermute | solution.py:76
  50.9 1.8 %factors.4 = (f32[8,3,48,128]{3,2,1,0:T(8,128)S(1)}, f32[8,128]{1,0:T(8,128)S(1)}) custom-call(s32[6]{0:T(128)S(1)} %stack.27.idx, f32[4,104,48,128]{3,2,1,0:T(8,128)S(1)} %get-tuple-element.27.iplane, f32[4,104,48,128]{3,2,1,0:T(8,128)S(1)} %copy-done.1, f32[3,96,56,128]{3,2,1,0:T(8,128)S(1)} %get-tuple-element.29.raw), custom_call_target="tpu_custom_call" | custom-call | flops 400000000 | bytes 1000000 | tf_op jit(solution)/shard_map/factors/pallas_call | solution.py:431
  52.8 0.0 collective-permute-done.5
  52.8 0.0 collective-permute-done.6
  52.8 0.0 copy-done.2
  52.8 0.1 add_add_fusion
  52.9 7.2 %collective-permute-done.1 = f32[8,3,48,128]{3,2,1,0:T(8,128)S(1)} collective-permute-done((f32[8,3,48,128]{3,2,1,0:T(8,128)S(1)}, f32[8,3,48,128]{3,2,1,0:T(8,128)S(1)}, u32[]{:S(2)}, u32[]{:S(2)}) %collective-permute-start.1) | collective-permute-done | bytes 589856 | tf_op jit(solution)/shard_map/ppermute | solution.py:76
  60.1 0.0 collective-permute-done.2
  60.1 2.8 %collective-permute-done.3 = f32[8,3,48,128]{3,2,1,0:T(8,128)S(1)} collective-permute-done((f32[8,3,48,128]{3,2,1,0:T(8,128)S(1)}, f32[8,3,48,128]{3,2,1,0:T(8,128)S(1)}, u32[]{:S(2)}, u32[]{:S(2)}) %collective-permute-start.3) | collective-permute-done | bytes 589856 | tf_op jit(solution)/shard_map/ppermute | solution.py:76
  63.0 0.2 add_add_fusion.1
  63.1 0.1 fusion.5
  63.2 1.7 %collective-permute-start.7 = (f32[2,6,48,128]{3,2,1,0:T(8,128)S(1)}, f32[2,6,48,128]{3,2,1,0:T(8,128)S(1)}, u32[]{:S(2)}, u32[]{:S(2)}) collective-permute-start(f32[2,6,48,128]{3,2,1,0:T(8,128)S(1)} %get-tuple-element.51), channel_id=1, source_target_pairs={{0,4},{1,5},{2,6},{3,7},{4,8},{5,9},{6,10},{7,11},{8,12},{9,13},{1... | collective-permute-start | bytes 884744 | tf_op jit(solution)/shard_map/ppermute | solution.py:76
  64.9 1.4 %collective-permute-start.8 = (f32[2,6,48,128]{3,2,1,0:T(8,128)S(1)}, f32[2,6,48,128]{3,2,1,0:T(8,128)S(1)}, u32[]{:S(2)}, u32[]{:S(2)}) collective-permute-start(f32[2,6,48,128]{3,2,1,0:T(8,128)S(1)} %get-tuple-element.53), channel_id=1, source_target_pairs={{0,8},{1,9},{2,10},{3,11},{4,12},{5,13},{6,14},{7,15},{8,0},{9,1},... | collective-permute-start | bytes 884744 | tf_op jit(solution)/shard_map/ppermute | solution.py:76
  66.4 2.0 %collective-permute-start.9 = (f32[2,6,48,128]{3,2,1,0:T(8,128)S(1)}, f32[2,6,48,128]{3,2,1,0:T(8,128)S(1)}, u32[]{:S(2)}, u32[]{:S(2)}) collective-permute-start(f32[2,6,48,128]{3,2,1,0:T(8,128)S(1)} %get-tuple-element.52), channel_id=1, source_target_pairs={{0,12},{1,13},{2,14},{3,15},{4,0},{5,1},{6,2},{7,3},{8,4},{9,5},{1... | collective-permute-start | bytes 884744 | tf_op jit(solution)/shard_map/ppermute | solution.py:76
  68.3 6.0 %collective-permute-done.7 = f32[2,6,48,128]{3,2,1,0:T(8,128)S(1)} collective-permute-done((f32[2,6,48,128]{3,2,1,0:T(8,128)S(1)}, f32[2,6,48,128]{3,2,1,0:T(8,128)S(1)}, u32[]{:S(2)}, u32[]{:S(2)}) %collective-permute-start.7) | collective-permute-done | bytes 294944 | tf_op jit(solution)/shard_map/ppermute | solution.py:76
  74.4 0.0 collective-permute-done.8
  74.4 0.9 collective-permute-done.9
  75.2 0.1 fusion.4
  75.4 2.8 %collective-permute-start.10 = (f32[296,128]{1,0:T(8,128)S(1)}, f32[296,128]{1,0:T(8,128)S(1)}, u32[]{:S(2)}, u32[]{:S(2)}) collective-permute-start(f32[296,128]{1,0:T(8,128)S(1)} %get-tuple-element.54), channel_id=1, source_target_pairs={{0,64},{1,65},{2,66},{3,67},{4,68},{5,69},{6,70},{7,71},{8,72},{9,... | collective-permute-start | bytes 454664 | tf_op jit(solution)/shard_map/ppermute | solution.py:76
  78.2 0.2 collective-permute-start.11
  78.3 3.1 %collective-permute-start.12 = (f32[296,128]{1,0:T(8,128)S(1)}, f32[296,128]{1,0:T(8,128)S(1)}, u32[]{:S(2)}, u32[]{:S(2)}) collective-permute-start(f32[296,128]{1,0:T(8,128)S(1)} %get-tuple-element.55), channel_id=1, source_target_pairs={{0,80},{1,81},{2,82},{3,83},{4,84},{5,85},{6,86},{7,87},{8,88},{9,... | collective-permute-start | bytes 454664 | tf_op jit(solution)/shard_map/ppermute | solution.py:76
  81.4 0.7 collective-permute-done.10
  82.1 2.4 %collective-permute-done.11 = f32[296,128]{1,0:T(8,128)S(1)} collective-permute-done((f32[296,128]{1,0:T(8,128)S(1)}, f32[296,128]{1,0:T(8,128)S(1)}, u32[]{:S(2)}, u32[]{:S(2)}) %collective-permute-start.11) | collective-permute-done | bytes 151584 | tf_op jit(solution)/shard_map/ppermute | solution.py:76
  84.6 0.0 collective-permute-done.12
  84.7 1.1 collective-permute-start.14
  85.8 3.0 %collective-permute-start.13 = (f32[96,128]{1,0:T(8,128)S(1)}, f32[96,128]{1,0:T(8,128)S(1)}, u32[]{:S(2)}, u32[]{:S(2)}) collective-permute-start(f32[96,128]{1,0:T(8,128)S(1)} %slice_select_fusion), channel_id=1, source_target_pairs={{0,2},{1,3},{2,4},{3,5},{4,6},{5,7},{6,8},{7,9},{8,10},{9,11},{10,... | collective-permute-start | bytes 147464 | tf_op jit(solution)/shard_map/ppermute | solution.py:76
  88.8 4.7 %collective-permute-done.14 = f32[192,128]{1,0:T(8,128)S(1)} collective-permute-done((f32[192,128]{1,0:T(8,128)S(1)}, f32[192,128]{1,0:T(8,128)S(1)}, u32[]{:S(2)}, u32[]{:S(2)}) %collective-permute-start.14) | collective-permute-done | bytes 98336 | tf_op jit(solution)/shard_map/ppermute | solution.py:76
  93.6 0.8 collective-permute-done.13
  94.5 4.8 %collective-permute-start.15 = (f32[288,128]{1,0:T(8,128)S(1)}, f32[288,128]{1,0:T(8,128)S(1)}, u32[]{:S(2)}, u32[]{:S(2)}) collective-permute-start(f32[288,128]{1,0:T(8,128)S(1)} %pad_maximum_fusion.4), channel_id=1, source_target_pairs={{0,64},{1,65},{2,66},{3,67},{4,68},{5,69},{6,70},{7,71},{8,72},{9,... | collective-permute-start | bytes 442376 | tf_op jit(solution)/shard_map/ppermute | solution.py:76
  99.3 3.1 %collective-permute-done.15.twin_ref = f32[288,128]{1,0:T(8,128)S(1)} collective-permute-done((f32[288,128]{1,0:T(8,128)S(1)}, f32[288,128]{1,0:T(8,128)S(1)}, u32[]{:S(2)}, u32[]{:S(2)}) %collective-permute-start.15) | collective-permute-done | bytes 147488 | tf_op jit(solution)/shard_map/ppermute | solution.py:76
  102.5 0.1 collective-permute-start.16
  102.6 0.5 collective-permute-start.17
  103.1 1.5 %collective-permute-done.17.iother_ref = bf16[15,48,128]{2,1,0:T(8,128)(2,1)S(1)} collective-permute-done((bf16[15,48,128]{2,1,0:T(8,128)(2,1)S(1)}, bf16[15,48,128]{2,1,0:T(8,128)(2,1)S(1)}, u32[]{:S(2)}, u32[]{:S(2)}) %collective-permute-start.17) | collective-permute-done | bytes 184352 | tf_op jit(solution)/shard_map/ppermute | solution.py:76
  104.6 0.0 collective-permute-done.16.other_ref
  104.6 2.8 %smooth_slab.1 = (f32[3,3,96,128]{3,2,1,0:T(8,128)S(1)}, f32[3,96,128]{2,1,0:T(8,128)S(1)}, f32[3,96,128]{2,1,0:T(8,128)S(1)}, f32[1,128]{1,0:T(1,128)S(1)}) custom-call(s32[6]{0:T(128)S(1)} %stack.27.idx, f32[584,128]{1,0:T(8,128)S(1)} %pad_maximum_fusion.1.own_ref, f32[288,128]{1,0:T(8,128)S(1)} %collective-permute-done.15.twin_ref, ...), custom_call_target="tpu_custom_call" | custom-call | flops 100000000 | bytes 3000000 | tf_op jit(solution)/shard_map/smooth_slab/pallas_call | solution.py:560
  107.4 13.2 %all_to_all.10 = f32[32,1,128]{2,1,0:T(1,128)S(1)} all-to-all(f32[32,1,128]{2,1,0:T(1,128)S(1)} %broadcast_in_dim.11), channel_id=1, replica_groups=mesh['grp'=4,'sub'=32] {'sub'}, dimensions={0} | all-to-all | bytes 32768 | tf_op jit(solution)/shard_map/all_to_all | solution.py:677
  120.6 0.9 finish.1
  (16 shorter events, 0.2 us)
Async XLA Ops:
  0.6 0.9 copy-start
  0.6 11.7 %collective-permute-start = (bf16[96,96,128]{2,1,0:T(8,128)(2,1)}, bf16[96,96,128]{2,1,0:T(8,128)(2,1)}, u32[]{:S(2)}, u32[]{:S(2)}) collective-permute-start(bf16[96,96,128]{2,1,0:T(8,128)(2,1)} %bitcast.23), channel_id=1, source_target_pairs={{0,32},{1,33},{2,34},{3,35},{4,36},{5,37},{6,38},{7,39},{8,40},{9,... | collective-permute-start | bytes 7077896 | tf_op jit(solution)/shard_map/ppermute | solution.py:76
  2.8 29.9 %all-to-all-start = ((bf16[32,3,56,128]{3,2,1,0:T(8,128)(2,1)}), bf16[32,3,56,128]{3,2,1,0:T(8,128)(2,1)S(1)}, u32[]{:S(2)}, u32[]{:S(2)}) async-start(bf16[32,3,56,128]{3,2,1,0:T(8,128)(2,1)} %broadcast_in_dim.8), calls=%async_computation | async-start | bytes 2752512 | tf_op jit(solution)/shard_map/all_to_all | solution.py:637
  22.0 27.1 %collective-permute-start.4 = (f32[8,3,48,128]{3,2,1,0:T(8,128)}, f32[8,3,48,128]{3,2,1,0:T(8,128)S(1)}, u32[]{:S(2)}, u32[]{:S(2)}) collective-permute-start(f32[8,3,48,128]{3,2,1,0:T(8,128)} %get-tuple-element.40), channel_id=1, source_target_pairs={{0,1},{1,2},{2,3},{3,0},{4,5},{5,6},{6,7},{7,4},{8,9},{9,10},{10,1... | collective-permute-start | bytes 1769480 | tf_op jit(solution)/shard_map/ppermute | solution.py:76
  23.8 28.9 %collective-permute-start.5 = (f32[8,3,48,128]{3,2,1,0:T(8,128)}, f32[8,3,48,128]{3,2,1,0:T(8,128)S(1)}, u32[]{:S(2)}, u32[]{:S(2)}) collective-permute-start(f32[8,3,48,128]{3,2,1,0:T(8,128)} %get-tuple-element.41), channel_id=1, source_target_pairs={{0,2},{1,3},{2,0},{3,1},{4,6},{5,7},{6,4},{7,5},{8,10},{9,11},{10,... | collective-permute-start | bytes 1769480 | tf_op jit(solution)/shard_map/ppermute | solution.py:76
  26.5 26.3 %collective-permute-start.6 = (f32[8,3,48,128]{3,2,1,0:T(8,128)}, f32[8,3,48,128]{3,2,1,0:T(8,128)S(1)}, u32[]{:S(2)}, u32[]{:S(2)}) collective-permute-start(f32[8,3,48,128]{3,2,1,0:T(8,128)} %get-tuple-element.42), channel_id=1, source_target_pairs={{0,3},{1,0},{2,1},{3,2},{4,7},{5,4},{6,5},{7,6},{8,11},{9,8},{10,9... | collective-permute-start | bytes 1769480 | tf_op jit(solution)/shard_map/ppermute | solution.py:76
  32.7 8.1 %copy-start.1 = (f32[4,104,48,128]{3,2,1,0:T(8,128)S(1)}, f32[4,104,48,128]{3,2,1,0:T(8,128)}, u32[]{:S(2)}) copy-start(f32[4,104,48,128]{3,2,1,0:T(8,128)} %get-tuple-element.28.jplane) | copy-start | bytes 30670852
  42.7 17.5 %collective-permute-start.1 = (f32[8,3,48,128]{3,2,1,0:T(8,128)S(1)}, f32[8,3,48,128]{3,2,1,0:T(8,128)S(1)}, u32[]{:S(2)}, u32[]{:S(2)}) collective-permute-start(f32[8,3,48,128]{3,2,1,0:T(8,128)S(1)} %get-tuple-element.31), channel_id=1, source_target_pairs={{0,1},{1,2},{2,3},{3,0},{4,5},{5,6},{6,7},{7,4},{8,9},{9,10},{10,1... | collective-permute-start | bytes 1769480 | tf_op jit(solution)/shard_map/ppermute | solution.py:76
  45.6 14.6 %collective-permute-start.2 = (f32[8,3,48,128]{3,2,1,0:T(8,128)S(1)}, f32[8,3,48,128]{3,2,1,0:T(8,128)S(1)}, u32[]{:S(2)}, u32[]{:S(2)}) collective-permute-start(f32[8,3,48,128]{3,2,1,0:T(8,128)S(1)} %get-tuple-element.32), channel_id=1, source_target_pairs={{0,2},{1,3},{2,0},{3,1},{4,6},{5,7},{6,4},{7,5},{8,10},{9,11},{10,... | collective-permute-start | bytes 1769480 | tf_op jit(solution)/shard_map/ppermute | solution.py:76
  49.1 3.6 %copy-start.2 = (f32[8,3,48,128]{3,2,1,0:T(8,128)S(1)}, f32[8,3,48,128]{3,2,1,0:T(8,128)}, u32[]{:S(2)}) copy-start(f32[8,3,48,128]{3,2,1,0:T(8,128)} %get-tuple-element.39) | copy-start | bytes 1769476
  49.2 13.8 %collective-permute-start.3 = (f32[8,3,48,128]{3,2,1,0:T(8,128)S(1)}, f32[8,3,48,128]{3,2,1,0:T(8,128)S(1)}, u32[]{:S(2)}, u32[]{:S(2)}) collective-permute-start(f32[8,3,48,128]{3,2,1,0:T(8,128)S(1)} %get-tuple-element.33), channel_id=1, source_target_pairs={{0,3},{1,0},{2,1},{3,2},{4,7},{5,4},{6,5},{7,6},{8,11},{9,8},{10,9... | collective-permute-start | bytes 1769480 | tf_op jit(solution)/shard_map/ppermute | solution.py:76
  63.2 11.2 %collective-permute-start.7 = (f32[2,6,48,128]{3,2,1,0:T(8,128)S(1)}, f32[2,6,48,128]{3,2,1,0:T(8,128)S(1)}, u32[]{:S(2)}, u32[]{:S(2)}) collective-permute-start(f32[2,6,48,128]{3,2,1,0:T(8,128)S(1)} %get-tuple-element.51), channel_id=1, source_target_pairs={{0,4},{1,5},{2,6},{3,7},{4,8},{5,9},{6,10},{7,11},{8,12},{9,13},{1... | collective-permute-start | bytes 884744 | tf_op jit(solution)/shard_map/ppermute | solution.py:76
  64.9 9.5 %collective-permute-start.8 = (f32[2,6,48,128]{3,2,1,0:T(8,128)S(1)}, f32[2,6,48,128]{3,2,1,0:T(8,128)S(1)}, u32[]{:S(2)}, u32[]{:S(2)}) collective-permute-start(f32[2,6,48,128]{3,2,1,0:T(8,128)S(1)} %get-tuple-element.53), channel_id=1, source_target_pairs={{0,8},{1,9},{2,10},{3,11},{4,12},{5,13},{6,14},{7,15},{8,0},{9,1},... | collective-permute-start | bytes 884744 | tf_op jit(solution)/shard_map/ppermute | solution.py:76
  66.4 8.9 %collective-permute-start.9 = (f32[2,6,48,128]{3,2,1,0:T(8,128)S(1)}, f32[2,6,48,128]{3,2,1,0:T(8,128)S(1)}, u32[]{:S(2)}, u32[]{:S(2)}) collective-permute-start(f32[2,6,48,128]{3,2,1,0:T(8,128)S(1)} %get-tuple-element.52), channel_id=1, source_target_pairs={{0,12},{1,13},{2,14},{3,15},{4,0},{5,1},{6,2},{7,3},{8,4},{9,5},{1... | collective-permute-start | bytes 884744 | tf_op jit(solution)/shard_map/ppermute | solution.py:76
  75.4 6.8 %collective-permute-start.10 = (f32[296,128]{1,0:T(8,128)S(1)}, f32[296,128]{1,0:T(8,128)S(1)}, u32[]{:S(2)}, u32[]{:S(2)}) collective-permute-start(f32[296,128]{1,0:T(8,128)S(1)} %get-tuple-element.54), channel_id=1, source_target_pairs={{0,64},{1,65},{2,66},{3,67},{4,68},{5,69},{6,70},{7,71},{8,72},{9,... | collective-permute-start | bytes 454664 | tf_op jit(solution)/shard_map/ppermute | solution.py:76
  78.2 6.4 %collective-permute-start.11 = (f32[296,128]{1,0:T(8,128)S(1)}, f32[296,128]{1,0:T(8,128)S(1)}, u32[]{:S(2)}, u32[]{:S(2)}) collective-permute-start(f32[296,128]{1,0:T(8,128)S(1)} %get-tuple-element.55), channel_id=1, source_target_pairs={{0,16},{1,17},{2,18},{3,19},{4,20},{5,21},{6,22},{7,23},{8,24},{9,... | collective-permute-start | bytes 454664 | tf_op jit(solution)/shard_map/ppermute | solution.py:76
  78.3 6.2 %collective-permute-start.12 = (f32[296,128]{1,0:T(8,128)S(1)}, f32[296,128]{1,0:T(8,128)S(1)}, u32[]{:S(2)}, u32[]{:S(2)}) collective-permute-start(f32[296,128]{1,0:T(8,128)S(1)} %get-tuple-element.55), channel_id=1, source_target_pairs={{0,80},{1,81},{2,82},{3,83},{4,84},{5,85},{6,86},{7,87},{8,88},{9,... | collective-permute-start | bytes 454664 | tf_op jit(solution)/shard_map/ppermute | solution.py:76
  84.7 8.9 %collective-permute-start.14 = (f32[192,128]{1,0:T(8,128)S(1)}, f32[192,128]{1,0:T(8,128)S(1)}, u32[]{:S(2)}, u32[]{:S(2)}) collective-permute-start(f32[192,128]{1,0:T(8,128)S(1)} %pad_maximum_fusion.5), channel_id=1, source_target_pairs={{0,1},{1,2},{2,3},{3,4},{4,5},{5,6},{6,7},{7,8},{8,9},{9,10},{10,1... | collective-permute-start | bytes 294920 | tf_op jit(solution)/shard_map/ppermute | solution.py:76
  85.8 8.6 %collective-permute-start.13 = (f32[96,128]{1,0:T(8,128)S(1)}, f32[96,128]{1,0:T(8,128)S(1)}, u32[]{:S(2)}, u32[]{:S(2)}) collective-permute-start(f32[96,128]{1,0:T(8,128)S(1)} %slice_select_fusion), channel_id=1, source_target_pairs={{0,2},{1,3},{2,4},{3,5},{4,6},{5,7},{6,8},{7,9},{8,10},{9,11},{10,... | collective-permute-start | bytes 147464 | tf_op jit(solution)/shard_map/ppermute | solution.py:76
  94.5 8.0 %collective-permute-start.15 = (f32[288,128]{1,0:T(8,128)S(1)}, f32[288,128]{1,0:T(8,128)S(1)}, u32[]{:S(2)}, u32[]{:S(2)}) collective-permute-start(f32[288,128]{1,0:T(8,128)S(1)} %pad_maximum_fusion.4), channel_id=1, source_target_pairs={{0,64},{1,65},{2,66},{3,67},{4,68},{5,69},{6,70},{7,71},{8,72},{9,... | collective-permute-start | bytes 442376 | tf_op jit(solution)/shard_map/ppermute | solution.py:76
  102.5 2.1 %collective-permute-start.16 = (f32[872,128]{1,0:T(8,128)S(1)}, f32[872,128]{1,0:T(8,128)S(1)}, u32[]{:S(2)}, u32[]{:S(2)}) collective-permute-start(f32[872,128]{1,0:T(8,128)S(1)} %pad_maximum_fusion), channel_id=1, source_target_pairs={{0,32},{1,33},{2,34},{3,35},{4,36},{5,37},{6,38},{7,39},{8,40},{9,... | collective-permute-start | bytes 1339400 | tf_op jit(solution)/shard_map/ppermute | solution.py:76
  102.6 2.0 %collective-permute-start.17 = (bf16[15,48,128]{2,1,0:T(8,128)(2,1)S(1)}, bf16[15,48,128]{2,1,0:T(8,128)(2,1)S(1)}, u32[]{:S(2)}, u32[]{:S(2)}) collective-permute-start(bf16[15,48,128]{2,1,0:T(8,128)(2,1)S(1)} %get-tuple-element.43.iown_ref), channel_id=1, source_target_pairs={{0,32},{1,33},{2,34},{3,35},{4,36},{5,37},{6,38},{7,39},{8,40},{9,... | collective-permute-start | bytes 552968 | tf_op jit(solution)/shard_map/ppermute | solution.py:76
